TPU v7x, 128 devices: a whole 4x4x4 slice. The times are simulated.
128 devices in a mesh: gx: 16 (over z, y), gy: 8 (over x, core).
Axes of the slice: x: 4, y: 4, z: 4, core: 2. Of those that a mesh axis runs over, the one named last changes fastest.
Arguments:
- rhs_field: float32 [3, 32, 64, 4096], P(None, None, 'gy', 'gx'), may hold values from -6 to 6
- couplings: float32 [6, 3, 3, 32, 64, 4096], P(None, None, None, None, 'gy', 'gx'), may hold values from -0.6 to 0.6
- pivot_inverses: float32 [3, 3, 32, 64, 4096], P(None, None, None, 'gy', 'gx'), may hold values from -3.5 to 3.5
- colours: int32 [32, 64, 4096], P(None, 'gy', 'gx'), may hold values from 0 to 3
- perf_cells: int32 [131072], P(('gx', 'gy')), may hold values from 0 to 65535
- perf_wells: int32 [131072], P(('gx', 'gy')), may hold values from 0 to 8191, as said below
- perf_segments: int32 [131072], P(('gx', 'gy')), may hold values from 0 to 15
- perf_gather: float32 [3, 131072], P(None, ('gx', 'gy')), may hold values from -3 to 3
- perf_return: float32 [3, 131072], P(None, ('gx', 'gy')), may hold values from -3 to 3
- well_slot: int32 [8192], replicated, may hold values from 0 to 8191, as said below
- seg_count: int32 [8192], replicated, may hold values from 1 to 16
- well_inverses: float32 [8192, 16, 16], P(('gx', 'gy')), may hold values from -1.5 to 1.5
Outputs:
- precond_field: float32 [3, 32, 64, 4096], P(None, None, 'gy', 'gx')
Inputs may be any that keep to these rules, and one draw needn't show every extreme that they name: `well_slot`: wells are numbered by owner: well w's slot lies in w // 64 * 64 to that plus 64 - 1, each slot taken once, so slot s belongs to tile s // 64 (tiles ordered with x slowest). `perf_wells`: A perforation listed with a tile may name a well of any owner.
All inputs are finite; a program needn't handle non-finite values.
Results may differ from a plain program's by a relative error of at most 0.0001.
Values sent between devices are 32-bit elements; how exact they have to be, the bound alone decides.
No kernel may reach another device: no remote copies, remote signals or barrier semaphores. Data moves between devices by JAX's collectives and lax.ppermute only.
A program may use at most 384 MiB of HBM per device.

v0:
```python
import jax
import jax.numpy as jnp
from jax import lax
from jax.sharding import PartitionSpec as P


def padded_2(cells, sides, width):
    for axis, dim in sides:
        count = lax.axis_size(axis)
        ends = count - 1
        head = lax.slice_in_dim(cells, 0, width, axis=dim)
        tail = lax.slice_in_dim(cells, cells.shape[dim] - width, cells.shape[dim], axis=dim)
        cells = jnp.concatenate(
            [
                lax.ppermute(tail, axis, [(i, (i + 1) % count) for i in range(ends)]),
                cells,
                lax.ppermute(head, axis, [((i + 1) % count, i) for i in range(ends)]),
            ],
            axis=dim,
        )
    return cells


def gather_beside(couplings, padded_xy):
    padded = jnp.pad(padded_xy, ((0, 0), (1, 1), (0, 0), (0, 0)))
    beside = jnp.stack(
        [
            padded[:, 1:-1, 1:-1, :-2],
            padded[:, 1:-1, 1:-1, 2:],
            padded[:, 1:-1, :-2, 1:-1],
            padded[:, 1:-1, 2:, 1:-1],
            padded[:, :-2, 1:-1, 1:-1],
            padded[:, 2:, 1:-1, 1:-1],
        ]
    )
    return jnp.sum(couplings * beside[:, None], axis=(0, 2))


def couple_lower(couplings, field):
    padded_xy = padded_2(field, (("gx", 3), ("gy", 2)), 1)
    return gather_beside(couplings, padded_xy)


def couple_upper(couplings, field):
    padded_xy = padded_2(field, (("gx", 3), ("gy", 2)), 1)
    return gather_beside(couplings, padded_xy)


def pivot(pivot_inverses, field):
    return jnp.sum(pivot_inverses * field[None], axis=1)


def well_solve(inverses, totals, seg_counts):
    seg_index = jnp.arange(totals.shape[1], dtype=jnp.int32)
    alive_mask = (seg_index[None, :] < seg_counts[:, None]).astype(jnp.float32)
    return alive_mask * jnp.einsum(
        "wst,wt->ws", inverses, alive_mask * totals, precision=lax.Precision.HIGHEST
    )


def shards(
    rhs_field,
    couplings,
    pivot_inverses,
    colours,
    perf_cells,
    perf_wells,
    perf_segments,
    perf_gather,
    perf_return,
    well_slot,
    seg_count,
    well_inverses,
):
    segments = well_inverses.shape[1]
    wells_all = well_slot.shape[0]
    owned = well_inverses.shape[0]
    lower = jnp.zeros_like(rhs_field)
    upper_in = jnp.zeros_like(rhs_field)
    for colour in range(4):
        chosen = (colours == colour)[None]
        if colour == 0:
            current = rhs_field
        else:
            current = rhs_field - couple_lower(couplings, lower)
        upper_in = jnp.where(chosen, current, upper_in)
        lower = jnp.where(chosen, pivot(pivot_inverses, current), lower)
    sweep_field = jnp.zeros_like(rhs_field)
    for colour in (3, 2, 1, 0):
        chosen = (colours == colour)[None]
        if colour == 3:
            current = pivot(pivot_inverses, upper_in)
        else:
            current = pivot(pivot_inverses, upper_in - couple_upper(couplings, sweep_field))
        sweep_field = jnp.where(chosen, current, sweep_field)
    flat_field = sweep_field.reshape(3, -1)
    terms = jnp.sum(perf_gather * flat_field[:, perf_cells], axis=0)
    slots = well_slot[perf_wells]
    slot_counts = jnp.zeros((wells_all,), jnp.int32).at[well_slot].set(seg_count)
    well_key = slots * segments + perf_segments
    local_totals = (
        jnp.zeros((wells_all * segments,), jnp.float32)
        .at[well_key]
        .add(terms)
        .reshape(wells_all, segments)
    )
    own_totals = lax.psum_scatter(local_totals, ("gx", "gy"), scatter_dimension=0, tiled=True)
    own_counts = lax.dynamic_slice_in_dim(slot_counts, lax.axis_index(("gx", "gy")) * owned, owned)
    own_values = well_solve(well_inverses, own_totals, own_counts)
    values_all = lax.all_gather(own_values, ("gx", "gy"), axis=0, tiled=True)
    at_perfs = values_all.reshape(-1)[well_key]
    result = flat_field.at[:, perf_cells].add(-perf_return * at_perfs[None])
    return result.reshape(sweep_field.shape)


def solution(mesh):
    return jax.shard_map(
        shards,
        mesh=mesh,
        in_specs=(
            P(None, None, "gy", "gx"),
            P(None, None, None, None, "gy", "gx"),
            P(None, None, None, "gy", "gx"),
            P(None, "gy", "gx"),
            P(("gx", "gy")),
            P(("gx", "gy")),
            P(("gx", "gy")),
            P(None, ("gx", "gy")),
            P(None, ("gx", "gy")),
            P(),
            P(),
            P(("gx", "gy"), None, None),
        ),
        out_specs=P(None, None, "gy", "gx"),
        check_vma=False,
    )
```

profile of v0, /device:TPU:1, one launch (start us, length us, event | category | flops | bytes accessed | tf_op | source)
XLA Modules:
  0.0 1179.3 jit_solution(10838318960054971814)
XLA Ops:
  16.0 6.5 collective-permute-done
  27.2 4.8 collective-permute-start.2
  43.2 9.3 multiply_reduce_fusion.5
  59.2 4.9 collective-permute-done.4
  69.1 6.1 collective-permute-start.6
  87.7 9.1 multiply_reduce_fusion.4
  99.5 4.9 collective-permute-start.8
  105.6 4.9 collective-permute-done.8
  115.5 5.4 collective-permute-start.10
  133.4 9.1 multiply_reduce_fusion.3
  149.9 4.9 collective-permute-done.12
  154.8 4.4 collective-permute-done.13
  160.0 4.9 collective-permute-start.14
  177.4 9.2 multiply_reduce_fusion.2
  190.1 4.8 collective-permute-start.16
  196.2 6.2 gather_fusion
  207.7 4.3 collective-permute-start.18
  227.9 9.2 multiply_reduce_fusion.1
  247.8 17.7 %copy.28 = f32[3,32,8,256]{0,3,2,1:T(8,128)} copy(f32[3,32,8,256]{3,2,1,0:T(8,128)} %copy-done.7) | data formatting | bytes 1572864 | tf_op jit(solution)/shard_map/reduce_sum | solution.py:50
  265.5 16.7 %copy.27 = f32[3,32,8,256]{0,3,2,1:T(8,128)} copy(f32[3,32,8,256]{3,2,1,0:T(8,128)S(1)} %copy-done.14) | data formatting | bytes 1572864 | tf_op jit(solution)/shard_map/reduce_sum | solution.py:50
  282.2 17.9 %copy.26 = f32[3,32,8,256]{0,3,2,1:T(8,128)} copy(f32[3,32,8,256]{3,2,1,0:T(8,128)} %copy-done.15) | data formatting | bytes 1572864 | tf_op jit(solution)/shard_map/reduce_sum | solution.py:50
  321.9 9.2 multiply_reduce_fusion
  332.6 16.8 %copy.25 = f32[3,32,8,256]{0,3,2,1:T(8,128)} copy(f32[3,32,8,256]{3,2,1,0:T(8,128)S(1)} %multiply_reduce_fusion.6) | data formatting | bytes 1572864 | tf_op jit(solution)/shard_map/reduce_sum | solution.py:50
  349.4 52.2 %fusion.2 = f32[3,65536]{0,1:T(8,128)} fusion(f32[3,32,8,256]{0,3,2,1:T(8,128)} %copy.28, f32[3,32,8,256]{0,3,2,1:T(8,128)} %copy.27, f32[3,32,8,256]{0,3,2,1:T(8,128)} %copy.26, f32[3,32,8,256]{0,3,2,1:T(8,128)} %copy.25, pred[65536]{0:T(1024)(128)(4,1)S(1)} %broadcast_in_dim.111, pred[65536]{0:T(1024)(128)(4,1)S(1)} %broadcast_in_dim.109, ...), kind=kLoop, calls=%fused_computation.9 | loop fusion | flops 786432 | bytes 4194304 | tf_op jit(solution)/shard_map/jit(_where)/select_n | solution.py:95
  401.6 13.3 %gather_fusion.1 = f32[1024,3]{1,0:T(8,128)S(1)} fusion(f32[3,65536]{0,1:T(8,128)} %fusion.2, s32[1024]{0:T(1024)S(1)} %get-tuple-element.35), kind=kCustom, calls=%fused_computation.1 | custom fusion | bytes 28672 | tf_op jit(solution)/shard_map/gather | solution.py:97
  415.2 6.1 scatter_custom_fusion.1
  424.2 30.7 %scatter_custom_fusion = s32[8192]{0:T(1024)S(1)} fusion(s32[8192]{0:T(1024)S(1)} %compare_select_fusion, s32[8192]{0:T(1024)} %param.22, s32[]{:T(128)} %constant.14.clone.1), kind=kCustom, calls=%fused_computation.208 | custom fusion | bytes 33280 | tf_op jit(solution)/shard_map/scatter | solution.py:99
  455.0 614.8 %reduce-scatter.2.cloned.1.call-done = f32[64,16]{1,0:T(8,128)} async-done(((f32[8192,16]{1,0:T(8,128)}), f32[64,16]{1,0:T(8,128)}) %reduce-scatter.2.cloned.1.call-update) | async-done | bytes 4112 | tf_op jit(solution)/shard_map/reduce_scatter | solution.py:107
  1071.4 42.0 %all-gather = f32[128,64,16]{1,2,0:T(8,128)S(1)} all-gather(f32[1,64,16]{1,2,0:T(8,128)S(1)} %copy.30), channel_id=1, replica_groups=mesh['gx'=16,'gy'=8] {'gx','gy'}, dimensions={0}, use_global_device_ids=true | all-gather | bytes 528384 | tf_op jit(solution)/shard_map/all_gather | solution.py:110
  1119.3 6.2 gather_fusion.2
  1125.7 27.0 %scatter_fusion = f32[3,65536]{0,1:T(8,128)} fusion(f32[3,65536]{0,1:T(8,128)} %fusion.2, s32[1024]{0:T(1024)S(1)} %get-tuple-element.36, f32[1024,3]{1,0:T(8,128)S(1)} %copy.32), kind=kCustom, calls=%fused_computation.5 | custom fusion | flops 3072 | bytes 40960 | tf_op jit(solution)/shard_map/scatter-add | solution.py:112
  1152.7 19.5 %copy.33 = f32[3,32,8,256]{3,2,1,0:T(8,128)} copy(f32[3,32,8,256]{0,3,2,1:T(8,128)} %bitcast.174) | data formatting | bytes 1572864 | tf_op jit(solution)/shard_map/reshape | solution.py:113
  (178 shorter events, 162.3 us)
Async XLA Ops:
  6.5 1063.3 %reduce-scatter.2.cloned.1.call-start = ((), (), s32[]{:S(2)}) async-start(), calls=%async_computation.1 | async-start | bytes 4227072 | tf_op jit(solution)/shard_map/reduce_scatter | solution.py:107
  10.7 11.8 %collective-permute-start = (f32[3,32,8,1]{3,2,1,0:T(8,128)S(1)}, f32[3,32,8,1]{3,2,1,0:T(8,128)S(1)}, u32[]{:S(2)}, u32[]{:S(2)}) collective-permute-start(f32[3,32,8,1]{3,2,1,0:T(8,128)S(1)} %get-tuple-element.30), channel_id=1, source_target_pairs={{0,8},{8,16},{16,24},{24,32},{32,40},{40,48},{48,56},{56,64},{64,7... | collective-permute-start | bytes 9224 | tf_op jit(solution)/shard_map/ppermute | solution.py:15
  14.7 11.6 collective-permute-start.1
  27.2 9.2 collective-permute-start.2
  32.1 6.5 collective-permute-start.3
  43.2 10.6 copy-start.1
  54.7 9.4 collective-permute-start.4
  57.9 10.3 collective-permute-start.5
  69.1 10.7 collective-permute-start.6
  75.3 6.5 collective-permute-start.7
  99.5 11.0 collective-permute-start.8
  104.3 10.3 collective-permute-start.9
  115.5 10.0 collective-permute-start.10
  120.9 6.5 collective-permute-start.11
  144.6 42.0 %copy-start.4 = (f32[3,32,8,256]{3,2,1,0:T(8,128)}, f32[3,32,8,256]{3,2,1,0:T(8,128)S(1)}, u32[]{:S(2)}) copy-start(f32[3,32,8,256]{3,2,1,0:T(8,128)S(1)} %select_select_fusion) | copy-start | bytes 2359300
  144.8 24.7 %copy-start.7 = (f32[3,32,8,256]{3,2,1,0:T(8,128)}, f32[3,32,8,256]{3,2,1,0:T(8,128)S(1)}, u32[]{:S(2)}) copy-start(f32[3,32,8,256]{3,2,1,0:T(8,128)S(1)} %multiply_reduce_fusion.9) | copy-start | bytes 2359300
  145.1 9.6 collective-permute-start.12
  148.6 10.5 collective-permute-start.13
  160.0 9.6 collective-permute-start.14
  165.0 6.5 collective-permute-start.15
  190.1 12.3 %collective-permute-start.16 = (f32[3,32,8,1]{3,2,1,0:T(8,128)}, f32[3,32,8,1]{3,2,1,0:T(8,128)}, u32[]{:S(2)}, u32[]{:S(2)}) collective-permute-start(f32[3,32,8,1]{3,2,1,0:T(8,128)} %get-tuple-element.22), channel_id=1, source_target_pairs={{0,8},{8,16},{16,24},{24,32},{32,40},{40,48},{48,56},{56,64},{64,7... | collective-permute-start | bytes 9224 | tf_op jit(solution)/shard_map/ppermute | solution.py:15
  194.9 10.6 collective-permute-start.17
  207.7 11.2 collective-permute-start.18
  212.0 6.8 collective-permute-start.19
  241.0 59.1 %collective-permute-start.20 = (f32[3,32,8,1]{3,2,1,0:T(8,128)}, f32[3,32,8,1]{3,2,1,0:T(8,128)}, u32[]{:S(2)}, u32[]{:S(2)}) collective-permute-start(f32[3,32,8,1]{3,2,1,0:T(8,128)} %get-tuple-element.20), channel_id=1, source_target_pairs={{0,8},{8,16},{16,24},{24,32},{32,40},{40,48},{48,56},{56,64},{64,7... | collective-permute-start | bytes 9224 | tf_op jit(solution)/shard_map/ppermute | solution.py:15
  245.2 54.9 %collective-permute-start.21 = (f32[3,32,8,1]{3,2,1,0:T(8,128)}, f32[3,32,8,1]{3,2,1,0:T(8,128)}, u32[]{:S(2)}, u32[]{:S(2)}) collective-permute-start(f32[3,32,8,1]{3,2,1,0:T(8,128)} %get-tuple-element.19), channel_id=1, source_target_pairs={{8,0},{16,8},{24,16},{32,24},{40,32},{48,40},{56,48},{64,56},{72,6... | collective-permute-start | bytes 9224 | tf_op jit(solution)/shard_map/ppermute | solution.py:17
  247.8 17.7 %copy-start.14 = (f32[3,32,8,256]{3,2,1,0:T(8,128)S(1)}, f32[3,32,8,256]{3,2,1,0:T(8,128)}, u32[]{:S(2)}) copy-start(f32[3,32,8,256]{3,2,1,0:T(8,128)} %copy-done.13) | copy-start | bytes 2359300
  282.2 17.9 %copy-start.3 = (f32[3,32,8,256]{3,2,1,0:T(8,128)S(1)}, f32[3,32,8,256]{3,2,1,0:T(8,128)}, u32[]{:S(2)}) copy-start(f32[3,32,8,256]{3,2,1,0:T(8,128)} %copy-done.2) | copy-start | bytes 2359300
  302.3 10.4 collective-permute-start.22
  306.3 6.5 collective-permute-start.23
  349.4 65.6 %copy-start.16 = (f32[3,1024]{0,1:T(8,128)S(1)}, f32[3,1024]{0,1:T(8,128)}, u32[]{:S(2)}) copy-start(f32[3,1024]{0,1:T(8,128)} %copy.29) | copy-start | bytes 36868
  1116.0 9.4 copy-start.19
  (16 other events, 72.1 us)
Sparse Core Ops, SparseCore 0:
  424.0 645.7 reduce-scatter.1
where the time goes:
time: 1190 us; the launch traced here: 1180 us
  waiting for transfers between devices  662 us (56%)
  other arithmetic  211 us (18%)
  local copies, waits for them, and re-layouts  175 us (15%)
  starting transfers between devices  74.6 us (6%)
  blocking collectives  42 us (4%)
  between operations  14.3 us (1%)
    reduce_scatter x1, waiting for transfers between devices, shards(): lax.psum_scatter(local_totals, ('gx', 'gy'), scatter_dimension=0, tiled=T...  615 us
    reduce_sum x4, local copies, waits for them, and re-layouts, pivot(): return jnp.sum(pivot_inverses * field[None], axis=1)  69 us
    reduce_sum x6, other arithmetic, gather_beside(): return jnp.sum(couplings * beside[:, None], axis=(0, 2))  55 us
    ppermute x12, starting transfers between devices, padded_2(): lax.ppermute(tail, axis, [(i, (i + 1) % count) for i in range(ends)])  54 us
    select_n x4, other arithmetic, shards(): sweep_field = jnp.where(chosen, current, sweep_field)  52.6 us
    all_gather x1, blocking collectives, shards(): values_all = lax.all_gather(own_values, ('gx', 'gy'), axis=0, tiled=True)  42 us
    unnamed x25, other arithmetic  37.9 us
    scatter x1, local copies, waits for them, and re-layouts, shards(): jnp.zeros((wells_all,), jnp.int32).at[well_slot].set(seg_count)  30.7 us
  transfers between devices with their start and end apart: 25, of which 14 were waited for; matrix products, arithmetic and copies ran while one was open for 9% of the time, Pallas kernels for 0%

commit v1 on v0

v1 whole, which is shorter than its diff:
```python
import jax
import jax.numpy as jnp
from jax import lax
from jax.experimental import pallas as pl
from jax.experimental.pallas import tpu as pltpu
from jax.sharding import PartitionSpec as P

F32 = jnp.float32
BF16 = jnp.bfloat16
VMEM_SPEC = pl.BlockSpec(memory_space=pltpu.VMEM)
SMEM_SPEC = pl.BlockSpec(memory_space=pltpu.SMEM)


def iota(shape, dim):
    return lax.broadcasted_iota(jnp.int32, shape, dim)


def split3(x):
    a = x.astype(BF16)
    r = x - a.astype(F32)
    b = r.astype(BF16)
    c = (r - b.astype(F32)).astype(BF16)
    return a, b, c


def dot(a, b, dims):
    return lax.dot_general(a, b, (dims, ((), ())), preferred_element_type=F32)


def in_vmem(x):
    return pltpu.with_memory_space_constraint(x, pltpu.VMEM)


def call(body, outs, ins, smem=0, name=None, cost=None, limit=None):
    specs = [SMEM_SPEC] * smem + [VMEM_SPEC] * (len(ins) - smem)
    args = list(ins[:smem]) + [in_vmem(x) for x in ins[smem:]]
    return pl.pallas_call(
        body,
        out_shape=tuple(pltpu.VMEM(s, d) for s, d in outs),
        in_specs=specs,
        out_specs=tuple(VMEM_SPEC for _ in outs),
        compiler_params=pltpu.CompilerParams(vmem_limit_bytes=limit or (8 << 20)),
        cost_estimate=cost,
        name=name,
    )(*args)


def emit_edges(new, z, nz, edges, ylo_ref, yhi_ref):
    xlo, xhi = edges
    lane = iota((8, 128), 1)
    for j in range(3):
        at = j * nz + z
        xlo = jnp.where(lane == at, pltpu.roll(new[j][:, :128], at, 1), xlo)
        xhi = jnp.where(lane == at, pltpu.roll(new[j][:, -128:], (at + 1) % 128, 1), xhi)
        ylo_ref[pl.ds(at, 1), :] = new[j][0:1, :]
        yhi_ref[pl.ds(at, 1), :] = new[j][-1:, :]
    return xlo, xhi


def zero_ends(ref, nz):
    zero = jnp.zeros(ref.shape[2:], F32)
    for j in range(3):
        ref[j, 0] = zero
        ref[j, nz + 1] = zero


def first_body(rhs_ref, piv_ref, col_ref, v_ref, xlo_ref, xhi_ref, ylo_ref, yhi_ref):
    nz = rhs_ref.shape[1]
    zero_ends(v_ref, nz)

    def step(z, edges):
        rhs = [rhs_ref[j, z] for j in range(3)]
        chosen = col_ref[z] == 0
        new = []
        for i in range(3):
            p = piv_ref[i, 0, z] * rhs[0] + piv_ref[i, 1, z] * rhs[1] + piv_ref[i, 2, z] * rhs[2]
            p = jnp.where(chosen, p, 0.0)
            v_ref[i, z + 1] = p
            new.append(p)
        return emit_edges(new, z, nz, edges, ylo_ref, yhi_ref)

    zero = jnp.zeros((8, 128), F32)
    xlo, xhi = lax.fori_loop(0, nz, step, (zero, zero))
    xlo_ref[...] = xlo
    xhi_ref[...] = xhi


def turn_body(colour, forward, final, *refs):
    (meta_ref, coup_ref, piv_ref, col_ref, base_ref, v_ref, hxlo_ref, hxhi_ref, hylo_ref, hyhi_ref) = refs[:10]
    refs = refs[10:]
    if forward:
        u_ref, nv_ref, *edge_refs = refs
    else:
        nv_ref, *edge_refs = refs
    if forward:
        rhs_ref, old_ref = base_ref, None
    nz = base_ref.shape[1]
    ny, nx = base_ref.shape[2:]
    keep = colour if forward else colour
    lane = iota((ny, 128), 1)
    row = iota((ny, nx), 0)
    fxlo = meta_ref[1].astype(F32)
    fxhi = meta_ref[2].astype(F32)
    fylo = meta_ref[3].astype(F32)
    fyhi = meta_ref[4].astype(F32)
    hxlo = hxlo_ref[...] * fxlo
    hxhi = hxhi_ref[...] * fxhi
    if not final:
        zero_ends(nv_ref, nz)

    def step(z, edges):
        acc = [jnp.zeros((ny, nx), F32) for _ in range(3)]
        old = []
        for j in range(3):
            at = j * nz + z
            vc = v_ref[j, z + 1]
            old.append(vc)
            xm = pltpu.roll(vc, 1, 1)
            head = jnp.where(lane == 0, pltpu.roll(hxlo, (128 - at) % 128, 1), xm[:, :128])
            xm = jnp.concatenate([head, xm[:, 128:]], axis=1)
            xp = pltpu.roll(vc, nx - 1, 1)
            tail = jnp.where(lane == 127, pltpu.roll(hxhi, 127 - at, 1), xp[:, -128:])
            xp = jnp.concatenate([xp[:, :-128], tail], axis=1)
            ym = jnp.where(row == 0, hylo_ref[pl.ds(at, 1), :] * fylo, pltpu.roll(vc, 1, 0))
            yp = jnp.where(row == ny - 1, hyhi_ref[pl.ds(at, 1), :] * fyhi, pltpu.roll(vc, ny - 1, 0))
            zm = v_ref[j, z]
            zp = v_ref[j, z + 2]
            for i in range(3):
                t = coup_ref[0, i, j, z] * xm + coup_ref[1, i, j, z] * xp
                t = t + (coup_ref[2, i, j, z] * ym + coup_ref[3, i, j, z] * yp)
                t = t + (coup_ref[4, i, j, z] * zm + coup_ref[5, i, j, z] * zp)
                acc[i] = acc[i] + t
        chosen = col_ref[z] == colour
        base = [base_ref[j, z] for j in range(3)]
        if forward:
            cur = []
            for j in range(3):
                cur.append(base[j] - acc[j])
        else:
            cur = [base[j] - acc[j] for j in range(3)]
        new = []
        for i in range(3):
            p = piv_ref[i, 0, z] * cur[0] + piv_ref[i, 1, z] * cur[1] + piv_ref[i, 2, z] * cur[2]
            if forward:
                u_ref[i, z] = jnp.where(chosen, cur[i], base[i])
                keep_old = 0.0 if colour == 3 else old[i]
            else:
                keep_old = old[i]
            p = jnp.where(chosen, p, keep_old)
            if final:
                nv_ref[i, z] = p
            else:
                nv_ref[i, z + 1] = p
            new.append(p)
        if final:
            return edges
        return emit_edges(new, z, nz, edges, edge_refs[2], edge_refs[3])

    zero = jnp.zeros((ny, 128), F32)
    xlo, xhi = lax.fori_loop(0, nz, step, (zero, zero))
    if not final:
        edge_refs[0][...] = xlo
        edge_refs[1][...] = xhi


def halos(edges):
    xlo, xhi, ylo, yhi = edges
    nx = lax.axis_size("gx")
    ny = lax.axis_size("gy")
    up_y = [(i, (i + 1) % ny) for i in range(ny)]
    dn_y = [((i + 1) % ny, i) for i in range(ny)]
    up_x = [(i, (i + 1) % nx) for i in range(nx)]
    dn_x = [((i + 1) % nx, i) for i in range(nx)]
    hylo = lax.ppermute(yhi, "gy", up_y)
    hyhi = lax.ppermute(ylo, "gy", dn_y)
    hxlo = lax.ppermute(xhi, "gx", up_x)
    hxhi = lax.ppermute(xlo, "gx", dn_x)
    return hxlo, hxhi, hylo, hyhi


def prep_body(meta_ref, slot_ref, count_ref, cells_ref, wells_ref, segs_ref, kh_ref, rt_ref, e_ref, alive_ref, lo_ref):
    n = cells_ref.shape[1]
    wells = wells_ref[...]
    table = slot_ref[...]
    pick = (iota((table.shape[0], n), 0) == (wells >> 7)).astype(BF16)
    high = dot((table >> 7).astype(F32).astype(BF16), pick, ((0,), (0,)))
    low = dot((table & 127).astype(F32).astype(BF16), pick, ((0,), (0,)))
    slot = jnp.where(iota((128, n), 0) == (wells & 127), high * 128.0 + low, 0.0)
    slot = jnp.sum(slot, axis=0, keepdims=True).astype(jnp.int32)
    key = slot * 16 + segs_ref[...]
    lo_ref[...] = key & 127
    kh_ref[...] = (iota(kh_ref.shape, 0) == (key >> 7)).astype(F32).astype(BF16)
    rt_ref[...] = (iota(rt_ref.shape, 0) == (cells_ref[...] >> 8)).astype(F32).astype(BF16)
    a = iota(e_ref.shape, 0)
    b = iota(e_ref.shape, 1)
    same = ((a >> 4) == ((b & 127) >> 4)) & ((a & 15) == (b >> 7))
    e_ref[...] = same.astype(F32).astype(BF16)
    tile = meta_ref[0]
    own_slot = slot_ref[pl.ds(tile // 2, 1), :] - tile * 64
    own_count = count_ref[pl.ds(tile // 2, 1), :].astype(F32)
    left = jnp.where(iota((8, 128), 0) == (own_slot >> 3), own_count, 0.0).astype(BF16)
    right = ((iota((128, 128), 0) >> 4) == (own_slot & 7)).astype(F32).astype(BF16)
    counts = dot(left, right, ((1,), (1,)))
    alive_ref[...] = ((iota((8, 128), 1) & 15).astype(F32) < counts).astype(F32)


def terms_body(s_ref, rt_ref, kh_ref, lo_ref, cells_ref, gather_ref, out_ref):
    n = cells_ref.shape[1]
    rt = rt_ref[...]
    at_col = iota((256, n), 0) == (cells_ref[...] & 255)
    term = jnp.zeros((1, n), F32)
    for i in range(3):
        f = s_ref[i].reshape(256, 256)
        g = sum(dot(h, rt, ((0,), (0,))) for h in split3(f))
        v = jnp.sum(jnp.where(at_col, g, 0.0), axis=0, keepdims=True)
        term = term + gather_ref[pl.ds(i, 1), :] * v
    at_low = iota((128, n), 0) == lo_ref[...]
    stack = jnp.concatenate([jnp.where(at_low, h.astype(F32), 0.0).astype(BF16) for h in split3(term)], axis=0)
    sums = dot(kh_ref[...], stack, ((1,), (1,)))
    out_ref[...] = sums[:, :128] + sums[:, 128:256] + sums[:, 256:]


def solve_body(got_ref, q_ref, e_ref, alive_ref, out_ref):
    alive = alive_ref[...]
    totals = jnp.sum(got_ref[...], axis=0) * alive
    spread = sum(dot(h, e_ref[...], ((1,), (0,))) for h in split3(totals))
    values = jnp.zeros((8, 128), F32)
    for j in range(16):
        values = values + q_ref[j] * spread[:, j * 128 : (j + 1) * 128]
    values = values * alive
    out_ref[...] = jnp.broadcast_to(values[None], out_ref.shape)


def return_body(table_ref, s_ref, rt_ref, kh_ref, lo_ref, cells_ref, back_ref, out_ref):
    n = cells_ref.shape[1]
    kh = kh_ref[...]
    table = table_ref[...].reshape(1024, 128)
    g = sum(dot(h, kh, ((0,), (0,))) for h in split3(table))
    values = jnp.sum(jnp.where(iota((128, n), 0) == lo_ref[...], g, 0.0), axis=0, keepdims=True)
    at_col = iota((256, n), 0) == (cells_ref[...] & 255)
    rt = rt_ref[...]
    for i in range(3):
        w = back_ref[pl.ds(i, 1), :] * values
        change = sum(
            dot(rt, jnp.where(at_col, h.astype(F32), 0.0).astype(BF16), ((1,), (1,))) for h in split3(w)
        )
        out_ref[i] = s_ref[i] - change.reshape(32, 8, 256)


def shards(
    rhs,
    couplings,
    pivots,
    colours,
    perf_cells,
    perf_wells,
    perf_segments,
    perf_gather,
    perf_return,
    well_slot,
    seg_count,
    well_inverses,
):
    axes = ("gx", "gy")
    devices = lax.axis_size(axes)
    gx = lax.axis_index("gx")
    gy = lax.axis_index("gy")
    tile = lax.axis_index(axes)
    meta = jnp.stack(
        [
            tile,
            (gx > 0).astype(jnp.int32),
            (gx < lax.axis_size("gx") - 1).astype(jnp.int32),
            (gy > 0).astype(jnp.int32),
            (gy < lax.axis_size("gy") - 1).astype(jnp.int32),
        ]
    ).astype(jnp.int32)
    _, nz, ny, nx = rhs.shape
    field = ((3, nz + 2, ny, nx), F32)
    plain = ((3, nz, ny, nx), F32)
    edges = [((ny, 128), F32)] * 2 + [((3 * nz, nx), F32)] * 2
    n = perf_cells.shape[0]
    cells = perf_cells.reshape(1, n)

    kh, rt, spread, alive, low = call(
        prep_body,
        [((1024, n), BF16), ((256, n), BF16), ((128, 2048), BF16), ((8, 128), F32), ((1, n), jnp.int32)],
        [
            meta,
            well_slot.reshape(-1, 128),
            seg_count.reshape(-1, 128),
            cells,
            perf_wells.reshape(1, n),
            perf_segments.reshape(1, n),
        ],
        smem=1,
        name="prep",
    )
    q = well_inverses.reshape(8, 8, 16, 16).transpose(3, 0, 1, 2).reshape(16, 8, 128)

    v, *edge = call(first_body, [field] + edges, [rhs, pivots, colours], name="first")
    base = rhs
    for colour in (1, 2, 3):
        halo = halos(edge)
        base, v, *edge = call(
            lambda *r, c=colour: turn_body(c, True, False, *r),
            [plain, field] + edges,
            [meta, couplings, pivots, colours, base, v, *halo],
            smem=1,
            name=f"forward{colour}",
        )
    for colour in (2, 1, 0):
        halo = halos(edge)
        final = colour == 0
        v, *edge = call(
            lambda *r, c=colour, f=final: turn_body(c, False, f, *r),
            [plain] if final else [field] + edges,
            [meta, couplings, pivots, colours, base, v, *halo],
            smem=1,
            name=f"backward{colour}",
        )
    (totals,) = call(
        terms_body, [((1024, 128), F32)], [v, rt, kh, low, cells, perf_gather], name="terms", limit=24 << 20
    )
    got = lax.all_to_all(totals.reshape(devices, 8, 128), axes, 0, 0, tiled=True)
    (values,) = call(solve_body, [((devices, 8, 128), F32)], [got, q, spread, alive], name="solve")
    table = lax.all_to_all(values, axes, 0, 0, tiled=True)
    return pl.pallas_call(
        return_body,
        out_shape=jax.ShapeDtypeStruct(rhs.shape, F32),
        in_specs=[VMEM_SPEC] * 7,
        out_specs=VMEM_SPEC,
        compiler_params=pltpu.CompilerParams(vmem_limit_bytes=24 << 20),
        name="back",
    )(*[in_vmem(x) for x in (table, v, rt, kh, low, cells, perf_return)])


def solution(mesh):
    return jax.shard_map(
        shards,
        mesh=mesh,
        in_specs=(
            P(None, None, "gy", "gx"),
            P(None, None, None, None, "gy", "gx"),
            P(None, None, None, "gy", "gx"),
            P(None, "gy", "gx"),
            P(("gx", "gy")),
            P(("gx", "gy")),
            P(("gx", "gy")),
            P(None, ("gx", "gy")),
            P(None, ("gx", "gy")),
            P(),
            P(),
            P(("gx", "gy"), None, None),
        ),
        out_specs=P(None, None, "gy", "gx"),
        check_vma=False,
    )
```

time: 1190 us -> 159 us (0.13)
  waiting for transfers between devices: 662 us -> 15 us
  other arithmetic: 211 us -> 0 us
  local copies, waits for them, and re-layouts: 175 us -> 16 us
  Pallas kernels: 0 us -> 48.3 us
  blocking collectives: 42 us -> 18 us
  between operations: 14.3 us -> 0.3 us
  starting transfers between devices: 74.6 us -> 61.4 us
    reduce_scatter x1 -> x0, waiting for transfers between devices: 615 us -> none  [shards(): lax.psum_scatter(local_totals, ('gx', 'gy'), scatter_dimension=0, tiled=T...]
    reduce_sum x4 -> x0, local copies, waits for them, and re-layouts: 69 us -> none  [pivot(): return jnp.sum(pivot_inverses * field[None], axis=1)]
    reduce_sum x14 -> x0, other arithmetic: 59.2 us -> none  [the longest x6 55 us: gather_beside(): return jnp.sum(couplings * beside[:, None], axis=(0, 2))]
    select_n x9 -> x0, other arithmetic: 55 us -> none  [the longest x4 52.6 us: shards(): sweep_field = jnp.where(chosen, current, sweep_field)]
    pallas_call x0 -> x11, Pallas kernels: none -> 48.3 us  [the longest x10 44.9 us: call(): pl.pallas_call(body, out_shape=tuple((pltpu.VMEM(s, d) for s, d in outs))...]
    ppermute x24, waiting for transfers between devices: 47.1 us -> 4.92 us  [the longest x6 4.87 us: halos(): hxlo = lax.ppermute(xhi, 'gx', up_x)]
    all_gather x1 -> x0, blocking collectives: 42 us -> none  [shards(): values_all = lax.all_gather(own_values, ('gx', 'gy'), axis=0, tiled=True)]
    unnamed x25 -> x0, other arithmetic: 37.9 us -> none
  transfers between devices with their start and end apart: 25 -> 25, of which waited for: 14 -> 6; matrix products, arithmetic and copies ran while one was open for 9% -> 2% of each run, Pallas kernels for 0% -> 1%
where the time goes in v1:
time: 159 us
  starting transfers between devices  61.4 us (39%)
  Pallas kernels  48.3 us (30%)
  blocking collectives  18 us (11%)
  local copies, waits for them, and re-layouts  16 us (10%)
  waiting for transfers between devices  15 us (9%)
    pallas_call x10, Pallas kernels, call(): pl.pallas_call(body, out_shape=tuple((pltpu.VMEM(s, d) for s, d in outs))...  44.9 us
    ppermute x6, starting transfers between devices, halos(): hxhi = lax.ppermute(xlo, 'gx', dn_x)  30.2 us
    all_to_all x1, blocking collectives, shards(): table = lax.all_to_all(values, axes, 0, 0, tiled=True)  18 us
    unnamed x48, local copies, waits for them, and re-layouts  12.8 us
    ppermute x6, starting transfers between devices, halos(): hyhi = lax.ppermute(ylo, 'gy', dn_y)  11.6 us
    all_to_all x1, waiting for transfers between devices, shards(): lax.all_to_all(totals.reshape(devices, 8, 128), axes, 0, 0, tiled=True)  10.1 us
    all_to_all x1, starting transfers between devices, shards(): lax.all_to_all(totals.reshape(devices, 8, 128), axes, 0, 0, tiled=True)  9.19 us
    ppermute x6, starting transfers between devices, halos(): hylo = lax.ppermute(yhi, 'gy', up_y)  9.1 us
  transfers between devices with their start and end apart: 25, of which 6 were waited for; matrix products, arithmetic and copies ran while one was open for 2% of the time, Pallas kernels for 1%

profile of v1, /device:TPU:1, one launch (start us, length us, event | category | flops | bytes accessed | tf_op | source)
XLA Modules:
  0.0 159.0 jit_solution(15451567523792508988)
XLA Ops:
  0.0 1.7 %copy-done.2 = f32[3,3,32,8,256]{4,3,2,1,0:T(8,128)S(1)} copy-done((f32[3,3,32,8,256]{4,3,2,1,0:T(8,128)S(1)}, f32[3,3,32,8,256]{4,3,2,1,0:T(8,128)}, u32[]{:S(2)}) %copy-start.2) | copy-done | bytes 2359320
  3.8 3.3 %first.1 = (f32[3,34,8,256]{3,2,1,0:T(8,128)S(1)}, f32[8,128]{1,0:T(8,128)S(1)}, f32[8,128]{1,0:T(8,128)S(1)}, f32[96,256]{1,0:T(8,128)}, f32[96,256]{1,0:T(8,128)}) custom-call(f32[3,32,8,256]{3,2,1,0:T(8,128)S(1)} %copy-done.8, f32[3,3,32,8,256]{4,3,2,1,0:T(8,128)S(1)} %copy-done.2, s32[32,8,256]{2,1,0:T(8,128)S(1)} %copy-done.4), custom_call_target="tpu_custom_call" | custom-call | tf_op jit(solution)/shard_map/first/pallas_call | solution.py:37
  8.0 2.6 %collective-permute-start.2 = (f32[96,256]{1,0:T(8,128)}, f32[96,256]{1,0:T(8,128)S(1)}, u32[]{:S(2)}, u32[]{:S(2)}) collective-permute-start(f32[96,256]{1,0:T(8,128)} %get-tuple-element.46), channel_id=1, source_target_pairs={{0,1},{1,2},{2,3},{3,4},{4,5},{5,6},{6,7},{7,0},{8,9},{9,10},{10,1... | collective-permute-start | bytes 294920 | tf_op jit(solution)/shard_map/ppermute | solution.py:174
  10.6 1.3 collective-permute-start
  11.9 4.9 %collective-permute-start.1 = (f32[8,128]{1,0:T(8,128)S(1)}, f32[8,128]{1,0:T(8,128)S(1)}, u32[]{:S(2)}, u32[]{:S(2)}) collective-permute-start(f32[8,128]{1,0:T(8,128)S(1)} %get-tuple-element.45), channel_id=1, source_target_pairs={{8,0},{16,8},{24,16},{32,24},{40,32},{48,40},{56,48},{64,56},{72,6... | collective-permute-start | bytes 12296 | tf_op jit(solution)/shard_map/ppermute | solution.py:177
  17.9 5.0 %copy-done = f32[6,3,3,32,8,256]{5,4,3,2,1,0:T(8,128)S(1)} copy-done((f32[6,3,3,32,8,256]{5,4,3,2,1,0:T(8,128)S(1)}, f32[6,3,3,32,8,256]{5,4,3,2,1,0:T(8,128)}, u32[]{:S(2)}) %copy-start) | copy-done | bytes 14155800
  24.0 6.6 %forward1.1 = (f32[3,32,8,256]{3,2,1,0:T(8,128)S(1)}, f32[3,34,8,256]{3,2,1,0:T(8,128)S(1)}, f32[8,128]{1,0:T(8,128)S(1)}, f32[8,128]{1,0:T(8,128)S(1)}, f32[96,256]{1,0:T(8,128)S(1)}, /*index=5*/f32[96,256]{1,0:T(8,128)S(1)}) custom-call(s32[5]{0:T(128)S(1)} %stack.39.r_0_.meta_ref, f32[6,3,3,32,8,256]{5,4,3,2,1,0:T(8,128)S(1)} %copy-done, ...), custom_call_target="tpu_custom_call" | custom-call | tf_op jit(solution)/shard_map/forward1/pallas_call | solution.py:37
  30.7 2.6 %collective-permute-start.6 = (f32[96,256]{1,0:T(8,128)S(1)}, f32[96,256]{1,0:T(8,128)S(1)}, u32[]{:S(2)}, u32[]{:S(2)}) collective-permute-start(f32[96,256]{1,0:T(8,128)S(1)} %get-tuple-element.52), channel_id=1, source_target_pairs={{0,1},{1,2},{2,3},{3,4},{4,5},{5,6},{6,7},{7,0},{8,9},{9,10},{10,1... | collective-permute-start | bytes 294920 | tf_op jit(solution)/shard_map/ppermute | solution.py:174
  33.4 5.1 %collective-permute-start.5 = (f32[8,128]{1,0:T(8,128)S(1)}, f32[8,128]{1,0:T(8,128)S(1)}, u32[]{:S(2)}, u32[]{:S(2)}) collective-permute-start(f32[8,128]{1,0:T(8,128)S(1)} %get-tuple-element.51), channel_id=1, source_target_pairs={{8,0},{16,8},{24,16},{32,24},{40,32},{48,40},{56,48},{64,56},{72,6... | collective-permute-start | bytes 12296 | tf_op jit(solution)/shard_map/ppermute | solution.py:177
  39.5 6.1 %forward2.1 = (f32[3,32,8,256]{3,2,1,0:T(8,128)S(1)}, f32[3,34,8,256]{3,2,1,0:T(8,128)S(1)}, f32[8,128]{1,0:T(8,128)S(1)}, f32[8,128]{1,0:T(8,128)S(1)}, f32[96,256]{1,0:T(8,128)S(1)}, /*index=5*/f32[96,256]{1,0:T(8,128)S(1)}) custom-call(s32[5]{0:T(128)S(1)} %stack.39.r_0_.meta_ref, f32[6,3,3,32,8,256]{5,4,3,2,1,0:T(8,128)S(1)} %copy-done.1, ...), custom_call_target="tpu_custom_call" | custom-call | tf_op jit(solution)/shard_map/forward2/pallas_call | solution.py:37
  45.6 2.5 %collective-permute-start.10 = (f32[96,256]{1,0:T(8,128)S(1)}, f32[96,256]{1,0:T(8,128)S(1)}, u32[]{:S(2)}, u32[]{:S(2)}) collective-permute-start(f32[96,256]{1,0:T(8,128)S(1)} %get-tuple-element.58), channel_id=1, source_target_pairs={{0,1},{1,2},{2,3},{3,4},{4,5},{5,6},{6,7},{7,0},{8,9},{9,10},{10,1... | collective-permute-start | bytes 294920 | tf_op jit(solution)/shard_map/ppermute | solution.py:174
  48.1 1.3 collective-permute-start.11
  49.4 5.1 %collective-permute-start.9 = (f32[8,128]{1,0:T(8,128)S(1)}, f32[8,128]{1,0:T(8,128)S(1)}, u32[]{:S(2)}, u32[]{:S(2)}) collective-permute-start(f32[8,128]{1,0:T(8,128)S(1)} %get-tuple-element.57), channel_id=1, source_target_pairs={{8,0},{16,8},{24,16},{32,24},{40,32},{48,40},{56,48},{64,56},{72,6... | collective-permute-start | bytes 12296 | tf_op jit(solution)/shard_map/ppermute | solution.py:177
  55.5 6.2 %forward3.1 = (f32[3,32,8,256]{3,2,1,0:T(8,128)S(1)}, f32[3,34,8,256]{3,2,1,0:T(8,128)S(1)}, f32[8,128]{1,0:T(8,128)S(1)}, f32[8,128]{1,0:T(8,128)S(1)}, f32[96,256]{1,0:T(8,128)S(1)}, /*index=5*/f32[96,256]{1,0:T(8,128)S(1)}) custom-call(s32[5]{0:T(128)S(1)} %stack.39.r_0_.meta_ref, f32[6,3,3,32,8,256]{5,4,3,2,1,0:T(8,128)S(1)} %copy-done.1, ...), custom_call_target="tpu_custom_call" | custom-call | tf_op jit(solution)/shard_map/forward3/pallas_call | solution.py:37
  61.7 1.3 collective-permute-start.14
  63.0 2.5 %collective-permute-start.15 = (f32[96,256]{1,0:T(8,128)S(1)}, f32[96,256]{1,0:T(8,128)S(1)}, u32[]{:S(2)}, u32[]{:S(2)}) collective-permute-start(f32[96,256]{1,0:T(8,128)S(1)} %get-tuple-element.65), channel_id=1, source_target_pairs={{1,0},{2,1},{3,2},{4,3},{5,4},{6,5},{7,6},{0,7},{9,8},{10,9},{11,1... | collective-permute-start | bytes 294920 | tf_op jit(solution)/shard_map/ppermute | solution.py:175
  65.6 5.1 %collective-permute-start.13 = (f32[8,128]{1,0:T(8,128)S(1)}, f32[8,128]{1,0:T(8,128)S(1)}, u32[]{:S(2)}, u32[]{:S(2)}) collective-permute-start(f32[8,128]{1,0:T(8,128)S(1)} %get-tuple-element.63), channel_id=1, source_target_pairs={{8,0},{16,8},{24,16},{32,24},{40,32},{48,40},{56,48},{64,56},{72,6... | collective-permute-start | bytes 12296 | tf_op jit(solution)/shard_map/ppermute | solution.py:177
  71.6 6.1 %backward2.1 = (f32[3,34,8,256]{3,2,1,0:T(8,128)S(1)}, f32[8,128]{1,0:T(8,128)S(1)}, f32[8,128]{1,0:T(8,128)S(1)}, f32[96,256]{1,0:T(8,128)S(1)}, f32[96,256]{1,0:T(8,128)S(1)}) custom-call(s32[5]{0:T(128)S(1)} %stack.39.r_0_.meta_ref, f32[6,3,3,32,8,256]{5,4,3,2,1,0:T(8,128)S(1)} %copy-done.1, f32[3,3,32,8,256]{4,3,2,1,0:T(8,128)S(1)} %copy-done.3, ...), custom_call_target="tpu_custom_call" | custom-call | tf_op jit(solution)/shard_map/backward2/pallas_call | solution.py:37
  77.8 3.7 %collective-permute-start.19 = (f32[96,256]{1,0:T(8,128)S(1)}, f32[96,256]{1,0:T(8,128)S(1)}, u32[]{:S(2)}, u32[]{:S(2)}) collective-permute-start(f32[96,256]{1,0:T(8,128)S(1)} %get-tuple-element.70), channel_id=1, source_target_pairs={{1,0},{2,1},{3,2},{4,3},{5,4},{6,5},{7,6},{0,7},{9,8},{10,9},{11,1... | collective-permute-start | bytes 294920 | tf_op jit(solution)/shard_map/ppermute | solution.py:175
  81.6 5.1 %collective-permute-start.17 = (f32[8,128]{1,0:T(8,128)S(1)}, f32[8,128]{1,0:T(8,128)S(1)}, u32[]{:S(2)}, u32[]{:S(2)}) collective-permute-start(f32[8,128]{1,0:T(8,128)S(1)} %get-tuple-element.68), channel_id=1, source_target_pairs={{8,0},{16,8},{24,16},{32,24},{40,32},{48,40},{56,48},{64,56},{72,6... | collective-permute-start | bytes 12296 | tf_op jit(solution)/shard_map/ppermute | solution.py:177
  87.7 6.1 %backward1.1 = (f32[3,34,8,256]{3,2,1,0:T(8,128)S(1)}, f32[8,128]{1,0:T(8,128)S(1)}, f32[8,128]{1,0:T(8,128)S(1)}, f32[96,256]{1,0:T(8,128)S(1)}, f32[96,256]{1,0:T(8,128)S(1)}) custom-call(s32[5]{0:T(128)S(1)} %stack.39.r_0_.meta_ref, f32[6,3,3,32,8,256]{5,4,3,2,1,0:T(8,128)S(1)} %copy-done.1, f32[3,3,32,8,256]{4,3,2,1,0:T(8,128)S(1)} %copy-done.3, ...), custom_call_target="tpu_custom_call" | custom-call | tf_op jit(solution)/shard_map/backward1/pallas_call | solution.py:37
  93.8 3.8 %collective-permute-start.23 = (f32[96,256]{1,0:T(8,128)S(1)}, f32[96,256]{1,0:T(8,128)S(1)}, u32[]{:S(2)}, u32[]{:S(2)}) collective-permute-start(f32[96,256]{1,0:T(8,128)S(1)} %get-tuple-element.75), channel_id=1, source_target_pairs={{1,0},{2,1},{3,2},{4,3},{5,4},{6,5},{7,6},{0,7},{9,8},{10,9},{11,1... | collective-permute-start | bytes 294920 | tf_op jit(solution)/shard_map/ppermute | solution.py:175
  97.7 5.1 %collective-permute-start.21 = (f32[8,128]{1,0:T(8,128)S(1)}, f32[8,128]{1,0:T(8,128)S(1)}, u32[]{:S(2)}, u32[]{:S(2)}) collective-permute-start(f32[8,128]{1,0:T(8,128)S(1)} %get-tuple-element.73), channel_id=1, source_target_pairs={{8,0},{16,8},{24,16},{32,24},{40,32},{48,40},{56,48},{64,56},{72,6... | collective-permute-start | bytes 12296 | tf_op jit(solution)/shard_map/ppermute | solution.py:177
  102.7 2.2 %prep.1 = (bf16[1024,1024]{1,0:T(8,128)(2,1)S(1)}, bf16[256,1024]{1,0:T(8,128)(2,1)S(1)}, bf16[128,2048]{1,0:T(8,128)(2,1)S(1)}, f32[8,128]{1,0:T(8,128)S(1)}, s32[1,1024]{1,0:T(1,128)S(1)}) custom-call(s32[5]{0:T(128)S(1)} %stack.39.r_0_.meta_ref, s32[64,128]{1,0:T(8,128)S(1)} %bitcast.20, s32[64,128]{1,0:T(8,128)S(1)} %bitcast.21, s32[1,1024]{1,0:T(1,128)S(1)} %bitcast.17, ...), custom_call_target="tpu_custom_call" | custom-call | tf_op jit(solution)/shard_map/prep/pallas_call | solution.py:37
  105.0 3.8 %backward0.1.s_ref = f32[3,32,8,256]{3,2,1,0:T(8,128)S(1)} custom-call(s32[5]{0:T(128)S(1)} %stack.39.r_0_.meta_ref, f32[6,3,3,32,8,256]{5,4,3,2,1,0:T(8,128)S(1)} %copy-done.1, f32[3,3,32,8,256]{4,3,2,1,0:T(8,128)S(1)} %copy-done.3, s32[32,8,256]{2,1,0:T(8,128)S(1)} %copy-done.5, f32[3,32,8,256]{3,2,1,0:T(8,128)S(1)} %get-tuple-element.60.r_4_, ...), custom_call_target="tpu_custom_call" | custom-call | tf_op jit(solution)/shard_map/backward0/pallas_call | solution.py:37
  108.9 2.8 %terms.1 = f32[1024,128]{1,0:T(8,128)S(1)} custom-call(f32[3,32,8,256]{3,2,1,0:T(8,128)S(1)} %backward0.1.s_ref, bf16[256,1024]{1,0:T(8,128)(2,1)S(1)} %get-tuple-element.76.rt_ref, bf16[1024,1024]{1,0:T(8,128)(2,1)S(1)} %get-tuple-element.77.kh_ref, s32[1,1024]{1,0:T(1,128)S(1)} %get-tuple-element.78.lo_ref, s32[1,1024]{1,0:T(1,128)S(1)} %bitcast.18, ...), custom_call_target="tpu_custom_call" | custom-call | tf_op jit(solution)/shard_map/terms/pallas_call | solution.py:37
  112.5 9.2 %all-to-all-start = ((f32[128,8,128]{2,1,0:T(8,128)}), f32[128,8,128]{2,1,0:T(8,128)}, u32[]{:S(2)}, u32[]{:S(2)}) async-start(f32[128,8,128]{2,1,0:T(8,128)} %bitcast.16), calls=%async_computation | async-start | bytes 1048576 | tf_op jit(solution)/shard_map/all_to_all | solution.py:325
  121.7 1.9 %copy.16 = f32[64,16,16]{1,0,2:T(8,128)} copy(f32[64,16,16]{0,2,1:T(8,128)} %param.23) | data formatting | bytes 131072 | tf_op jit(solution)/shard_map/transpose | solution.py:299
  124.9 10.1 %all-to-all-done.got_ref = f32[128,8,128]{2,1,0:T(8,128)} async-done(((f32[128,8,128]{2,1,0:T(8,128)}), f32[128,8,128]{2,1,0:T(8,128)}, u32[]{:S(2)}, u32[]{:S(2)}) %all-to-all-start) | async-done | bytes 524320 | tf_op jit(solution)/shard_map/all_to_all | solution.py:325
  136.0 1.5 solve.1
  137.6 18.0 %all_to_all.10.table_ref = f32[128,8,128]{2,1,0:T(8,128)S(1)} all-to-all(f32[128,8,128]{2,1,0:T(8,128)S(1)} %solve.1), channel_id=1, replica_groups=mesh['gx'=16,'gy'=8] {'gx','gy'}, dimensions={0} | all-to-all | bytes 1048576 | tf_op jit(solution)/shard_map/all_to_all | solution.py:327
  155.6 3.4 %back.1 = f32[3,32,8,256]{3,2,1,0:T(8,128)} custom-call(f32[128,8,128]{2,1,0:T(8,128)S(1)} %all_to_all.10.table_ref, f32[3,32,8,256]{3,2,1,0:T(8,128)S(1)} %backward0.1.s_ref, bf16[256,1024]{1,0:T(8,128)(2,1)S(1)} %copy-done.11, bf16[1024,1024]{1,0:T(8,128)(2,1)S(1)} %copy-done.7, s32[1,1024]{1,0:T(1,128)S(1)} %get-tuple-element.78.lo_ref, ...), custom_call_target="tpu_custom_call" | custom-call | tf_op jit(solution)/shard_map/back/pallas_call | solution.py:328
  (81 shorter events, 12.5 us)
Async XLA Ops:
  8.0 9.8 %collective-permute-start.2 = (f32[96,256]{1,0:T(8,128)}, f32[96,256]{1,0:T(8,128)S(1)}, u32[]{:S(2)}, u32[]{:S(2)}) collective-permute-start(f32[96,256]{1,0:T(8,128)} %get-tuple-element.46), channel_id=1, source_target_pairs={{0,1},{1,2},{2,3},{3,4},{4,5},{5,6},{6,7},{7,0},{8,9},{9,10},{10,1... | collective-permute-start | bytes 294920 | tf_op jit(solution)/shard_map/ppermute | solution.py:174
  10.6 7.2 %collective-permute-start.3 = (f32[96,256]{1,0:T(8,128)}, f32[96,256]{1,0:T(8,128)}, u32[]{:S(2)}, u32[]{:S(2)}) collective-permute-start(f32[96,256]{1,0:T(8,128)} %get-tuple-element.47), channel_id=1, source_target_pairs={{1,0},{2,1},{3,2},{4,3},{5,4},{6,5},{7,6},{0,7},{9,8},{10,9},{11,1... | collective-permute-start | bytes 294920 | tf_op jit(solution)/shard_map/ppermute | solution.py:175
  10.6 7.2 %collective-permute-start = (f32[8,128]{1,0:T(8,128)S(1)}, f32[8,128]{1,0:T(8,128)S(1)}, u32[]{:S(2)}, u32[]{:S(2)}) collective-permute-start(f32[8,128]{1,0:T(8,128)S(1)} %get-tuple-element.44), channel_id=1, source_target_pairs={{0,8},{8,16},{16,24},{24,32},{32,40},{40,48},{48,56},{56,64},{64,7... | collective-permute-start | bytes 12296 | tf_op jit(solution)/shard_map/ppermute | solution.py:176
  11.9 5.9 %collective-permute-start.1 = (f32[8,128]{1,0:T(8,128)S(1)}, f32[8,128]{1,0:T(8,128)S(1)}, u32[]{:S(2)}, u32[]{:S(2)}) collective-permute-start(f32[8,128]{1,0:T(8,128)S(1)} %get-tuple-element.45), channel_id=1, source_target_pairs={{8,0},{16,8},{24,16},{32,24},{40,32},{48,40},{56,48},{64,56},{72,6... | collective-permute-start | bytes 12296 | tf_op jit(solution)/shard_map/ppermute | solution.py:177
  24.0 15.4 %copy-start.1 = (f32[6,3,3,32,8,256]{5,4,3,2,1,0:T(8,128)S(1)}, f32[6,3,3,32,8,256]{5,4,3,2,1,0:T(8,128)}, u32[]{:S(2)}) copy-start(f32[6,3,3,32,8,256]{5,4,3,2,1,0:T(8,128)} %r_1_.11) | copy-start | bytes 42467332
  30.7 8.8 %collective-permute-start.6 = (f32[96,256]{1,0:T(8,128)S(1)}, f32[96,256]{1,0:T(8,128)S(1)}, u32[]{:S(2)}, u32[]{:S(2)}) collective-permute-start(f32[96,256]{1,0:T(8,128)S(1)} %get-tuple-element.52), channel_id=1, source_target_pairs={{0,1},{1,2},{2,3},{3,4},{4,5},{5,6},{6,7},{7,0},{8,9},{9,10},{10,1... | collective-permute-start | bytes 294920 | tf_op jit(solution)/shard_map/ppermute | solution.py:174
  33.3 6.2 %collective-permute-start.7 = (f32[96,256]{1,0:T(8,128)S(1)}, f32[96,256]{1,0:T(8,128)S(1)}, u32[]{:S(2)}, u32[]{:S(2)}) collective-permute-start(f32[96,256]{1,0:T(8,128)S(1)} %get-tuple-element.53), channel_id=1, source_target_pairs={{1,0},{2,1},{3,2},{4,3},{5,4},{6,5},{7,6},{0,7},{9,8},{10,9},{11,1... | collective-permute-start | bytes 294920 | tf_op jit(solution)/shard_map/ppermute | solution.py:175
  33.4 6.1 %collective-permute-start.4 = (f32[8,128]{1,0:T(8,128)S(1)}, f32[8,128]{1,0:T(8,128)S(1)}, u32[]{:S(2)}, u32[]{:S(2)}) collective-permute-start(f32[8,128]{1,0:T(8,128)S(1)} %get-tuple-element.50), channel_id=1, source_target_pairs={{0,8},{8,16},{16,24},{24,32},{32,40},{40,48},{48,56},{56,64},{64,7... | collective-permute-start | bytes 12296 | tf_op jit(solution)/shard_map/ppermute | solution.py:176
  33.4 6.1 %collective-permute-start.5 = (f32[8,128]{1,0:T(8,128)S(1)}, f32[8,128]{1,0:T(8,128)S(1)}, u32[]{:S(2)}, u32[]{:S(2)}) collective-permute-start(f32[8,128]{1,0:T(8,128)S(1)} %get-tuple-element.51), channel_id=1, source_target_pairs={{8,0},{16,8},{24,16},{32,24},{40,32},{48,40},{56,48},{64,56},{72,6... | collective-permute-start | bytes 12296 | tf_op jit(solution)/shard_map/ppermute | solution.py:177
  45.6 9.9 %collective-permute-start.10 = (f32[96,256]{1,0:T(8,128)S(1)}, f32[96,256]{1,0:T(8,128)S(1)}, u32[]{:S(2)}, u32[]{:S(2)}) collective-permute-start(f32[96,256]{1,0:T(8,128)S(1)} %get-tuple-element.58), channel_id=1, source_target_pairs={{0,1},{1,2},{2,3},{3,4},{4,5},{5,6},{6,7},{7,0},{8,9},{9,10},{10,1... | collective-permute-start | bytes 294920 | tf_op jit(solution)/shard_map/ppermute | solution.py:174
  48.1 7.4 %collective-permute-start.11 = (f32[96,256]{1,0:T(8,128)S(1)}, f32[96,256]{1,0:T(8,128)S(1)}, u32[]{:S(2)}, u32[]{:S(2)}) collective-permute-start(f32[96,256]{1,0:T(8,128)S(1)} %get-tuple-element.59), channel_id=1, source_target_pairs={{1,0},{2,1},{3,2},{4,3},{5,4},{6,5},{7,6},{0,7},{9,8},{10,9},{11,1... | collective-permute-start | bytes 294920 | tf_op jit(solution)/shard_map/ppermute | solution.py:175
  49.4 6.1 %collective-permute-start.8 = (f32[8,128]{1,0:T(8,128)S(1)}, f32[8,128]{1,0:T(8,128)S(1)}, u32[]{:S(2)}, u32[]{:S(2)}) collective-permute-start(f32[8,128]{1,0:T(8,128)S(1)} %get-tuple-element.56), channel_id=1, source_target_pairs={{0,8},{8,16},{16,24},{24,32},{32,40},{40,48},{48,56},{56,64},{64,7... | collective-permute-start | bytes 12296 | tf_op jit(solution)/shard_map/ppermute | solution.py:176
  49.4 6.1 %collective-permute-start.9 = (f32[8,128]{1,0:T(8,128)S(1)}, f32[8,128]{1,0:T(8,128)S(1)}, u32[]{:S(2)}, u32[]{:S(2)}) collective-permute-start(f32[8,128]{1,0:T(8,128)S(1)} %get-tuple-element.57), channel_id=1, source_target_pairs={{8,0},{16,8},{24,16},{32,24},{40,32},{48,40},{56,48},{64,56},{72,6... | collective-permute-start | bytes 12296 | tf_op jit(solution)/shard_map/ppermute | solution.py:177
  61.7 9.9 %collective-permute-start.14 = (f32[96,256]{1,0:T(8,128)S(1)}, f32[96,256]{1,0:T(8,128)S(1)}, u32[]{:S(2)}, u32[]{:S(2)}) collective-permute-start(f32[96,256]{1,0:T(8,128)S(1)} %get-tuple-element.64), channel_id=1, source_target_pairs={{0,1},{1,2},{2,3},{3,4},{4,5},{5,6},{6,7},{7,0},{8,9},{9,10},{10,1... | collective-permute-start | bytes 294920 | tf_op jit(solution)/shard_map/ppermute | solution.py:174
  63.0 8.6 %collective-permute-start.15 = (f32[96,256]{1,0:T(8,128)S(1)}, f32[96,256]{1,0:T(8,128)S(1)}, u32[]{:S(2)}, u32[]{:S(2)}) collective-permute-start(f32[96,256]{1,0:T(8,128)S(1)} %get-tuple-element.65), channel_id=1, source_target_pairs={{1,0},{2,1},{3,2},{4,3},{5,4},{6,5},{7,6},{0,7},{9,8},{10,9},{11,1... | collective-permute-start | bytes 294920 | tf_op jit(solution)/shard_map/ppermute | solution.py:175
  65.6 6.0 %collective-permute-start.12 = (f32[8,128]{1,0:T(8,128)S(1)}, f32[8,128]{1,0:T(8,128)S(1)}, u32[]{:S(2)}, u32[]{:S(2)}) collective-permute-start(f32[8,128]{1,0:T(8,128)S(1)} %get-tuple-element.62), channel_id=1, source_target_pairs={{0,8},{8,16},{16,24},{24,32},{32,40},{40,48},{48,56},{56,64},{64,7... | collective-permute-start | bytes 12296 | tf_op jit(solution)/shard_map/ppermute | solution.py:176
  65.6 6.0 %collective-permute-start.13 = (f32[8,128]{1,0:T(8,128)S(1)}, f32[8,128]{1,0:T(8,128)S(1)}, u32[]{:S(2)}, u32[]{:S(2)}) collective-permute-start(f32[8,128]{1,0:T(8,128)S(1)} %get-tuple-element.63), channel_id=1, source_target_pairs={{8,0},{16,8},{24,16},{32,24},{40,32},{48,40},{56,48},{64,56},{72,6... | collective-permute-start | bytes 12296 | tf_op jit(solution)/shard_map/ppermute | solution.py:177
  77.7 9.9 %collective-permute-start.18 = (f32[96,256]{1,0:T(8,128)S(1)}, f32[96,256]{1,0:T(8,128)S(1)}, u32[]{:S(2)}, u32[]{:S(2)}) collective-permute-start(f32[96,256]{1,0:T(8,128)S(1)} %get-tuple-element.69), channel_id=1, source_target_pairs={{0,1},{1,2},{2,3},{3,4},{4,5},{5,6},{6,7},{7,0},{8,9},{9,10},{10,1... | collective-permute-start | bytes 294920 | tf_op jit(solution)/shard_map/ppermute | solution.py:174
  77.8 9.8 %collective-permute-start.19 = (f32[96,256]{1,0:T(8,128)S(1)}, f32[96,256]{1,0:T(8,128)S(1)}, u32[]{:S(2)}, u32[]{:S(2)}) collective-permute-start(f32[96,256]{1,0:T(8,128)S(1)} %get-tuple-element.70), channel_id=1, source_target_pairs={{1,0},{2,1},{3,2},{4,3},{5,4},{6,5},{7,6},{0,7},{9,8},{10,9},{11,1... | collective-permute-start | bytes 294920 | tf_op jit(solution)/shard_map/ppermute | solution.py:175
  81.6 6.0 %collective-permute-start.16 = (f32[8,128]{1,0:T(8,128)S(1)}, f32[8,128]{1,0:T(8,128)S(1)}, u32[]{:S(2)}, u32[]{:S(2)}) collective-permute-start(f32[8,128]{1,0:T(8,128)S(1)} %get-tuple-element.67), channel_id=1, source_target_pairs={{0,8},{8,16},{16,24},{24,32},{32,40},{40,48},{48,56},{56,64},{64,7... | collective-permute-start | bytes 12296 | tf_op jit(solution)/shard_map/ppermute | solution.py:176
  81.6 6.0 %collective-permute-start.17 = (f32[8,128]{1,0:T(8,128)S(1)}, f32[8,128]{1,0:T(8,128)S(1)}, u32[]{:S(2)}, u32[]{:S(2)}) collective-permute-start(f32[8,128]{1,0:T(8,128)S(1)} %get-tuple-element.68), channel_id=1, source_target_pairs={{8,0},{16,8},{24,16},{32,24},{40,32},{48,40},{56,48},{64,56},{72,6... | collective-permute-start | bytes 12296 | tf_op jit(solution)/shard_map/ppermute | solution.py:177
  87.6 15.1 %copy-start.17 = (s32[1024]{0:T(1024)S(1)}, s32[1024]{0:T(1024)}, u32[]{:S(2)}) copy-start(s32[1024]{0:T(1024)} %param.16) | copy-start | bytes 12292
  87.7 15.1 %copy-start.18 = (s32[8192]{0:T(1024)S(1)}, s32[8192]{0:T(1024)}, u32[]{:S(2)}) copy-start(s32[8192]{0:T(1024)} %param.21) | copy-start | bytes 98308
  87.7 15.0 %copy-start.19 = (s32[8192]{0:T(1024)S(1)}, s32[8192]{0:T(1024)}, u32[]{:S(2)}) copy-start(s32[8192]{0:T(1024)} %param.22) | copy-start | bytes 98308
  93.8 11.2 %collective-permute-start.22 = (f32[96,256]{1,0:T(8,128)S(1)}, f32[96,256]{1,0:T(8,128)S(1)}, u32[]{:S(2)}, u32[]{:S(2)}) collective-permute-start(f32[96,256]{1,0:T(8,128)S(1)} %get-tuple-element.74), channel_id=1, source_target_pairs={{0,1},{1,2},{2,3},{3,4},{4,5},{5,6},{6,7},{7,0},{8,9},{9,10},{10,1... | collective-permute-start | bytes 294920 | tf_op jit(solution)/shard_map/ppermute | solution.py:174
  93.8 11.2 %collective-permute-start.23 = (f32[96,256]{1,0:T(8,128)S(1)}, f32[96,256]{1,0:T(8,128)S(1)}, u32[]{:S(2)}, u32[]{:S(2)}) collective-permute-start(f32[96,256]{1,0:T(8,128)S(1)} %get-tuple-element.75), channel_id=1, source_target_pairs={{1,0},{2,1},{3,2},{4,3},{5,4},{6,5},{7,6},{0,7},{9,8},{10,9},{11,1... | collective-permute-start | bytes 294920 | tf_op jit(solution)/shard_map/ppermute | solution.py:175
  97.6 7.3 %collective-permute-start.20 = (f32[8,128]{1,0:T(8,128)S(1)}, f32[8,128]{1,0:T(8,128)S(1)}, u32[]{:S(2)}, u32[]{:S(2)}) collective-permute-start(f32[8,128]{1,0:T(8,128)S(1)} %get-tuple-element.72), channel_id=1, source_target_pairs={{0,8},{8,16},{16,24},{24,32},{32,40},{40,48},{48,56},{56,64},{64,7... | collective-permute-start | bytes 12296 | tf_op jit(solution)/shard_map/ppermute | solution.py:176
  97.7 7.3 %collective-permute-start.21 = (f32[8,128]{1,0:T(8,128)S(1)}, f32[8,128]{1,0:T(8,128)S(1)}, u32[]{:S(2)}, u32[]{:S(2)}) collective-permute-start(f32[8,128]{1,0:T(8,128)S(1)} %get-tuple-element.73), channel_id=1, source_target_pairs={{8,0},{16,8},{24,16},{32,24},{40,32},{48,40},{56,48},{64,56},{72,6... | collective-permute-start | bytes 12296 | tf_op jit(solution)/shard_map/ppermute | solution.py:177
  108.9 46.7 %copy-start.21 = (f32[3,1024]{1,0:T(4,128)S(1)}, f32[3,1024]{1,0:T(4,128)}, u32[]{:S(2)}) copy-start(f32[3,1024]{1,0:T(4,128)} %back_ref.1) | copy-start | bytes 36868
  112.5 43.1 %copy-start.7 = (bf16[1024,1024]{1,0:T(8,128)(2,1)S(1)}, bf16[1024,1024]{1,0:T(8,128)(2,1)}, u32[]{:S(2)}) copy-start(bf16[1024,1024]{1,0:T(8,128)(2,1)} %copy-done.6) | copy-start | bytes 6291460
  112.5 43.1 %copy-start.11 = (bf16[256,1024]{1,0:T(8,128)(2,1)S(1)}, bf16[256,1024]{1,0:T(8,128)(2,1)}, u32[]{:S(2)}) copy-start(bf16[256,1024]{1,0:T(8,128)(2,1)} %copy-done.10) | copy-start | bytes 1572868
  112.5 22.5 %all-to-all-start = ((f32[128,8,128]{2,1,0:T(8,128)}), f32[128,8,128]{2,1,0:T(8,128)}, u32[]{:S(2)}, u32[]{:S(2)}) async-start(f32[128,8,128]{2,1,0:T(8,128)} %bitcast.16), calls=%async_computation | async-start | bytes 1048576 | tf_op jit(solution)/shard_map/all_to_all | solution.py:325
  (17 other events, 100.7 us)

commit v2 on v1

v2 whole, which is shorter than its diff:
```python
import jax
import jax.numpy as jnp
from jax import lax
from jax.experimental import pallas as pl
from jax.experimental.pallas import tpu as pltpu
from jax.sharding import PartitionSpec as P

F32 = jnp.float32
BF16 = jnp.bfloat16
UNROLL = 8
PARTS = 4
VMEM_SPEC = pl.BlockSpec(memory_space=pltpu.VMEM)
SMEM_SPEC = pl.BlockSpec(memory_space=pltpu.SMEM)


def iota(shape, dim):
    return lax.broadcasted_iota(jnp.int32, shape, dim)


def split3(x):
    a = x.astype(BF16)
    r = x - a.astype(F32)
    b = r.astype(BF16)
    c = (r - b.astype(F32)).astype(BF16)
    return a, b, c


def dot(a, b, dims):
    return lax.dot_general(a, b, (dims, ((), ())), preferred_element_type=F32)


def in_vmem(x):
    return pltpu.with_memory_space_constraint(x, pltpu.VMEM)


def call(body, outs, ins, smem=0, hbm=(), scratch=(), name=None, limit=None):
    specs, args = [], []
    for k, x in enumerate(ins):
        if k < smem:
            specs.append(SMEM_SPEC)
        elif k in hbm:
            specs.append(pl.BlockSpec(memory_space=pltpu.HBM))
            x = pltpu.with_memory_space_constraint(x, pltpu.HBM)
        else:
            specs.append(VMEM_SPEC)
            x = in_vmem(x)
        args.append(x)
    return pl.pallas_call(
        body,
        out_shape=tuple(pltpu.VMEM(s, d) for s, d in outs),
        in_specs=specs,
        out_specs=tuple(VMEM_SPEC for _ in outs),
        scratch_shapes=list(scratch),
        compiler_params=pltpu.CompilerParams(vmem_limit_bytes=limit or (8 << 20)),
        name=name,
    )(*args)


def emit_edges(new, z, nz, edges, y_odd, ya_ref, yb_ref):
    xlo, xhi = edges
    lane = iota((8, 128), 1)
    for j in range(3):
        at = j * nz + z
        xlo = jnp.where(lane == at, pltpu.roll(new[j][:, :128], at, 1), xlo)
        xhi = jnp.where(lane == at, pltpu.roll(new[j][:, -128:], (at + 1) % 128, 1), xhi)
        first, last = new[j][0:1, :], new[j][-1:, :]
        ya_ref[pl.ds(at, 1), :] = jnp.where(y_odd, first, last)
        yb_ref[pl.ds(at, 1), :] = jnp.where(y_odd, last, first)
    return xlo, xhi


def store_columns(x_odd, edges, xa_ref, xb_ref):
    xlo, xhi = edges
    xa_ref[...] = jnp.where(x_odd, xlo, xhi)
    xb_ref[...] = jnp.where(x_odd, xhi, xlo)


def zero_ends(ref, nz):
    zero = jnp.zeros(ref.shape[2:], F32)
    for j in range(3):
        ref[j, 0] = zero
        ref[j, nz + 1] = zero


def chunk_copies(pairs, sems, part, size, axes):
    out = []
    for k, ((src, dst), axis) in enumerate(zip(pairs, axes)):
        at = (slice(None),) * axis + (pl.ds(part * size, size),)
        out.append(pltpu.make_async_copy(src.at[at], dst.at[at], sems.at[k, part]))
    return out


def first_body(meta_ref, rhs_hbm, piv_hbm, col_hbm, rhs_ref, piv_ref, col_ref, v_ref, xa_ref, xb_ref, ya_ref, yb_ref, sems):
    nz = rhs_ref.shape[1]
    size = nz // PARTS
    pairs = [(rhs_hbm, rhs_ref), (piv_hbm, piv_ref), (col_hbm, col_ref)]
    for part in range(PARTS):
        for c in chunk_copies(pairs, sems, part, size, (1, 2, 0)):
            c.start()
    zero_ends(v_ref, nz)
    x_odd = meta_ref[5] > 0
    y_odd = meta_ref[6] > 0

    def step(z, edges):
        rhs = [rhs_ref[j, z] for j in range(3)]
        chosen = col_ref[z] == 0
        new = []
        for i in range(3):
            p = piv_ref[i, 0, z] * rhs[0] + piv_ref[i, 1, z] * rhs[1] + piv_ref[i, 2, z] * rhs[2]
            p = jnp.where(chosen, p, 0.0)
            v_ref[i, z + 1] = p
            new.append(p)
        return emit_edges(new, z, nz, edges, y_odd, ya_ref, yb_ref)

    def block(part, edges):
        for c in chunk_copies(pairs, sems, part, size, (1, 2, 0)):
            c.wait()
        return lax.fori_loop(0, size, lambda k, e: step(part * size + k, e), edges, unroll=UNROLL)

    zero = jnp.zeros((8, 128), F32)
    edges = lax.fori_loop(0, PARTS, block, (zero, zero))
    store_columns(x_odd, edges, xa_ref, xb_ref)


def turn_body(colour, forward, final, load, *refs):
    (meta_ref, coup_ref, piv_ref, col_ref, base_ref, v_ref, hxa_ref, hxb_ref, hya_ref, hyb_ref) = refs[:10]
    refs = list(refs[10:])
    if load:
        sems = refs.pop()
        coup_hbm, coup_ref = coup_ref, refs.pop(0)
    u_ref = refs.pop(0) if forward else None
    nv_ref, *edge_refs = refs
    nz = base_ref.shape[1]
    ny, nx = base_ref.shape[2:]
    size = nz // PARTS
    pairs = [(coup_hbm, coup_ref)] if load else []
    if load:
        for part in range(PARTS):
            for c in chunk_copies(pairs, sems, part, size, (3,)):
                c.start()
    lane = iota((ny, 128), 1)
    row = iota((ny, nx), 0)
    x_odd = meta_ref[5] > 0
    y_odd = meta_ref[6] > 0
    has = [meta_ref[k] > 0 for k in range(1, 5)]
    hxa, hxb = hxa_ref[...], hxb_ref[...]
    hxlo = jnp.where(has[0], jnp.where(x_odd, hxa, hxb), 0.0)
    hxhi = jnp.where(has[1], jnp.where(x_odd, hxb, hxa), 0.0)
    if not final:
        zero_ends(nv_ref, nz)

    def step(z, edges):
        acc = [jnp.zeros((ny, nx), F32) for _ in range(3)]
        old = []
        for j in range(3):
            at = j * nz + z
            vc = v_ref[j, z + 1]
            old.append(vc)
            xm = pltpu.roll(vc, 1, 1)
            head = jnp.where(lane == 0, pltpu.roll(hxlo, (128 - at) % 128, 1), xm[:, :128])
            xm = jnp.concatenate([head, xm[:, 128:]], axis=1)
            xp = pltpu.roll(vc, nx - 1, 1)
            tail = jnp.where(lane == 127, pltpu.roll(hxhi, 127 - at, 1), xp[:, -128:])
            xp = jnp.concatenate([xp[:, :-128], tail], axis=1)
            ha, hb = hya_ref[pl.ds(at, 1), :], hyb_ref[pl.ds(at, 1), :]
            hylo = jnp.where(has[2], jnp.where(y_odd, ha, hb), 0.0)
            hyhi = jnp.where(has[3], jnp.where(y_odd, hb, ha), 0.0)
            ym = jnp.where(row == 0, hylo, pltpu.roll(vc, 1, 0))
            yp = jnp.where(row == ny - 1, hyhi, pltpu.roll(vc, ny - 1, 0))
            zm = v_ref[j, z]
            zp = v_ref[j, z + 2]
            for i in range(3):
                t = coup_ref[0, i, j, z] * xm + coup_ref[1, i, j, z] * xp
                t = t + (coup_ref[2, i, j, z] * ym + coup_ref[3, i, j, z] * yp)
                t = t + (coup_ref[4, i, j, z] * zm + coup_ref[5, i, j, z] * zp)
                acc[i] = acc[i] + t
        chosen = col_ref[z] == colour
        base = [base_ref[j, z] for j in range(3)]
        cur = [base[j] - acc[j] for j in range(3)]
        new = []
        for i in range(3):
            p = piv_ref[i, 0, z] * cur[0] + piv_ref[i, 1, z] * cur[1] + piv_ref[i, 2, z] * cur[2]
            if forward:
                u_ref[i, z] = jnp.where(chosen, cur[i], base[i])
                keep_old = 0.0 if colour == 3 else old[i]
            else:
                keep_old = old[i]
            p = jnp.where(chosen, p, keep_old)
            if final:
                nv_ref[i, z] = p
            else:
                nv_ref[i, z + 1] = p
            new.append(p)
        if final:
            return edges
        return emit_edges(new, z, nz, edges, y_odd, edge_refs[2], edge_refs[3])

    def block(part, edges):
        for c in chunk_copies(pairs, sems, part, size, (3,)):
            c.wait()
        return lax.fori_loop(0, size, lambda k, e: step(part * size + k, e), edges, unroll=UNROLL)

    zero = jnp.zeros((ny, 128), F32)
    if load:
        edges = lax.fori_loop(0, PARTS, block, (zero, zero))
    else:
        edges = lax.fori_loop(0, nz, step, (zero, zero), unroll=UNROLL)
    if not final:
        store_columns(x_odd, edges, edge_refs[0], edge_refs[1])


def swaps(size, odd):
    out = []
    for i in range(odd, size + odd, 2):
        a, b = i % size, (i + 1) % size
        out += [(a, b), (b, a)]
    return out


def halos(edges):
    xa, xb, ya, yb = edges
    nx = lax.axis_size("gx")
    ny = lax.axis_size("gy")
    hxb = lax.ppermute(xb, "gx", swaps(nx, 1))
    hyb = lax.ppermute(yb, "gy", swaps(ny, 1))
    hxa = lax.ppermute(xa, "gx", swaps(nx, 0))
    hya = lax.ppermute(ya, "gy", swaps(ny, 0))
    return hxa, hxb, hya, hyb


def prep_body(meta_ref, slot_ref, count_ref, cells_ref, wells_ref, segs_ref, kh_ref, rt_ref, alive_ref, lo_ref):
    n = cells_ref.shape[1]
    wells = wells_ref[...]
    table = slot_ref[...]
    pick = (iota((table.shape[0], n), 0) == (wells >> 7)).astype(BF16)
    high = dot((table >> 7).astype(F32).astype(BF16), pick, ((0,), (0,)))
    low = dot((table & 127).astype(F32).astype(BF16), pick, ((0,), (0,)))
    slot = jnp.where(iota((128, n), 0) == (wells & 127), high * 128.0 + low, 0.0)
    slot = jnp.sum(slot, axis=0, keepdims=True).astype(jnp.int32)
    segs = segs_ref[...]
    owner = slot >> 6
    tile = meta_ref[0]
    rows = ((owner ^ tile) & 1) * 512 + (owner >> 1) * 8 + (segs & 7)
    lo_ref[...] = (segs >> 3) * 64 + (slot & 63)
    kh_ref[...] = (iota(kh_ref.shape, 0) == rows).astype(F32).astype(BF16)
    rt_ref[...] = (iota(rt_ref.shape, 0) == (cells_ref[...] >> 8)).astype(F32).astype(BF16)
    own_slot = slot_ref[pl.ds(tile // 2, 1), :] - tile * 64
    own_count = jnp.broadcast_to(count_ref[pl.ds(tile // 2, 1), :].astype(F32), (8, 128)).astype(BF16)
    match = (iota((128, 128), 0) == own_slot).astype(F32).astype(BF16)
    counts = dot(own_count, match, ((1,), (1,)))
    alive_ref[0:8] = (iota((8, 128), 0).astype(F32) < counts).astype(F32)
    alive_ref[8:16] = ((iota((8, 128), 0) + 8).astype(F32) < counts).astype(F32)


def terms_body(s_ref, rt_ref, kh_ref, lo_ref, cells_ref, gather_ref, mine_ref, other_ref):
    n = cells_ref.shape[1]
    rt = rt_ref[...]
    at_col = iota((256, n), 0) == (cells_ref[...] & 255)
    term = jnp.zeros((1, n), F32)
    for i in range(3):
        f = s_ref[i].reshape(256, 256)
        g = sum(dot(h, rt, ((0,), (0,))) for h in split3(f))
        v = jnp.sum(jnp.where(at_col, g, 0.0), axis=0, keepdims=True)
        term = term + gather_ref[pl.ds(i, 1), :] * v
    at_low = iota((128, n), 0) == lo_ref[...]
    stack = jnp.concatenate([jnp.where(at_low, h.astype(F32), 0.0).astype(BF16) for h in split3(term)], axis=0)
    sums = dot(kh_ref[...], stack, ((1,), (1,)))
    sums = sums[:, :128] + sums[:, 128:256] + sums[:, 256:]
    mine_ref[...] = sums[:512]
    other_ref[...] = sums[512:]


def solve_body(got_ref, inv_ref, alive_ref, out_ref):
    alive = alive_ref[:, :64]
    totals = jnp.sum(got_ref[...], axis=0)
    totals = jnp.concatenate([totals[:, :64], totals[:, 64:]], axis=0) * alive
    rows = [jnp.sum(inv_ref[i] * totals, axis=0, keepdims=True) for i in range(16)]
    values = jnp.concatenate(rows, axis=0) * alive
    values = jnp.concatenate([values[:8], values[8:]], axis=1)
    out_ref[...] = jnp.broadcast_to(values[None], out_ref.shape)


def return_body(mine_ref, other_ref, s_ref, rt_ref, kh_ref, lo_ref, cells_ref, back_ref, out_ref):
    n = cells_ref.shape[1]
    g = sum(dot(h, kh_ref[0:512], ((0,), (0,))) for h in split3(mine_ref[...]))
    g = g + sum(dot(h, kh_ref[512:1024], ((0,), (0,))) for h in split3(other_ref[...]))
    values = jnp.sum(jnp.where(iota((128, n), 0) == lo_ref[...], g, 0.0), axis=0, keepdims=True)
    at_col = iota((256, n), 0) == (cells_ref[...] & 255)
    rt = rt_ref[...]
    for i in range(3):
        w = back_ref[pl.ds(i, 1), :] * values
        change = sum(
            dot(rt, jnp.where(at_col, h.astype(F32), 0.0).astype(BF16), ((1,), (1,))) for h in split3(w)
        )
        out_ref[i] = s_ref[i] - change.reshape(32, 8, 256)


def shards(
    rhs,
    couplings,
    pivots,
    colours,
    perf_cells,
    perf_wells,
    perf_segments,
    perf_gather,
    perf_return,
    well_slot,
    seg_count,
    well_inverses,
):
    axes = ("gx", "gy")
    devices = lax.axis_size(axes)
    gx = lax.axis_index("gx")
    gy = lax.axis_index("gy")
    tile = lax.axis_index(axes)
    meta = jnp.stack(
        [
            tile,
            gx > 0,
            gx < lax.axis_size("gx") - 1,
            gy > 0,
            gy < lax.axis_size("gy") - 1,
            gx % 2,
            gy % 2,
        ]
    ).astype(jnp.int32)
    _, nz, ny, nx = rhs.shape
    field = ((3, nz + 2, ny, nx), F32)
    plain = ((3, nz, ny, nx), F32)
    edges = [((ny, 128), F32)] * 2 + [((3 * nz, nx), F32)] * 2
    n = perf_cells.shape[0]
    cells = perf_cells.reshape(1, n)

    rhs, pivots, colours, v, *edge = call(
        first_body,
        [plain, (pivots.shape, F32), (colours.shape, jnp.int32), field] + edges,
        [meta, rhs, pivots, colours],
        smem=1,
        hbm=(1, 2, 3),
        scratch=[pltpu.SemaphoreType.DMA((3, PARTS))],
        name="first",
    )
    base = rhs
    for colour in (1, 2, 3):
        halo = halos(edge)
        load = colour == 1
        got = call(
            lambda *r, c=colour, l=load: turn_body(c, True, False, l, *r),
            ([(couplings.shape, F32)] if load else []) + [plain, field] + edges,
            [meta, couplings, pivots, colours, base, v, *halo],
            smem=1,
            hbm=(1,) if load else (),
            scratch=[pltpu.SemaphoreType.DMA((1, PARTS))] if load else [],
            name=f"forward{colour}",
        )
        if load:
            couplings, *got = got
        base, v, *edge = got
    kh, rt, alive, low = call(
        prep_body,
        [((1024, n), BF16), ((256, n), BF16), ((16, 128), F32), ((1, n), jnp.int32)],
        [
            meta,
            well_slot.reshape(-1, 128),
            seg_count.reshape(-1, 128),
            cells,
            perf_wells.reshape(1, n),
            perf_segments.reshape(1, n),
        ],
        smem=1,
        name="prep",
    )
    for colour in (2, 1, 0):
        halo = halos(edge)
        final = colour == 0
        v, *edge = call(
            lambda *r, c=colour, f=final: turn_body(c, False, f, False, *r),
            [plain] if final else [field] + edges,
            [meta, couplings, pivots, colours, base, v, *halo],
            smem=1,
            name=f"backward{colour}",
        )
    pairs = swaps(lax.axis_size("gy"), 0)
    cores = [[d for d in range(devices) if d % 2 == core] for core in range(2)]
    mine, other = call(
        terms_body, [((512, 128), F32)] * 2, [v, rt, kh, low, cells, perf_gather], name="terms", limit=24 << 20
    )
    mine = mine + lax.ppermute(other, "gy", pairs)
    got = lax.all_to_all(mine.reshape(64, 8, 128), axes, 0, 0, axis_index_groups=cores, tiled=True)
    (values,) = call(
        solve_body, [((64, 8, 128), F32)], [got, well_inverses.transpose(1, 2, 0), alive], name="solve"
    )
    mine = lax.all_to_all(values, axes, 0, 0, axis_index_groups=cores, tiled=True).reshape(512, 128)
    other = lax.ppermute(mine, "gy", pairs)
    return pl.pallas_call(
        return_body,
        out_shape=jax.ShapeDtypeStruct(plain[0], F32),
        in_specs=[VMEM_SPEC] * 8,
        out_specs=VMEM_SPEC,
        compiler_params=pltpu.CompilerParams(vmem_limit_bytes=24 << 20),
        name="back",
    )(*[in_vmem(x) for x in (mine, other, v, rt, kh, low, cells, perf_return)])


def solution(mesh):
    return jax.shard_map(
        shards,
        mesh=mesh,
        in_specs=(
            P(None, None, "gy", "gx"),
            P(None, None, None, None, "gy", "gx"),
            P(None, None, None, "gy", "gx"),
            P(None, "gy", "gx"),
            P(("gx", "gy")),
            P(("gx", "gy")),
            P(("gx", "gy")),
            P(None, ("gx", "gy")),
            P(None, ("gx", "gy")),
            P(),
            P(),
            P(("gx", "gy"), None, None),
        ),
        out_specs=P(None, None, "gy", "gx"),
        check_vma=False,
    )
```

time: 159 us -> 122 us (0.77)
  local copies, waits for them, and re-layouts: 16 us -> 0.13 us
  Pallas kernels: 48.3 us -> 32.5 us
  blocking collectives: 18 us -> 31.1 us
  starting transfers between devices: 61.4 us -> 50.9 us
  waiting for transfers between devices: 15 us -> 7.33 us
    pallas_call x10, Pallas kernels: 44.9 us -> 29.1 us  [call(): pl.pallas_call(body, out_shape=tuple((pltpu.VMEM(s, d) for s, d in outs))...]
    all_to_all x1 -> x2, blocking collectives: 18 us -> 31.1 us  [the longest x1 17.3 us: shards(): lax.all_to_all(mine.reshape(64, 8, 128), axes, 0, 0, axis_index_groups=co...]
    unnamed x48 -> x16, local copies, waits for them, and re-layouts: 12.8 us -> 0.05 us
    all_to_all x1 -> x0, waiting for transfers between devices: 10.1 us -> none  [shards(): lax.all_to_all(totals.reshape(devices, 8, 128), axes, 0, 0, tiled=True)]
    all_to_all x1 -> x0, starting transfers between devices: 9.19 us -> none  [shards(): lax.all_to_all(totals.reshape(devices, 8, 128), axes, 0, 0, tiled=True)]
    ppermute x24 -> x26, waiting for transfers between devices: 4.92 us -> 7.33 us  [the longest x6 4.96 us: halos(): hxb = lax.ppermute(xb, 'gx', swaps(nx, 1))]
    transpose x1 -> x0, local copies, waits for them, and re-layouts: 1.92 us -> none  [shards(): well_inverses.reshape(8, 8, 16, 16).transpose(3, 0, 1, 2)]
    ppermute x24 -> x26, starting transfers between devices: 52.2 us -> 50.9 us  [the longest x6 30.4 us: halos(): hxb = lax.ppermute(xb, 'gx', swaps(nx, 1))]
  transfers between devices with their start and end apart: 25 -> 26, of which waited for: 6 -> 7; matrix products, arithmetic and copies ran while one was open for 2% -> 0% of each run, Pallas kernels for 1% -> 2%
where the time goes in v2:
time: 122 us
  starting transfers between devices  50.9 us (42%)
  Pallas kernels  32.5 us (27%)
  blocking collectives  31.1 us (25%)
  waiting for transfers between devices  7.33 us (6%)
    ppermute x6, starting transfers between devices, halos(): hxb = lax.ppermute(xb, 'gx', swaps(nx, 1))  30.4 us
    pallas_call x10, Pallas kernels, call(): pl.pallas_call(body, out_shape=tuple((pltpu.VMEM(s, d) for s, d in outs))...  29.1 us
    all_to_all x1, blocking collectives, shards(): lax.all_to_all(mine.reshape(64, 8, 128), axes, 0, 0, axis_index_groups=co...  17.3 us
    all_to_all x1, blocking collectives, shards(): lax.all_to_all(values, axes, 0, 0, axis_index_groups=cores, tiled=True)  13.8 us
    ppermute x6, starting transfers between devices, halos(): hya = lax.ppermute(ya, 'gy', swaps(ny, 0))  11.2 us
    ppermute x6, waiting for transfers between devices, halos(): hxb = lax.ppermute(xb, 'gx', swaps(nx, 1))  4.96 us
    ppermute x6, starting transfers between devices, halos(): hyb = lax.ppermute(yb, 'gy', swaps(ny, 1))  3.61 us
    pallas_call x1, Pallas kernels, shards(): pl.pallas_call(return_body, out_shape=jax.ShapeDtypeStruct(plain[0], F32)...  3.37 us
  transfers between devices with their start and end apart: 26, of which 7 were waited for; matrix products, arithmetic and copies ran while one was open for 0% of the time, Pallas kernels for 2%

profile of v2, /device:TPU:1, one launch (start us, length us, event | category | flops | bytes accessed | tf_op | source)
XLA Modules:
  0.0 122.1 jit_solution(3571805709293699889)
XLA Ops:
  0.1 2.8 %first.1 = (f32[3,32,8,256]{3,2,1,0:T(8,128)S(1)}, f32[3,3,32,8,256]{4,3,2,1,0:T(8,128)S(1)}, s32[32,8,256]{2,1,0:T(8,128)S(1)}, f32[3,34,8,256]{3,2,1,0:T(8,128...) custom-call(s32[7]{0:T(128)S(1)} %stack.47.meta_ref.r_0_, ...), custom_call_target="tpu_custom_call" | custom-call | tf_op jit(solution)/shard_map/first/pallas_call | solution.py:48
  2.9 1.5 %collective-permute-start.2 = (f32[96,256]{1,0:T(8,128)S(1)}, f32[96,256]{1,0:T(8,128)S(1)}, u32[]{:S(2)}, u32[]{:S(2)}) collective-permute-start(f32[96,256]{1,0:T(8,128)S(1)} %get-tuple-element.54), channel_id=1, source_target_pairs={{0,1},{1,0},{2,3},{3,2},{4,5},{5,4},{6,7},{7,6},{8,9},{9,8},{10,11... | collective-permute-start | bytes 294920 | tf_op jit(solution)/shard_map/ppermute | solution.py:227
  4.3 1.3 %collective-permute-start.3 = (f32[96,256]{1,0:T(8,128)S(1)}, f32[96,256]{1,0:T(8,128)S(1)}, u32[]{:S(2)}, u32[]{:S(2)}) collective-permute-start(f32[96,256]{1,0:T(8,128)S(1)} %get-tuple-element.55), channel_id=1, source_target_pairs={{1,2},{2,1},{3,4},{4,3},{5,6},{6,5},{7,0},{0,7},{9,10},{10,9},{11,... | collective-permute-start | bytes 294920 | tf_op jit(solution)/shard_map/ppermute | solution.py:225
  5.6 1.3 %collective-permute-start = (f32[8,128]{1,0:T(8,128)S(1)}, f32[8,128]{1,0:T(8,128)S(1)}, u32[]{:S(2)}, u32[]{:S(2)}) collective-permute-start(f32[8,128]{1,0:T(8,128)S(1)} %get-tuple-element.52), channel_id=1, source_target_pairs={{0,8},{8,0},{16,24},{24,16},{32,40},{40,32},{48,56},{56,48},{64,72... | collective-permute-start | bytes 12296 | tf_op jit(solution)/shard_map/ppermute | solution.py:226
  6.9 5.4 %collective-permute-start.1 = (f32[8,128]{1,0:T(8,128)S(1)}, f32[8,128]{1,0:T(8,128)S(1)}, u32[]{:S(2)}, u32[]{:S(2)}) collective-permute-start(f32[8,128]{1,0:T(8,128)S(1)} %get-tuple-element.53), channel_id=1, source_target_pairs={{8,16},{16,8},{24,32},{32,24},{40,48},{48,40},{56,64},{64,56},{72,... | collective-permute-start | bytes 12296 | tf_op jit(solution)/shard_map/ppermute | solution.py:224
  13.3 6.3 %forward1.1 = (f32[6,3,3,32,8,256]{5,4,3,2,1,0:T(8,128)S(1)}, f32[3,32,8,256]{3,2,1,0:T(8,128)S(1)}, f32[3,34,8,256]{3,2,1,0:T(8,128)S(1)}, f32[8,128]{1,0:T(8,1...) custom-call(s32[7]{0:T(128)S(1)} %stack.47.meta_ref.r_0_, ...), custom_call_target="tpu_custom_call" | custom-call | tf_op jit(solution)/shard_map/forward1/pallas_call | solution.py:48
  19.6 2.9 %collective-permute-start.6 = (f32[96,256]{1,0:T(8,128)S(1)}, f32[96,256]{1,0:T(8,128)S(1)}, u32[]{:S(2)}, u32[]{:S(2)}) collective-permute-start(f32[96,256]{1,0:T(8,128)S(1)} %get-tuple-element.61), channel_id=1, source_target_pairs={{0,1},{1,0},{2,3},{3,2},{4,5},{5,4},{6,7},{7,6},{8,9},{9,8},{10,11... | collective-permute-start | bytes 294920 | tf_op jit(solution)/shard_map/ppermute | solution.py:227
  22.6 5.1 %collective-permute-start.5 = (f32[8,128]{1,0:T(8,128)S(1)}, f32[8,128]{1,0:T(8,128)S(1)}, u32[]{:S(2)}, u32[]{:S(2)}) collective-permute-start(f32[8,128]{1,0:T(8,128)S(1)} %get-tuple-element.60), channel_id=1, source_target_pairs={{8,16},{16,8},{24,32},{32,24},{40,48},{48,40},{56,64},{64,56},{72,... | collective-permute-start | bytes 12296 | tf_op jit(solution)/shard_map/ppermute | solution.py:224
  27.6 1.0 collective-permute-done.5.r_7_
  28.6 3.1 %forward2.1 = (f32[3,32,8,256]{3,2,1,0:T(8,128)S(1)}, f32[3,34,8,256]{3,2,1,0:T(8,128)S(1)}, f32[8,128]{1,0:T(8,128)S(1)}, f32[8,128]{1,0:T(8,128)S(1)}, f32[96,256]{1,0:T(8,128)S(1)}, /*index=5*/f32[96,256]{1,0:T(8,128)S(1)}) custom-call(s32[7]{0:T(128)S(1)} %stack.47.meta_ref.r_0_, f32[6,3,3,32,8,256]{5,4,3,2,1,0:T(8,128)S(1)} %get-tuple-element.56.r_1_, ...), custom_call_target="tpu_custom_call" | custom-call | tf_op jit(solution)/shard_map/forward2/pallas_call | solution.py:48
  31.8 1.9 %collective-permute-start.10 = (f32[96,256]{1,0:T(8,128)S(1)}, f32[96,256]{1,0:T(8,128)S(1)}, u32[]{:S(2)}, u32[]{:S(2)}) collective-permute-start(f32[96,256]{1,0:T(8,128)S(1)} %get-tuple-element.67), channel_id=1, source_target_pairs={{0,1},{1,0},{2,3},{3,2},{4,5},{5,4},{6,7},{7,6},{8,9},{9,8},{10,11... | collective-permute-start | bytes 294920 | tf_op jit(solution)/shard_map/ppermute | solution.py:227
  34.5 5.1 %collective-permute-start.9 = (f32[8,128]{1,0:T(8,128)S(1)}, f32[8,128]{1,0:T(8,128)S(1)}, u32[]{:S(2)}, u32[]{:S(2)}) collective-permute-start(f32[8,128]{1,0:T(8,128)S(1)} %get-tuple-element.66), channel_id=1, source_target_pairs={{8,16},{16,8},{24,32},{32,24},{40,48},{48,40},{56,64},{64,56},{72,... | collective-permute-start | bytes 12296 | tf_op jit(solution)/shard_map/ppermute | solution.py:224
  40.6 3.1 %forward3.1 = (f32[3,32,8,256]{3,2,1,0:T(8,128)S(1)}, f32[3,34,8,256]{3,2,1,0:T(8,128)S(1)}, f32[8,128]{1,0:T(8,128)S(1)}, f32[8,128]{1,0:T(8,128)S(1)}, f32[96,256]{1,0:T(8,128)S(1)}, /*index=5*/f32[96,256]{1,0:T(8,128)S(1)}) custom-call(s32[7]{0:T(128)S(1)} %stack.47.meta_ref.r_0_, f32[6,3,3,32,8,256]{5,4,3,2,1,0:T(8,128)S(1)} %get-tuple-element.56.r_1_, ...), custom_call_target="tpu_custom_call" | custom-call | tf_op jit(solution)/shard_map/forward3/pallas_call | solution.py:48
  43.7 1.4 %collective-permute-start.14 = (f32[96,256]{1,0:T(8,128)S(1)}, f32[96,256]{1,0:T(8,128)S(1)}, u32[]{:S(2)}, u32[]{:S(2)}) collective-permute-start(f32[96,256]{1,0:T(8,128)S(1)} %get-tuple-element.73), channel_id=1, source_target_pairs={{0,1},{1,0},{2,3},{3,2},{4,5},{5,4},{6,7},{7,6},{8,9},{9,8},{10,11... | collective-permute-start | bytes 294920 | tf_op jit(solution)/shard_map/ppermute | solution.py:227
  45.6 5.1 %collective-permute-start.13 = (f32[8,128]{1,0:T(8,128)S(1)}, f32[8,128]{1,0:T(8,128)S(1)}, u32[]{:S(2)}, u32[]{:S(2)}) collective-permute-start(f32[8,128]{1,0:T(8,128)S(1)} %get-tuple-element.72), channel_id=1, source_target_pairs={{8,16},{16,8},{24,32},{32,24},{40,48},{48,40},{56,64},{64,56},{72,... | collective-permute-start | bytes 12296 | tf_op jit(solution)/shard_map/ppermute | solution.py:224
  51.7 3.1 %backward2.1 = (f32[3,34,8,256]{3,2,1,0:T(8,128)S(1)}, f32[8,128]{1,0:T(8,128)S(1)}, f32[8,128]{1,0:T(8,128)S(1)}, f32[96,256]{1,0:T(8,128)S(1)}, f32[96,256]{1,0:T(8,128)S(1)}) custom-call(s32[7]{0:T(128)S(1)} %stack.47.meta_ref.r_0_, f32[6,3,3,32,8,256]{5,4,3,2,1,0:T(8,128)S(1)} %get-tuple-element.56.r_1_, ...), custom_call_target="tpu_custom_call" | custom-call | tf_op jit(solution)/shard_map/backward2/pallas_call | solution.py:48
  54.8 1.4 %collective-permute-start.18 = (f32[96,256]{1,0:T(8,128)S(1)}, f32[96,256]{1,0:T(8,128)S(1)}, u32[]{:S(2)}, u32[]{:S(2)}) collective-permute-start(f32[96,256]{1,0:T(8,128)S(1)} %get-tuple-element.78), channel_id=1, source_target_pairs={{0,1},{1,0},{2,3},{3,2},{4,5},{5,4},{6,7},{7,6},{8,9},{9,8},{10,11... | collective-permute-start | bytes 294920 | tf_op jit(solution)/shard_map/ppermute | solution.py:227
  57.1 4.8 %collective-permute-start.17 = (f32[8,128]{1,0:T(8,128)S(1)}, f32[8,128]{1,0:T(8,128)S(1)}, u32[]{:S(2)}, u32[]{:S(2)}) collective-permute-start(f32[8,128]{1,0:T(8,128)S(1)} %get-tuple-element.77), channel_id=1, source_target_pairs={{8,16},{16,8},{24,32},{32,24},{40,48},{48,40},{56,64},{64,56},{72,... | collective-permute-start | bytes 12296 | tf_op jit(solution)/shard_map/ppermute | solution.py:224
  61.8 1.0 collective-permute-done.17.r_7_
  62.9 3.1 %backward1.1 = (f32[3,34,8,256]{3,2,1,0:T(8,128)S(1)}, f32[8,128]{1,0:T(8,128)S(1)}, f32[8,128]{1,0:T(8,128)S(1)}, f32[96,256]{1,0:T(8,128)S(1)}, f32[96,256]{1,0:T(8,128)S(1)}) custom-call(s32[7]{0:T(128)S(1)} %stack.47.meta_ref.r_0_, f32[6,3,3,32,8,256]{5,4,3,2,1,0:T(8,128)S(1)} %get-tuple-element.56.r_1_, ...), custom_call_target="tpu_custom_call" | custom-call | tf_op jit(solution)/shard_map/backward1/pallas_call | solution.py:48
  66.0 2.2 %collective-permute-start.22 = (f32[96,256]{1,0:T(8,128)S(1)}, f32[96,256]{1,0:T(8,128)S(1)}, u32[]{:S(2)}, u32[]{:S(2)}) collective-permute-start(f32[96,256]{1,0:T(8,128)S(1)} %get-tuple-element.83), channel_id=1, source_target_pairs={{0,1},{1,0},{2,3},{3,2},{4,5},{5,4},{6,7},{7,6},{8,9},{9,8},{10,11... | collective-permute-start | bytes 294920 | tf_op jit(solution)/shard_map/ppermute | solution.py:227
  68.2 5.1 %collective-permute-start.21 = (f32[8,128]{1,0:T(8,128)S(1)}, f32[8,128]{1,0:T(8,128)S(1)}, u32[]{:S(2)}, u32[]{:S(2)}) collective-permute-start(f32[8,128]{1,0:T(8,128)S(1)} %get-tuple-element.82), channel_id=1, source_target_pairs={{8,16},{16,8},{24,32},{32,24},{40,48},{48,40},{56,64},{64,56},{72,... | collective-permute-start | bytes 12296 | tf_op jit(solution)/shard_map/ppermute | solution.py:224
  73.3 2.0 %prep.1 = (bf16[1024,1024]{1,0:T(8,128)(2,1)S(1)}, bf16[256,1024]{1,0:T(8,128)(2,1)S(1)}, f32[16,128]{1,0:T(8,128)S(1)}, s32[1,1024]{1,0:T(1,128)S(1)}) custom-call(s32[7]{0:T(128)S(1)} %stack.47.meta_ref.r_0_, s32[64,128]{1,0:T(8,128)S(1)} %bitcast.22, s32[64,128]{1,0:T(8,128)S(1)} %bitcast.23, s32[1,1024]{1,0:T(1,128)S(1)} %bitcast.19, ...), custom_call_target="tpu_custom_call" | custom-call | tf_op jit(solution)/shard_map/prep/pallas_call | solution.py:48
  75.4 2.5 %backward0.1.s_ref = f32[3,32,8,256]{3,2,1,0:T(8,128)S(1)} custom-call(s32[7]{0:T(128)S(1)} %stack.47.meta_ref.r_0_, f32[6,3,3,32,8,256]{5,4,3,2,1,0:T(8,128)S(1)} %get-tuple-element.56.r_1_, f32[3,3,32,8,256]{4,3,2,1,0:T(8,128)S(1)} %get-tuple-element.48.r_2_, s32[32,8,256]{2,1,0:T(8,128)S(1)} %get-tuple-element.49.r_3_, ...), custom_call_target="tpu_custom_call" | custom-call | tf_op jit(solution)/shard_map/backward0/pallas_call | solution.py:48
  77.9 2.8 %terms.1 = (f32[512,128]{1,0:T(8,128)S(1)}, f32[512,128]{1,0:T(8,128)S(1)}) custom-call(f32[3,32,8,256]{3,2,1,0:T(8,128)S(1)} %backward0.1.s_ref, bf16[256,1024]{1,0:T(8,128)(2,1)S(1)} %get-tuple-element.85.rt_ref, bf16[1024,1024]{1,0:T(8,128)(2,1)S(1)} %get-tuple-element.86.kh_ref, s32[1,1024]{1,0:T(1,128)S(1)} %get-tuple-element.87.lo_ref, ...), custom_call_target="tpu_custom_call" | custom-call | tf_op jit(solution)/shard_map/terms/pallas_call | solution.py:48
  80.7 1.3 %collective-permute-start.24 = (f32[512,128]{1,0:T(8,128)S(1)}, f32[512,128]{1,0:T(8,128)S(1)}, u32[]{:S(2)}, u32[]{:S(2)}) collective-permute-start(f32[512,128]{1,0:T(8,128)S(1)} %get-tuple-element.89), channel_id=1, source_target_pairs={{0,1},{1,0},{2,3},{3,2},{4,5},{5,4},{6,7},{7,6},{8,9},{9,8},{10,11... | collective-permute-start | bytes 786440 | tf_op jit(solution)/shard_map/ppermute | solution.py:389
  82.0 1.2 collective-permute-done.24
  83.2 17.3 %all_to_all.10.got_ref = f32[64,8,128]{2,1,0:T(8,128)S(1)} all-to-all(f32[64,8,128]{2,1,0:T(8,128)S(1)} %add_bitcast_fusion), channel_id=1, replica_groups={{0,2,4,6,8,10,12,14,16,18,20,22,24,26,28,30,32,34,36,38,40,42,44,46,48,..., dimensions={0} | all-to-all | bytes 524288 | tf_op jit(solution)/shard_map/all_to_all | solution.py:390
  100.7 13.8 %all_to_all.11 = f32[64,8,128]{2,1,0:T(8,128)S(1)} all-to-all(f32[64,8,128]{2,1,0:T(8,128)S(1)} %solve.1), channel_id=1, replica_groups={{0,2,4,6,8,10,12,14,16,18,20,22,24,26,28,30,32,34,36,38,40,42,44,46,48,..., dimensions={0} | all-to-all | bytes 524288 | tf_op jit(solution)/shard_map/all_to_all | solution.py:394
  114.5 3.0 %collective-permute-start.25 = (f32[512,128]{1,0:T(8,128)S(1)}, f32[512,128]{1,0:T(8,128)S(1)}, u32[]{:S(2)}, u32[]{:S(2)}) collective-permute-start(f32[512,128]{1,0:T(8,128)S(1)} %bitcast.16), channel_id=1, source_target_pairs={{0,1},{1,0},{2,3},{3,2},{4,5},{5,4},{6,7},{7,6},{8,9},{9,8},{10,11... | collective-permute-start | bytes 786440 | tf_op jit(solution)/shard_map/ppermute | solution.py:395
  117.6 1.2 collective-permute-done.25.other_ref
  118.7 3.4 %back.1 = f32[3,32,8,256]{3,2,1,0:T(8,128)} custom-call(f32[512,128]{1,0:T(8,128)S(1)} %bitcast.17, f32[512,128]{1,0:T(8,128)S(1)} %collective-permute-done.25.other_ref, f32[3,32,8,256]{3,2,1,0:T(8,128)S(1)} %backward0.1.s_ref, bf16[256,1024]{1,0:T(8,128)(2,1)S(1)} %get-tuple-element.85.rt_ref, bf16[1024,1024]{1,0:T(8,128)(2,1)S(1)} %get-tuple-element.86.kh_ref, ...), custom_call_target="tpu_custom_call" | custom-call | tf_op jit(solution)/shard_map/back/pallas_call | solution.py:396
  (51 shorter events, 5.7 us)
Async XLA Ops:
  2.9 10.4 %collective-permute-start.2 = (f32[96,256]{1,0:T(8,128)S(1)}, f32[96,256]{1,0:T(8,128)S(1)}, u32[]{:S(2)}, u32[]{:S(2)}) collective-permute-start(f32[96,256]{1,0:T(8,128)S(1)} %get-tuple-element.54), channel_id=1, source_target_pairs={{0,1},{1,0},{2,3},{3,2},{4,5},{5,4},{6,7},{7,6},{8,9},{9,8},{10,11... | collective-permute-start | bytes 294920 | tf_op jit(solution)/shard_map/ppermute | solution.py:227
  4.3 9.0 %collective-permute-start.3 = (f32[96,256]{1,0:T(8,128)S(1)}, f32[96,256]{1,0:T(8,128)S(1)}, u32[]{:S(2)}, u32[]{:S(2)}) collective-permute-start(f32[96,256]{1,0:T(8,128)S(1)} %get-tuple-element.55), channel_id=1, source_target_pairs={{1,2},{2,1},{3,4},{4,3},{5,6},{6,5},{7,0},{0,7},{9,10},{10,9},{11,... | collective-permute-start | bytes 294920 | tf_op jit(solution)/shard_map/ppermute | solution.py:225
  5.6 6.7 %collective-permute-start = (f32[8,128]{1,0:T(8,128)S(1)}, f32[8,128]{1,0:T(8,128)S(1)}, u32[]{:S(2)}, u32[]{:S(2)}) collective-permute-start(f32[8,128]{1,0:T(8,128)S(1)} %get-tuple-element.52), channel_id=1, source_target_pairs={{0,8},{8,0},{16,24},{24,16},{32,40},{40,32},{48,56},{56,48},{64,72... | collective-permute-start | bytes 12296 | tf_op jit(solution)/shard_map/ppermute | solution.py:226
  6.9 6.4 %collective-permute-start.1 = (f32[8,128]{1,0:T(8,128)S(1)}, f32[8,128]{1,0:T(8,128)S(1)}, u32[]{:S(2)}, u32[]{:S(2)}) collective-permute-start(f32[8,128]{1,0:T(8,128)S(1)} %get-tuple-element.53), channel_id=1, source_target_pairs={{8,16},{16,8},{24,32},{32,24},{40,48},{48,40},{56,64},{64,56},{72,... | collective-permute-start | bytes 12296 | tf_op jit(solution)/shard_map/ppermute | solution.py:224
  19.6 9.0 %collective-permute-start.6 = (f32[96,256]{1,0:T(8,128)S(1)}, f32[96,256]{1,0:T(8,128)S(1)}, u32[]{:S(2)}, u32[]{:S(2)}) collective-permute-start(f32[96,256]{1,0:T(8,128)S(1)} %get-tuple-element.61), channel_id=1, source_target_pairs={{0,1},{1,0},{2,3},{3,2},{4,5},{5,4},{6,7},{7,6},{8,9},{9,8},{10,11... | collective-permute-start | bytes 294920 | tf_op jit(solution)/shard_map/ppermute | solution.py:227
  22.6 6.1 %collective-permute-start.7 = (f32[96,256]{1,0:T(8,128)S(1)}, f32[96,256]{1,0:T(8,128)S(1)}, u32[]{:S(2)}, u32[]{:S(2)}) collective-permute-start(f32[96,256]{1,0:T(8,128)S(1)} %get-tuple-element.62), channel_id=1, source_target_pairs={{1,2},{2,1},{3,4},{4,3},{5,6},{6,5},{7,0},{0,7},{9,10},{10,9},{11,... | collective-permute-start | bytes 294920 | tf_op jit(solution)/shard_map/ppermute | solution.py:225
  22.6 5.1 %collective-permute-start.4 = (f32[8,128]{1,0:T(8,128)S(1)}, f32[8,128]{1,0:T(8,128)S(1)}, u32[]{:S(2)}, u32[]{:S(2)}) collective-permute-start(f32[8,128]{1,0:T(8,128)S(1)} %get-tuple-element.59), channel_id=1, source_target_pairs={{0,8},{8,0},{16,24},{24,16},{32,40},{40,32},{48,56},{56,48},{64,72... | collective-permute-start | bytes 12296 | tf_op jit(solution)/shard_map/ppermute | solution.py:226
  22.6 6.1 %collective-permute-start.5 = (f32[8,128]{1,0:T(8,128)S(1)}, f32[8,128]{1,0:T(8,128)S(1)}, u32[]{:S(2)}, u32[]{:S(2)}) collective-permute-start(f32[8,128]{1,0:T(8,128)S(1)} %get-tuple-element.60), channel_id=1, source_target_pairs={{8,16},{16,8},{24,32},{32,24},{40,48},{48,40},{56,64},{64,56},{72,... | collective-permute-start | bytes 12296 | tf_op jit(solution)/shard_map/ppermute | solution.py:224
  31.8 8.8 %collective-permute-start.10 = (f32[96,256]{1,0:T(8,128)S(1)}, f32[96,256]{1,0:T(8,128)S(1)}, u32[]{:S(2)}, u32[]{:S(2)}) collective-permute-start(f32[96,256]{1,0:T(8,128)S(1)} %get-tuple-element.67), channel_id=1, source_target_pairs={{0,1},{1,0},{2,3},{3,2},{4,5},{5,4},{6,7},{7,6},{8,9},{9,8},{10,11... | collective-permute-start | bytes 294920 | tf_op jit(solution)/shard_map/ppermute | solution.py:227
  33.6 7.0 %collective-permute-start.11 = (f32[96,256]{1,0:T(8,128)S(1)}, f32[96,256]{1,0:T(8,128)S(1)}, u32[]{:S(2)}, u32[]{:S(2)}) collective-permute-start(f32[96,256]{1,0:T(8,128)S(1)} %get-tuple-element.68), channel_id=1, source_target_pairs={{1,2},{2,1},{3,4},{4,3},{5,6},{6,5},{7,0},{0,7},{9,10},{10,9},{11,... | collective-permute-start | bytes 294920 | tf_op jit(solution)/shard_map/ppermute | solution.py:225
  34.5 5.1 %collective-permute-start.8 = (f32[8,128]{1,0:T(8,128)S(1)}, f32[8,128]{1,0:T(8,128)S(1)}, u32[]{:S(2)}, u32[]{:S(2)}) collective-permute-start(f32[8,128]{1,0:T(8,128)S(1)} %get-tuple-element.65), channel_id=1, source_target_pairs={{0,8},{8,0},{16,24},{24,16},{32,40},{40,32},{48,56},{56,48},{64,72... | collective-permute-start | bytes 12296 | tf_op jit(solution)/shard_map/ppermute | solution.py:226
  34.5 6.1 %collective-permute-start.9 = (f32[8,128]{1,0:T(8,128)S(1)}, f32[8,128]{1,0:T(8,128)S(1)}, u32[]{:S(2)}, u32[]{:S(2)}) collective-permute-start(f32[8,128]{1,0:T(8,128)S(1)} %get-tuple-element.66), channel_id=1, source_target_pairs={{8,16},{16,8},{24,32},{32,24},{40,48},{48,40},{56,64},{64,56},{72,... | collective-permute-start | bytes 12296 | tf_op jit(solution)/shard_map/ppermute | solution.py:224
  43.7 7.9 %collective-permute-start.14 = (f32[96,256]{1,0:T(8,128)S(1)}, f32[96,256]{1,0:T(8,128)S(1)}, u32[]{:S(2)}, u32[]{:S(2)}) collective-permute-start(f32[96,256]{1,0:T(8,128)S(1)} %get-tuple-element.73), channel_id=1, source_target_pairs={{0,1},{1,0},{2,3},{3,2},{4,5},{5,4},{6,7},{7,6},{8,9},{9,8},{10,11... | collective-permute-start | bytes 294920 | tf_op jit(solution)/shard_map/ppermute | solution.py:227
  45.1 6.6 %collective-permute-start.15 = (f32[96,256]{1,0:T(8,128)S(1)}, f32[96,256]{1,0:T(8,128)S(1)}, u32[]{:S(2)}, u32[]{:S(2)}) collective-permute-start(f32[96,256]{1,0:T(8,128)S(1)} %get-tuple-element.74), channel_id=1, source_target_pairs={{1,2},{2,1},{3,4},{4,3},{5,6},{6,5},{7,0},{0,7},{9,10},{10,9},{11,... | collective-permute-start | bytes 294920 | tf_op jit(solution)/shard_map/ppermute | solution.py:225
  45.6 5.1 %collective-permute-start.12 = (f32[8,128]{1,0:T(8,128)S(1)}, f32[8,128]{1,0:T(8,128)S(1)}, u32[]{:S(2)}, u32[]{:S(2)}) collective-permute-start(f32[8,128]{1,0:T(8,128)S(1)} %get-tuple-element.71), channel_id=1, source_target_pairs={{0,8},{8,0},{16,24},{24,16},{32,40},{40,32},{48,56},{56,48},{64,72... | collective-permute-start | bytes 12296 | tf_op jit(solution)/shard_map/ppermute | solution.py:226
  45.6 6.1 %collective-permute-start.13 = (f32[8,128]{1,0:T(8,128)S(1)}, f32[8,128]{1,0:T(8,128)S(1)}, u32[]{:S(2)}, u32[]{:S(2)}) collective-permute-start(f32[8,128]{1,0:T(8,128)S(1)} %get-tuple-element.72), channel_id=1, source_target_pairs={{8,16},{16,8},{24,32},{32,24},{40,48},{48,40},{56,64},{64,56},{72,... | collective-permute-start | bytes 12296 | tf_op jit(solution)/shard_map/ppermute | solution.py:224
  54.8 8.1 %collective-permute-start.18 = (f32[96,256]{1,0:T(8,128)S(1)}, f32[96,256]{1,0:T(8,128)S(1)}, u32[]{:S(2)}, u32[]{:S(2)}) collective-permute-start(f32[96,256]{1,0:T(8,128)S(1)} %get-tuple-element.78), channel_id=1, source_target_pairs={{0,1},{1,0},{2,3},{3,2},{4,5},{5,4},{6,7},{7,6},{8,9},{9,8},{10,11... | collective-permute-start | bytes 294920 | tf_op jit(solution)/shard_map/ppermute | solution.py:227
  56.2 6.7 %collective-permute-start.19 = (f32[96,256]{1,0:T(8,128)S(1)}, f32[96,256]{1,0:T(8,128)S(1)}, u32[]{:S(2)}, u32[]{:S(2)}) collective-permute-start(f32[96,256]{1,0:T(8,128)S(1)} %get-tuple-element.79), channel_id=1, source_target_pairs={{1,2},{2,1},{3,4},{4,3},{5,6},{6,5},{7,0},{0,7},{9,10},{10,9},{11,... | collective-permute-start | bytes 294920 | tf_op jit(solution)/shard_map/ppermute | solution.py:225
  57.1 4.8 %collective-permute-start.16 = (f32[8,128]{1,0:T(8,128)S(1)}, f32[8,128]{1,0:T(8,128)S(1)}, u32[]{:S(2)}, u32[]{:S(2)}) collective-permute-start(f32[8,128]{1,0:T(8,128)S(1)} %get-tuple-element.76), channel_id=1, source_target_pairs={{0,8},{8,0},{16,24},{24,16},{32,40},{40,32},{48,56},{56,48},{64,72... | collective-permute-start | bytes 12296 | tf_op jit(solution)/shard_map/ppermute | solution.py:226
  57.1 5.8 %collective-permute-start.17 = (f32[8,128]{1,0:T(8,128)S(1)}, f32[8,128]{1,0:T(8,128)S(1)}, u32[]{:S(2)}, u32[]{:S(2)}) collective-permute-start(f32[8,128]{1,0:T(8,128)S(1)} %get-tuple-element.77), channel_id=1, source_target_pairs={{8,16},{16,8},{24,32},{32,24},{40,48},{48,40},{56,64},{64,56},{72,... | collective-permute-start | bytes 12296 | tf_op jit(solution)/shard_map/ppermute | solution.py:224
  62.8 10.4 %copy-start.1 = (s32[1024]{0:T(1024)S(1)}, s32[1024]{0:T(1024)}, u32[]{:S(2)}) copy-start(s32[1024]{0:T(1024)} %param.16) | copy-start | bytes 12292
  62.8 10.4 %copy-start.2 = (s32[8192]{0:T(1024)S(1)}, s32[8192]{0:T(1024)}, u32[]{:S(2)}) copy-start(s32[8192]{0:T(1024)} %param.21) | copy-start | bytes 98308
  62.9 10.4 %copy-start.3 = (s32[8192]{0:T(1024)S(1)}, s32[8192]{0:T(1024)}, u32[]{:S(2)}) copy-start(s32[8192]{0:T(1024)} %param.22) | copy-start | bytes 98308
  62.9 10.4 %copy-start.6 = (s32[1024]{0:T(1024)S(1)}, s32[1024]{0:T(1024)}, u32[]{:S(2)}) copy-start(s32[1024]{0:T(1024)} %param.17) | copy-start | bytes 12292
  66.0 9.4 %collective-permute-start.22 = (f32[96,256]{1,0:T(8,128)S(1)}, f32[96,256]{1,0:T(8,128)S(1)}, u32[]{:S(2)}, u32[]{:S(2)}) collective-permute-start(f32[96,256]{1,0:T(8,128)S(1)} %get-tuple-element.83), channel_id=1, source_target_pairs={{0,1},{1,0},{2,3},{3,2},{4,5},{5,4},{6,7},{7,6},{8,9},{9,8},{10,11... | collective-permute-start | bytes 294920 | tf_op jit(solution)/shard_map/ppermute | solution.py:227
  68.2 7.1 %collective-permute-start.23 = (f32[96,256]{1,0:T(8,128)S(1)}, f32[96,256]{1,0:T(8,128)S(1)}, u32[]{:S(2)}, u32[]{:S(2)}) collective-permute-start(f32[96,256]{1,0:T(8,128)S(1)} %get-tuple-element.84), channel_id=1, source_target_pairs={{1,2},{2,1},{3,4},{4,3},{5,6},{6,5},{7,0},{0,7},{9,10},{10,9},{11,... | collective-permute-start | bytes 294920 | tf_op jit(solution)/shard_map/ppermute | solution.py:225
  68.2 7.1 %collective-permute-start.20 = (f32[8,128]{1,0:T(8,128)S(1)}, f32[8,128]{1,0:T(8,128)S(1)}, u32[]{:S(2)}, u32[]{:S(2)}) collective-permute-start(f32[8,128]{1,0:T(8,128)S(1)} %get-tuple-element.81), channel_id=1, source_target_pairs={{0,8},{8,0},{16,24},{24,16},{32,40},{40,32},{48,56},{56,48},{64,72... | collective-permute-start | bytes 12296 | tf_op jit(solution)/shard_map/ppermute | solution.py:226
  68.2 7.1 %collective-permute-start.21 = (f32[8,128]{1,0:T(8,128)S(1)}, f32[8,128]{1,0:T(8,128)S(1)}, u32[]{:S(2)}, u32[]{:S(2)}) collective-permute-start(f32[8,128]{1,0:T(8,128)S(1)} %get-tuple-element.82), channel_id=1, source_target_pairs={{8,16},{16,8},{24,32},{32,24},{40,48},{48,40},{56,64},{64,56},{72,... | collective-permute-start | bytes 12296 | tf_op jit(solution)/shard_map/ppermute | solution.py:224
  77.9 22.6 %copy-start = (f32[64,16,16]{0,2,1:T(8,128)S(1)}, f32[64,16,16]{0,2,1:T(8,128)}, u32[]{:S(2)}) copy-start(f32[64,16,16]{0,2,1:T(8,128)} %param.23) | copy-start | bytes 196612
  77.9 40.9 %copy-start.5 = (f32[3,1024]{1,0:T(4,128)S(1)}, f32[3,1024]{1,0:T(4,128)}, u32[]{:S(2)}) copy-start(f32[3,1024]{1,0:T(4,128)} %back_ref.1) | copy-start | bytes 36868
  80.7 2.5 %collective-permute-start.24 = (f32[512,128]{1,0:T(8,128)S(1)}, f32[512,128]{1,0:T(8,128)S(1)}, u32[]{:S(2)}, u32[]{:S(2)}) collective-permute-start(f32[512,128]{1,0:T(8,128)S(1)} %get-tuple-element.89), channel_id=1, source_target_pairs={{0,1},{1,0},{2,3},{3,2},{4,5},{5,4},{6,7},{7,6},{8,9},{9,8},{10,11... | collective-permute-start | bytes 786440 | tf_op jit(solution)/shard_map/ppermute | solution.py:389
  114.5 4.2 %collective-permute-start.25 = (f32[512,128]{1,0:T(8,128)S(1)}, f32[512,128]{1,0:T(8,128)S(1)}, u32[]{:S(2)}, u32[]{:S(2)}) collective-permute-start(f32[512,128]{1,0:T(8,128)S(1)} %bitcast.16), channel_id=1, source_target_pairs={{0,1},{1,0},{2,3},{3,2},{4,5},{5,4},{6,7},{7,6},{8,9},{9,8},{10,11... | collective-permute-start | bytes 786440 | tf_op jit(solution)/shard_map/ppermute | solution.py:395
  (2 other events, 12.9 us)

commit v3 on v2

--- a/solution.py
+++ b/solution.py
@@ -17,12 +17,9 @@
     return lax.broadcasted_iota(jnp.int32, shape, dim)
 
 
-def split3(x):
+def split(x):
     a = x.astype(BF16)
-    r = x - a.astype(F32)
-    b = r.astype(BF16)
-    c = (r - b.astype(F32)).astype(BF16)
-    return a, b, c
+    return a, (x - a.astype(F32)).astype(BF16)
 
 
 def dot(a, b, dims):
@@ -33,7 +30,7 @@
     return pltpu.with_memory_space_constraint(x, pltpu.VMEM)
 
 
-def call(body, outs, ins, smem=0, hbm=(), scratch=(), name=None, limit=None):
+def call(body, outs, ins, smem=0, hbm=(), scratch=(), name=None, limit=None, cost=None, alias=None):
     specs, args = [], []
     for k, x in enumerate(ins):
         if k < smem:
@@ -52,27 +49,33 @@
         out_specs=tuple(VMEM_SPEC for _ in outs),
         scratch_shapes=list(scratch),
         compiler_params=pltpu.CompilerParams(vmem_limit_bytes=limit or (8 << 20)),
+        cost_estimate=cost,
+        input_output_aliases=alias or {},
         name=name,
     )(*args)
 
 
-def emit_edges(new, z, nz, edges, y_odd, ya_ref, yb_ref):
+def emit_edges(new, z, nz, edges, ylo_ref, yhi_ref):
     xlo, xhi = edges
     lane = iota((8, 128), 1)
     for j in range(3):
         at = j * nz + z
         xlo = jnp.where(lane == at, pltpu.roll(new[j][:, :128], at, 1), xlo)
         xhi = jnp.where(lane == at, pltpu.roll(new[j][:, -128:], (at + 1) % 128, 1), xhi)
-        first, last = new[j][0:1, :], new[j][-1:, :]
-        ya_ref[pl.ds(at, 1), :] = jnp.where(y_odd, first, last)
-        yb_ref[pl.ds(at, 1), :] = jnp.where(y_odd, last, first)
+        ylo_ref[pl.ds(at, 1), :] = new[j][0:1, :]
+        yhi_ref[pl.ds(at, 1), :] = new[j][-1:, :]
     return xlo, xhi
 
 
-def store_columns(x_odd, edges, xa_ref, xb_ref):
-    xlo, xhi = edges
+def store_edges(meta_ref, columns, ylo_ref, yhi_ref, xa_ref, xb_ref, ya_ref, yb_ref):
+    x_odd = meta_ref[5] > 0
+    y_odd = meta_ref[6] > 0
+    xlo, xhi = columns
     xa_ref[...] = jnp.where(x_odd, xlo, xhi)
     xb_ref[...] = jnp.where(x_odd, xhi, xlo)
+    ylo, yhi = ylo_ref[...], yhi_ref[...]
+    ya_ref[...] = jnp.where(y_odd, ylo, yhi)
+    yb_ref[...] = jnp.where(y_odd, yhi, ylo)
 
 
 def zero_ends(ref, nz):
@@ -90,7 +93,7 @@
     return out
 
 
-def first_body(meta_ref, rhs_hbm, piv_hbm, col_hbm, rhs_ref, piv_ref, col_ref, v_ref, xa_ref, xb_ref, ya_ref, yb_ref, sems):
+def first_body(meta_ref, rhs_hbm, piv_hbm, col_hbm, rhs_ref, piv_ref, col_ref, v_ref, xa_ref, xb_ref, ya_ref, yb_ref, ylo_ref, yhi_ref, sems):
     nz = rhs_ref.shape[1]
     size = nz // PARTS
     pairs = [(rhs_hbm, rhs_ref), (piv_hbm, piv_ref), (col_hbm, col_ref)]
@@ -98,8 +101,6 @@
         for c in chunk_copies(pairs, sems, part, size, (1, 2, 0)):
             c.start()
     zero_ends(v_ref, nz)
-    x_odd = meta_ref[5] > 0
-    y_odd = meta_ref[6] > 0
 
     def step(z, edges):
         rhs = [rhs_ref[j, z] for j in range(3)]
@@ -110,7 +111,7 @@
             p = jnp.where(chosen, p, 0.0)
             v_ref[i, z + 1] = p
             new.append(p)
-        return emit_edges(new, z, nz, edges, y_odd, ya_ref, yb_ref)
+        return emit_edges(new, z, nz, edges, ylo_ref, yhi_ref)
 
     def block(part, edges):
         for c in chunk_copies(pairs, sems, part, size, (1, 2, 0)):
@@ -119,7 +120,7 @@
 
     zero = jnp.zeros((8, 128), F32)
     edges = lax.fori_loop(0, PARTS, block, (zero, zero))
-    store_columns(x_odd, edges, xa_ref, xb_ref)
+    store_edges(meta_ref, edges, ylo_ref, yhi_ref, xa_ref, xb_ref, ya_ref, yb_ref)
 
 
 def turn_body(colour, forward, final, load, *refs):
@@ -127,7 +128,10 @@
     refs = list(refs[10:])
     if load:
         sems = refs.pop()
+        prep_in, refs = refs[:5], refs[5:]
         coup_hbm, coup_ref = coup_ref, refs.pop(0)
+        prep_out, refs = refs[:4], refs[4:]
+    refs, (hylo_ref, hyhi_ref, ylo_ref, yhi_ref) = refs[:-4], refs[-4:]
     u_ref = refs.pop(0) if forward else None
     nv_ref, *edge_refs = refs
     nz = base_ref.shape[1]
@@ -138,6 +142,7 @@
         for part in range(PARTS):
             for c in chunk_copies(pairs, sems, part, size, (3,)):
                 c.start()
+        prep_body(meta_ref, *prep_in, *prep_out)
     lane = iota((ny, 128), 1)
     row = iota((ny, nx), 0)
     x_odd = meta_ref[5] > 0
@@ -146,6 +151,9 @@
     hxa, hxb = hxa_ref[...], hxb_ref[...]
     hxlo = jnp.where(has[0], jnp.where(x_odd, hxa, hxb), 0.0)
     hxhi = jnp.where(has[1], jnp.where(x_odd, hxb, hxa), 0.0)
+    hya, hyb = hya_ref[...], hyb_ref[...]
+    hylo_ref[...] = jnp.where(has[2], jnp.where(y_odd, hya, hyb), 0.0)
+    hyhi_ref[...] = jnp.where(has[3], jnp.where(y_odd, hyb, hya), 0.0)
     if not final:
         zero_ends(nv_ref, nz)
 
@@ -162,11 +170,8 @@
             xp = pltpu.roll(vc, nx - 1, 1)
             tail = jnp.where(lane == 127, pltpu.roll(hxhi, 127 - at, 1), xp[:, -128:])
             xp = jnp.concatenate([xp[:, :-128], tail], axis=1)
-            ha, hb = hya_ref[pl.ds(at, 1), :], hyb_ref[pl.ds(at, 1), :]
-            hylo = jnp.where(has[2], jnp.where(y_odd, ha, hb), 0.0)
-            hyhi = jnp.where(has[3], jnp.where(y_odd, hb, ha), 0.0)
-            ym = jnp.where(row == 0, hylo, pltpu.roll(vc, 1, 0))
-            yp = jnp.where(row == ny - 1, hyhi, pltpu.roll(vc, ny - 1, 0))
+            ym = jnp.where(row == 0, hylo_ref[pl.ds(at, 1), :], pltpu.roll(vc, 1, 0))
+            yp = jnp.where(row == ny - 1, hyhi_ref[pl.ds(at, 1), :], pltpu.roll(vc, ny - 1, 0))
             zm = v_ref[j, z]
             zp = v_ref[j, z + 2]
             for i in range(3):
@@ -193,7 +198,7 @@
             new.append(p)
         if final:
             return edges
-        return emit_edges(new, z, nz, edges, y_odd, edge_refs[2], edge_refs[3])
+        return emit_edges(new, z, nz, edges, ylo_ref, yhi_ref)
 
     def block(part, edges):
         for c in chunk_copies(pairs, sems, part, size, (3,)):
@@ -206,7 +211,7 @@
     else:
         edges = lax.fori_loop(0, nz, step, (zero, zero), unroll=UNROLL)
     if not final:
-        store_columns(x_odd, edges, edge_refs[0], edge_refs[1])
+        store_edges(meta_ref, edges, ylo_ref, yhi_ref, *edge_refs)
 
 
 def swaps(size, odd):
@@ -259,13 +264,13 @@
     term = jnp.zeros((1, n), F32)
     for i in range(3):
         f = s_ref[i].reshape(256, 256)
-        g = sum(dot(h, rt, ((0,), (0,))) for h in split3(f))
+        g = sum(dot(h, rt, ((0,), (0,))) for h in split(f))
         v = jnp.sum(jnp.where(at_col, g, 0.0), axis=0, keepdims=True)
         term = term + gather_ref[pl.ds(i, 1), :] * v
     at_low = iota((128, n), 0) == lo_ref[...]
-    stack = jnp.concatenate([jnp.where(at_low, h.astype(F32), 0.0).astype(BF16) for h in split3(term)], axis=0)
+    stack = jnp.concatenate([jnp.where(at_low, h.astype(F32), 0.0).astype(BF16) for h in split(term)], axis=0)
     sums = dot(kh_ref[...], stack, ((1,), (1,)))
-    sums = sums[:, :128] + sums[:, 128:256] + sums[:, 256:]
+    sums = sums[:, :128] + sums[:, 128:]
     mine_ref[...] = sums[:512]
     other_ref[...] = sums[512:]
 
@@ -282,15 +287,15 @@
 
 def return_body(mine_ref, other_ref, s_ref, rt_ref, kh_ref, lo_ref, cells_ref, back_ref, out_ref):
     n = cells_ref.shape[1]
-    g = sum(dot(h, kh_ref[0:512], ((0,), (0,))) for h in split3(mine_ref[...]))
-    g = g + sum(dot(h, kh_ref[512:1024], ((0,), (0,))) for h in split3(other_ref[...]))
+    g = sum(dot(h, kh_ref[0:512], ((0,), (0,))) for h in split(mine_ref[...]))
+    g = g + sum(dot(h, kh_ref[512:1024], ((0,), (0,))) for h in split(other_ref[...]))
     values = jnp.sum(jnp.where(iota((128, n), 0) == lo_ref[...], g, 0.0), axis=0, keepdims=True)
     at_col = iota((256, n), 0) == (cells_ref[...] & 255)
     rt = rt_ref[...]
     for i in range(3):
         w = back_ref[pl.ds(i, 1), :] * values
         change = sum(
-            dot(rt, jnp.where(at_col, h.astype(F32), 0.0).astype(BF16), ((1,), (1,))) for h in split3(w)
+            dot(rt, jnp.where(at_col, h.astype(F32), 0.0).astype(BF16), ((1,), (1,))) for h in split(w)
         )
         out_ref[i] = s_ref[i] - change.reshape(32, 8, 256)
 
@@ -331,6 +336,15 @@
     edges = [((ny, 128), F32)] * 2 + [((3 * nz, nx), F32)] * 2
     n = perf_cells.shape[0]
     cells = perf_cells.reshape(1, n)
+    rows = [pltpu.VMEM((3 * nz, nx), F32)] * 4
+    prep_ins = [
+        well_slot.reshape(-1, 128),
+        seg_count.reshape(-1, 128),
+        cells,
+        perf_wells.reshape(1, n),
+        perf_segments.reshape(1, n),
+    ]
+    prep_outs = [((1024, n), BF16), ((256, n), BF16), ((16, 128), F32), ((1, n), jnp.int32)]
 
     rhs, pivots, colours, v, *edge = call(
         first_body,
@@ -338,39 +352,28 @@
         [meta, rhs, pivots, colours],
         smem=1,
         hbm=(1, 2, 3),
-        scratch=[pltpu.SemaphoreType.DMA((3, PARTS))],
+        scratch=rows[:2] + [pltpu.SemaphoreType.DMA((3, PARTS))],
         name="first",
+        cost=pl.CostEstimate(flops=10**10, transcendentals=0, bytes_accessed=10**8),
     )
+    kh, rt, alive, low = call(prep_body, prep_outs, [meta] + prep_ins, smem=1, name="prep")
     base = rhs
     for colour in (1, 2, 3):
         halo = halos(edge)
-        load = colour == 1
+        load = False
         got = call(
             lambda *r, c=colour, l=load: turn_body(c, True, False, l, *r),
-            ([(couplings.shape, F32)] if load else []) + [plain, field] + edges,
-            [meta, couplings, pivots, colours, base, v, *halo],
+            ([(couplings.shape, F32)] + prep_outs if load else []) + [plain, field] + edges,
+            [meta, couplings, pivots, colours, base, v, *halo] + (prep_ins if load else []),
             smem=1,
             hbm=(1,) if load else (),
-            scratch=[pltpu.SemaphoreType.DMA((1, PARTS))] if load else [],
+            scratch=rows + ([pltpu.SemaphoreType.DMA((1, PARTS))] if load else []),
             name=f"forward{colour}",
+            limit=16 << 20,
         )
         if load:
-            couplings, *got = got
+            couplings, kh, rt, alive, low, *got = got
         base, v, *edge = got
-    kh, rt, alive, low = call(
-        prep_body,
-        [((1024, n), BF16), ((256, n), BF16), ((16, 128), F32), ((1, n), jnp.int32)],
-        [
-            meta,
-            well_slot.reshape(-1, 128),
-            seg_count.reshape(-1, 128),
-            cells,
-            perf_wells.reshape(1, n),
-            perf_segments.reshape(1, n),
-        ],
-        smem=1,
-        name="prep",
-    )
     for colour in (2, 1, 0):
         halo = halos(edge)
         final = colour == 0
@@ -379,6 +382,7 @@
             [plain] if final else [field] + edges,
             [meta, couplings, pivots, colours, base, v, *halo],
             smem=1,
+            scratch=rows,
             name=f"backward{colour}",
         )
     pairs = swaps(lax.axis_size("gy"), 0)

time: 122 us -> 118 us (0.967)
  Pallas kernels: 32.5 us -> 27.6 us
    pallas_call x10, Pallas kernels: 29.1 us -> 24.9 us  [call(): pl.pallas_call(body, out_shape=tuple((pltpu.VMEM(s, d) for s, d in outs))...]
where the time goes in v3:
time: 118 us; the launch traced here: 117 us
  starting transfers between devices  50.9 us (43%)
  blocking collectives  31.1 us (26%)
  Pallas kernels  27.6 us (23%)
  waiting for transfers between devices  7.33 us (6%)
    ppermute x6, starting transfers between devices, halos(): hxb = lax.ppermute(xb, 'gx', swaps(nx, 1))  30.4 us
    pallas_call x10, Pallas kernels, call(): pl.pallas_call(body, out_shape=tuple((pltpu.VMEM(s, d) for s, d in outs))...  24.9 us
    all_to_all x1, blocking collectives, shards(): lax.all_to_all(mine.reshape(64, 8, 128), axes, 0, 0, axis_index_groups=co...  17.3 us
    all_to_all x1, blocking collectives, shards(): lax.all_to_all(values, axes, 0, 0, axis_index_groups=cores, tiled=True)  13.7 us
    ppermute x6, starting transfers between devices, halos(): hya = lax.ppermute(ya, 'gy', swaps(ny, 0))  11.3 us
    ppermute x6, waiting for transfers between devices, halos(): hxb = lax.ppermute(xb, 'gx', swaps(nx, 1))  4.96 us
    ppermute x6, starting transfers between devices, halos(): hyb = lax.ppermute(yb, 'gy', swaps(ny, 1))  3.61 us
    ppermute x1, starting transfers between devices, shards(): other = lax.ppermute(mine, 'gy', pairs)  3.04 us
  transfers between devices with their start and end apart: 26, of which 7 were waited for; matrix products, arithmetic and copies ran while one was open for 0% of the time, Pallas kernels for 2%

profile of v3, /device:TPU:1, one launch (start us, length us, event | category | flops | bytes accessed | tf_op | source)
XLA Modules:
  0.0 117.4 jit_solution(14576172564721578149)
XLA Ops:
  0.1 3.1 %first.1 = (f32[3,32,8,256]{3,2,1,0:T(8,128)S(1)}, f32[3,3,32,8,256]{4,3,2,1,0:T(8,128)S(1)}, s32[32,8,256]{2,1,0:T(8,128)S(1)}, f32[3,34,8,256]{3,2,1,0:T(8,128...) custom-call(s32[7]{0:T(128)S(1)} %stack.47.meta_ref.r_0_, ...), custom_call_target="tpu_custom_call" | custom-call | flops 10000000000 | bytes 100000000 | tf_op jit(solution)/shard_map/first/pallas_call | solution.py:45
  3.2 1.5 %collective-permute-start.2 = (f32[96,256]{1,0:T(8,128)S(1)}, f32[96,256]{1,0:T(8,128)S(1)}, u32[]{:S(2)}, u32[]{:S(2)}) collective-permute-start(f32[96,256]{1,0:T(8,128)S(1)} %get-tuple-element.53), channel_id=1, source_target_pairs={{0,1},{1,0},{2,3},{3,2},{4,5},{5,4},{6,7},{7,6},{8,9},{9,8},{10,11... | collective-permute-start | bytes 294920 | tf_op jit(solution)/shard_map/ppermute | solution.py:232
  4.7 1.3 %collective-permute-start.3 = (f32[96,256]{1,0:T(8,128)S(1)}, f32[96,256]{1,0:T(8,128)S(1)}, u32[]{:S(2)}, u32[]{:S(2)}) collective-permute-start(f32[96,256]{1,0:T(8,128)S(1)} %get-tuple-element.54), channel_id=1, source_target_pairs={{1,2},{2,1},{3,4},{4,3},{5,6},{6,5},{7,0},{0,7},{9,10},{10,9},{11,... | collective-permute-start | bytes 294920 | tf_op jit(solution)/shard_map/ppermute | solution.py:230
  6.0 1.3 %collective-permute-start = (f32[8,128]{1,0:T(8,128)S(1)}, f32[8,128]{1,0:T(8,128)S(1)}, u32[]{:S(2)}, u32[]{:S(2)}) collective-permute-start(f32[8,128]{1,0:T(8,128)S(1)} %get-tuple-element.51), channel_id=1, source_target_pairs={{0,8},{8,0},{16,24},{24,16},{32,40},{40,32},{48,56},{56,48},{64,72... | collective-permute-start | bytes 12296 | tf_op jit(solution)/shard_map/ppermute | solution.py:231
  7.3 5.4 %collective-permute-start.1 = (f32[8,128]{1,0:T(8,128)S(1)}, f32[8,128]{1,0:T(8,128)S(1)}, u32[]{:S(2)}, u32[]{:S(2)}) collective-permute-start(f32[8,128]{1,0:T(8,128)S(1)} %get-tuple-element.52), channel_id=1, source_target_pairs={{8,16},{16,8},{24,32},{32,24},{40,48},{48,40},{56,64},{64,56},{72,... | collective-permute-start | bytes 12296 | tf_op jit(solution)/shard_map/ppermute | solution.py:229
  13.7 3.1 %forward1.1 = (f32[3,32,8,256]{3,2,1,0:T(8,128)S(1)}, f32[3,34,8,256]{3,2,1,0:T(8,128)S(1)}, f32[8,128]{1,0:T(8,128)S(1)}, f32[8,128]{1,0:T(8,128)S(1)}, f32[96,256]{1,0:T(8,128)S(1)}, /*index=5*/f32[96,256]{1,0:T(8,128)S(1)}) custom-call(s32[7]{0:T(128)S(1)} %stack.47.meta_ref.r_0_, f32[6,3,3,32,8,256]{5,4,3,2,1,0:T(8,128)S(1)} %bitcast.17, ...), custom_call_target="tpu_custom_call" | custom-call | tf_op jit(solution)/shard_map/forward1/pallas_call | solution.py:45
  16.8 2.9 %collective-permute-start.6 = (f32[96,256]{1,0:T(8,128)S(1)}, f32[96,256]{1,0:T(8,128)S(1)}, u32[]{:S(2)}, u32[]{:S(2)}) collective-permute-start(f32[96,256]{1,0:T(8,128)S(1)} %get-tuple-element.59), channel_id=1, source_target_pairs={{0,1},{1,0},{2,3},{3,2},{4,5},{5,4},{6,7},{7,6},{8,9},{9,8},{10,11... | collective-permute-start | bytes 294920 | tf_op jit(solution)/shard_map/ppermute | solution.py:232
  19.7 5.1 %collective-permute-start.5 = (f32[8,128]{1,0:T(8,128)S(1)}, f32[8,128]{1,0:T(8,128)S(1)}, u32[]{:S(2)}, u32[]{:S(2)}) collective-permute-start(f32[8,128]{1,0:T(8,128)S(1)} %get-tuple-element.58), channel_id=1, source_target_pairs={{8,16},{16,8},{24,32},{32,24},{40,48},{48,40},{56,64},{64,56},{72,... | collective-permute-start | bytes 12296 | tf_op jit(solution)/shard_map/ppermute | solution.py:229
  24.8 1.0 collective-permute-done.5.r_7_
  25.8 3.1 %forward2.1 = (f32[3,32,8,256]{3,2,1,0:T(8,128)S(1)}, f32[3,34,8,256]{3,2,1,0:T(8,128)S(1)}, f32[8,128]{1,0:T(8,128)S(1)}, f32[8,128]{1,0:T(8,128)S(1)}, f32[96,256]{1,0:T(8,128)S(1)}, /*index=5*/f32[96,256]{1,0:T(8,128)S(1)}) custom-call(s32[7]{0:T(128)S(1)} %stack.47.meta_ref.r_0_, f32[6,3,3,32,8,256]{5,4,3,2,1,0:T(8,128)S(1)} %bitcast.17, ...), custom_call_target="tpu_custom_call" | custom-call | tf_op jit(solution)/shard_map/forward2/pallas_call | solution.py:45
  28.8 1.9 %collective-permute-start.10 = (f32[96,256]{1,0:T(8,128)S(1)}, f32[96,256]{1,0:T(8,128)S(1)}, u32[]{:S(2)}, u32[]{:S(2)}) collective-permute-start(f32[96,256]{1,0:T(8,128)S(1)} %get-tuple-element.65), channel_id=1, source_target_pairs={{0,1},{1,0},{2,3},{3,2},{4,5},{5,4},{6,7},{7,6},{8,9},{9,8},{10,11... | collective-permute-start | bytes 294920 | tf_op jit(solution)/shard_map/ppermute | solution.py:232
  31.6 5.1 %collective-permute-start.9 = (f32[8,128]{1,0:T(8,128)S(1)}, f32[8,128]{1,0:T(8,128)S(1)}, u32[]{:S(2)}, u32[]{:S(2)}) collective-permute-start(f32[8,128]{1,0:T(8,128)S(1)} %get-tuple-element.64), channel_id=1, source_target_pairs={{8,16},{16,8},{24,32},{32,24},{40,48},{48,40},{56,64},{64,56},{72,... | collective-permute-start | bytes 12296 | tf_op jit(solution)/shard_map/ppermute | solution.py:229
  36.7 1.0 collective-permute-done.9.r_7_
  37.7 3.0 %forward3.1 = (f32[3,32,8,256]{3,2,1,0:T(8,128)S(1)}, f32[3,34,8,256]{3,2,1,0:T(8,128)S(1)}, f32[8,128]{1,0:T(8,128)S(1)}, f32[8,128]{1,0:T(8,128)S(1)}, f32[96,256]{1,0:T(8,128)S(1)}, /*index=5*/f32[96,256]{1,0:T(8,128)S(1)}) custom-call(s32[7]{0:T(128)S(1)} %stack.47.meta_ref.r_0_, f32[6,3,3,32,8,256]{5,4,3,2,1,0:T(8,128)S(1)} %bitcast.17, ...), custom_call_target="tpu_custom_call" | custom-call | tf_op jit(solution)/shard_map/forward3/pallas_call | solution.py:45
  40.7 1.4 %collective-permute-start.14 = (f32[96,256]{1,0:T(8,128)S(1)}, f32[96,256]{1,0:T(8,128)S(1)}, u32[]{:S(2)}, u32[]{:S(2)}) collective-permute-start(f32[96,256]{1,0:T(8,128)S(1)} %get-tuple-element.71), channel_id=1, source_target_pairs={{0,1},{1,0},{2,3},{3,2},{4,5},{5,4},{6,7},{7,6},{8,9},{9,8},{10,11... | collective-permute-start | bytes 294920 | tf_op jit(solution)/shard_map/ppermute | solution.py:232
  42.6 5.1 %collective-permute-start.13 = (f32[8,128]{1,0:T(8,128)S(1)}, f32[8,128]{1,0:T(8,128)S(1)}, u32[]{:S(2)}, u32[]{:S(2)}) collective-permute-start(f32[8,128]{1,0:T(8,128)S(1)} %get-tuple-element.70), channel_id=1, source_target_pairs={{8,16},{16,8},{24,32},{32,24},{40,48},{48,40},{56,64},{64,56},{72,... | collective-permute-start | bytes 12296 | tf_op jit(solution)/shard_map/ppermute | solution.py:229
  48.7 3.0 %backward2.1 = (f32[3,34,8,256]{3,2,1,0:T(8,128)S(1)}, f32[8,128]{1,0:T(8,128)S(1)}, f32[8,128]{1,0:T(8,128)S(1)}, f32[96,256]{1,0:T(8,128)S(1)}, f32[96,256]{1,0:T(8,128)S(1)}) custom-call(s32[7]{0:T(128)S(1)} %stack.47.meta_ref.r_0_, f32[6,3,3,32,8,256]{5,4,3,2,1,0:T(8,128)S(1)} %bitcast.17, f32[3,3,32,8,256]{4,3,2,1,0:T(8,128)S(1)} %get-tuple-element.47.r_2_, ...), custom_call_target="tpu_custom_call" | custom-call | tf_op jit(solution)/shard_map/backward2/pallas_call | solution.py:45
  51.7 1.4 %collective-permute-start.18 = (f32[96,256]{1,0:T(8,128)S(1)}, f32[96,256]{1,0:T(8,128)S(1)}, u32[]{:S(2)}, u32[]{:S(2)}) collective-permute-start(f32[96,256]{1,0:T(8,128)S(1)} %get-tuple-element.76), channel_id=1, source_target_pairs={{0,1},{1,0},{2,3},{3,2},{4,5},{5,4},{6,7},{7,6},{8,9},{9,8},{10,11... | collective-permute-start | bytes 294920 | tf_op jit(solution)/shard_map/ppermute | solution.py:232
  54.0 4.8 %collective-permute-start.17 = (f32[8,128]{1,0:T(8,128)S(1)}, f32[8,128]{1,0:T(8,128)S(1)}, u32[]{:S(2)}, u32[]{:S(2)}) collective-permute-start(f32[8,128]{1,0:T(8,128)S(1)} %get-tuple-element.75), channel_id=1, source_target_pairs={{8,16},{16,8},{24,32},{32,24},{40,48},{48,40},{56,64},{64,56},{72,... | collective-permute-start | bytes 12296 | tf_op jit(solution)/shard_map/ppermute | solution.py:229
  59.8 3.1 %backward1.1 = (f32[3,34,8,256]{3,2,1,0:T(8,128)S(1)}, f32[8,128]{1,0:T(8,128)S(1)}, f32[8,128]{1,0:T(8,128)S(1)}, f32[96,256]{1,0:T(8,128)S(1)}, f32[96,256]{1,0:T(8,128)S(1)}) custom-call(s32[7]{0:T(128)S(1)} %stack.47.meta_ref.r_0_, f32[6,3,3,32,8,256]{5,4,3,2,1,0:T(8,128)S(1)} %bitcast.17, f32[3,3,32,8,256]{4,3,2,1,0:T(8,128)S(1)} %get-tuple-element.47.r_2_, ...), custom_call_target="tpu_custom_call" | custom-call | tf_op jit(solution)/shard_map/backward1/pallas_call | solution.py:45
  62.9 2.2 %collective-permute-start.22 = (f32[96,256]{1,0:T(8,128)S(1)}, f32[96,256]{1,0:T(8,128)S(1)}, u32[]{:S(2)}, u32[]{:S(2)}) collective-permute-start(f32[96,256]{1,0:T(8,128)S(1)} %get-tuple-element.81), channel_id=1, source_target_pairs={{0,1},{1,0},{2,3},{3,2},{4,5},{5,4},{6,7},{7,6},{8,9},{9,8},{10,11... | collective-permute-start | bytes 294920 | tf_op jit(solution)/shard_map/ppermute | solution.py:232
  65.2 5.1 %collective-permute-start.21 = (f32[8,128]{1,0:T(8,128)S(1)}, f32[8,128]{1,0:T(8,128)S(1)}, u32[]{:S(2)}, u32[]{:S(2)}) collective-permute-start(f32[8,128]{1,0:T(8,128)S(1)} %get-tuple-element.80), channel_id=1, source_target_pairs={{8,16},{16,8},{24,32},{32,24},{40,48},{48,40},{56,64},{64,56},{72,... | collective-permute-start | bytes 12296 | tf_op jit(solution)/shard_map/ppermute | solution.py:229
  70.3 2.0 %prep.1 = (bf16[1024,1024]{1,0:T(8,128)(2,1)S(1)}, bf16[256,1024]{1,0:T(8,128)(2,1)S(1)}, f32[16,128]{1,0:T(8,128)S(1)}, s32[1,1024]{1,0:T(1,128)S(1)}) custom-call(s32[7]{0:T(128)S(1)} %stack.47.meta_ref.r_0_, s32[64,128]{1,0:T(8,128)S(1)} %bitcast.24, s32[64,128]{1,0:T(8,128)S(1)} %bitcast.25, s32[1,1024]{1,0:T(1,128)S(1)} %bitcast.21, ...), custom_call_target="tpu_custom_call" | custom-call | tf_op jit(solution)/shard_map/prep/pallas_call | solution.py:45
  72.3 2.4 %backward0.1.s_ref = f32[3,32,8,256]{3,2,1,0:T(8,128)S(1)} custom-call(s32[7]{0:T(128)S(1)} %stack.47.meta_ref.r_0_, f32[6,3,3,32,8,256]{5,4,3,2,1,0:T(8,128)S(1)} %bitcast.17, f32[3,3,32,8,256]{4,3,2,1,0:T(8,128)S(1)} %get-tuple-element.47.r_2_, s32[32,8,256]{2,1,0:T(8,128)S(1)} %get-tuple-element.48.r_3_, f32[3,32,8,256]{3,2,1,0:T(8,128)S(1)} %get-tuple-element.67.r_4_, ...), custom_call_target="tpu_custom_call" | custom-call | tf_op jit(solution)/shard_map/backward0/pallas_call | solution.py:45
  74.8 1.9 %terms.1 = (f32[512,128]{1,0:T(8,128)S(1)}, f32[512,128]{1,0:T(8,128)S(1)}) custom-call(f32[3,32,8,256]{3,2,1,0:T(8,128)S(1)} %backward0.1.s_ref, bf16[256,1024]{1,0:T(8,128)(2,1)S(1)} %get-tuple-element.83.rt_ref, bf16[1024,1024]{1,0:T(8,128)(2,1)S(1)} %get-tuple-element.84.kh_ref, s32[1,1024]{1,0:T(1,128)S(1)} %get-tuple-element.85.lo_ref, ...), custom_call_target="tpu_custom_call" | custom-call | tf_op jit(solution)/shard_map/terms/pallas_call | solution.py:45
  76.7 1.3 %collective-permute-start.24 = (f32[512,128]{1,0:T(8,128)S(1)}, f32[512,128]{1,0:T(8,128)S(1)}, u32[]{:S(2)}, u32[]{:S(2)}) collective-permute-start(f32[512,128]{1,0:T(8,128)S(1)} %get-tuple-element.87), channel_id=1, source_target_pairs={{0,1},{1,0},{2,3},{3,2},{4,5},{5,4},{6,7},{7,6},{8,9},{9,8},{10,11... | collective-permute-start | bytes 786440 | tf_op jit(solution)/shard_map/ppermute | solution.py:393
  78.0 1.2 collective-permute-done.24
  79.2 17.3 %all_to_all.10.got_ref = f32[64,8,128]{2,1,0:T(8,128)S(1)} all-to-all(f32[64,8,128]{2,1,0:T(8,128)S(1)} %add_bitcast_fusion), channel_id=1, replica_groups={{0,2,4,6,8,10,12,14,16,18,20,22,24,26,28,30,32,34,36,38,40,42,44,46,48,..., dimensions={0} | all-to-all | bytes 524288 | tf_op jit(solution)/shard_map/all_to_all | solution.py:394
  96.8 13.7 %all_to_all.11 = f32[64,8,128]{2,1,0:T(8,128)S(1)} all-to-all(f32[64,8,128]{2,1,0:T(8,128)S(1)} %solve.1), channel_id=1, replica_groups={{0,2,4,6,8,10,12,14,16,18,20,22,24,26,28,30,32,34,36,38,40,42,44,46,48,..., dimensions={0} | all-to-all | bytes 524288 | tf_op jit(solution)/shard_map/all_to_all | solution.py:398
  110.5 3.0 %collective-permute-start.25 = (f32[512,128]{1,0:T(8,128)S(1)}, f32[512,128]{1,0:T(8,128)S(1)}, u32[]{:S(2)}, u32[]{:S(2)}) collective-permute-start(f32[512,128]{1,0:T(8,128)S(1)} %bitcast.18), channel_id=1, source_target_pairs={{0,1},{1,0},{2,3},{3,2},{4,5},{5,4},{6,7},{7,6},{8,9},{9,8},{10,11... | collective-permute-start | bytes 786440 | tf_op jit(solution)/shard_map/ppermute | solution.py:399
  113.5 1.2 collective-permute-done.25.other_ref
  114.7 2.7 %back.1 = f32[3,32,8,256]{3,2,1,0:T(8,128)} custom-call(f32[512,128]{1,0:T(8,128)S(1)} %bitcast.19, f32[512,128]{1,0:T(8,128)S(1)} %collective-permute-done.25.other_ref, f32[3,32,8,256]{3,2,1,0:T(8,128)S(1)} %backward0.1.s_ref, bf16[256,1024]{1,0:T(8,128)(2,1)S(1)} %get-tuple-element.83.rt_ref, bf16[1024,1024]{1,0:T(8,128)(2,1)S(1)} %get-tuple-element.84.kh_ref, ...), custom_call_target="tpu_custom_call" | custom-call | tf_op jit(solution)/shard_map/back/pallas_call | solution.py:400
  (60 shorter events, 5.8 us)
Async XLA Ops:
  0.0 13.6 %slice-start = ((s8[14155776]{0:T(1024)(128)(4,1)}), s8[1572864]{0:T(1024)(128)(4,1)S(1)}, s32[]{:S(2)}) async-start(s8[14155776]{0:T(1024)(128)(4,1)} %bitcast.16), calls=%async_computation.2 | async-start | bytes 3145728
  0.1 13.6 %slice-start.1 = ((s8[14155776]{0:T(1024)(128)(4,1)}), s8[4194304]{0:T(1024)(128)(4,1)S(1)}, s32[]{:S(2)}) async-start(s8[14155776]{0:T(1024)(128)(4,1)} %bitcast.16), calls=%async_computation.3 | async-start | bytes 8388608
  0.1 13.6 %slice-start.2 = ((s8[14155776]{0:T(1024)(128)(4,1)}), s8[4194304]{0:T(1024)(128)(4,1)S(1)}, s32[]{:S(2)}) async-start(s8[14155776]{0:T(1024)(128)(4,1)} %bitcast.16), calls=%async_computation.4 | async-start | bytes 8388608
  0.1 13.6 %slice-start.3 = ((s8[14155776]{0:T(1024)(128)(4,1)}), s8[4194304]{0:T(1024)(128)(4,1)S(1)}, s32[]{:S(2)}) async-start(s8[14155776]{0:T(1024)(128)(4,1)} %bitcast.16), calls=%async_computation.5 | async-start | bytes 8388608
  3.2 10.4 %collective-permute-start.2 = (f32[96,256]{1,0:T(8,128)S(1)}, f32[96,256]{1,0:T(8,128)S(1)}, u32[]{:S(2)}, u32[]{:S(2)}) collective-permute-start(f32[96,256]{1,0:T(8,128)S(1)} %get-tuple-element.53), channel_id=1, source_target_pairs={{0,1},{1,0},{2,3},{3,2},{4,5},{5,4},{6,7},{7,6},{8,9},{9,8},{10,11... | collective-permute-start | bytes 294920 | tf_op jit(solution)/shard_map/ppermute | solution.py:232
  4.7 9.0 %collective-permute-start.3 = (f32[96,256]{1,0:T(8,128)S(1)}, f32[96,256]{1,0:T(8,128)S(1)}, u32[]{:S(2)}, u32[]{:S(2)}) collective-permute-start(f32[96,256]{1,0:T(8,128)S(1)} %get-tuple-element.54), channel_id=1, source_target_pairs={{1,2},{2,1},{3,4},{4,3},{5,6},{6,5},{7,0},{0,7},{9,10},{10,9},{11,... | collective-permute-start | bytes 294920 | tf_op jit(solution)/shard_map/ppermute | solution.py:230
  6.0 6.7 %collective-permute-start = (f32[8,128]{1,0:T(8,128)S(1)}, f32[8,128]{1,0:T(8,128)S(1)}, u32[]{:S(2)}, u32[]{:S(2)}) collective-permute-start(f32[8,128]{1,0:T(8,128)S(1)} %get-tuple-element.51), channel_id=1, source_target_pairs={{0,8},{8,0},{16,24},{24,16},{32,40},{40,32},{48,56},{56,48},{64,72... | collective-permute-start | bytes 12296 | tf_op jit(solution)/shard_map/ppermute | solution.py:231
  7.3 6.4 %collective-permute-start.1 = (f32[8,128]{1,0:T(8,128)S(1)}, f32[8,128]{1,0:T(8,128)S(1)}, u32[]{:S(2)}, u32[]{:S(2)}) collective-permute-start(f32[8,128]{1,0:T(8,128)S(1)} %get-tuple-element.52), channel_id=1, source_target_pairs={{8,16},{16,8},{24,32},{32,24},{40,48},{48,40},{56,64},{64,56},{72,... | collective-permute-start | bytes 12296 | tf_op jit(solution)/shard_map/ppermute | solution.py:229
  16.8 9.0 %collective-permute-start.6 = (f32[96,256]{1,0:T(8,128)S(1)}, f32[96,256]{1,0:T(8,128)S(1)}, u32[]{:S(2)}, u32[]{:S(2)}) collective-permute-start(f32[96,256]{1,0:T(8,128)S(1)} %get-tuple-element.59), channel_id=1, source_target_pairs={{0,1},{1,0},{2,3},{3,2},{4,5},{5,4},{6,7},{7,6},{8,9},{9,8},{10,11... | collective-permute-start | bytes 294920 | tf_op jit(solution)/shard_map/ppermute | solution.py:232
  19.7 6.1 %collective-permute-start.7 = (f32[96,256]{1,0:T(8,128)S(1)}, f32[96,256]{1,0:T(8,128)S(1)}, u32[]{:S(2)}, u32[]{:S(2)}) collective-permute-start(f32[96,256]{1,0:T(8,128)S(1)} %get-tuple-element.60), channel_id=1, source_target_pairs={{1,2},{2,1},{3,4},{4,3},{5,6},{6,5},{7,0},{0,7},{9,10},{10,9},{11,... | collective-permute-start | bytes 294920 | tf_op jit(solution)/shard_map/ppermute | solution.py:230
  19.7 5.1 %collective-permute-start.4 = (f32[8,128]{1,0:T(8,128)S(1)}, f32[8,128]{1,0:T(8,128)S(1)}, u32[]{:S(2)}, u32[]{:S(2)}) collective-permute-start(f32[8,128]{1,0:T(8,128)S(1)} %get-tuple-element.57), channel_id=1, source_target_pairs={{0,8},{8,0},{16,24},{24,16},{32,40},{40,32},{48,56},{56,48},{64,72... | collective-permute-start | bytes 12296 | tf_op jit(solution)/shard_map/ppermute | solution.py:231
  19.7 6.1 %collective-permute-start.5 = (f32[8,128]{1,0:T(8,128)S(1)}, f32[8,128]{1,0:T(8,128)S(1)}, u32[]{:S(2)}, u32[]{:S(2)}) collective-permute-start(f32[8,128]{1,0:T(8,128)S(1)} %get-tuple-element.58), channel_id=1, source_target_pairs={{8,16},{16,8},{24,32},{32,24},{40,48},{48,40},{56,64},{64,56},{72,... | collective-permute-start | bytes 12296 | tf_op jit(solution)/shard_map/ppermute | solution.py:229
  28.8 8.8 %collective-permute-start.10 = (f32[96,256]{1,0:T(8,128)S(1)}, f32[96,256]{1,0:T(8,128)S(1)}, u32[]{:S(2)}, u32[]{:S(2)}) collective-permute-start(f32[96,256]{1,0:T(8,128)S(1)} %get-tuple-element.65), channel_id=1, source_target_pairs={{0,1},{1,0},{2,3},{3,2},{4,5},{5,4},{6,7},{7,6},{8,9},{9,8},{10,11... | collective-permute-start | bytes 294920 | tf_op jit(solution)/shard_map/ppermute | solution.py:232
  30.7 7.0 %collective-permute-start.11 = (f32[96,256]{1,0:T(8,128)S(1)}, f32[96,256]{1,0:T(8,128)S(1)}, u32[]{:S(2)}, u32[]{:S(2)}) collective-permute-start(f32[96,256]{1,0:T(8,128)S(1)} %get-tuple-element.66), channel_id=1, source_target_pairs={{1,2},{2,1},{3,4},{4,3},{5,6},{6,5},{7,0},{0,7},{9,10},{10,9},{11,... | collective-permute-start | bytes 294920 | tf_op jit(solution)/shard_map/ppermute | solution.py:230
  31.6 5.1 %collective-permute-start.8 = (f32[8,128]{1,0:T(8,128)S(1)}, f32[8,128]{1,0:T(8,128)S(1)}, u32[]{:S(2)}, u32[]{:S(2)}) collective-permute-start(f32[8,128]{1,0:T(8,128)S(1)} %get-tuple-element.63), channel_id=1, source_target_pairs={{0,8},{8,0},{16,24},{24,16},{32,40},{40,32},{48,56},{56,48},{64,72... | collective-permute-start | bytes 12296 | tf_op jit(solution)/shard_map/ppermute | solution.py:231
  31.6 6.1 %collective-permute-start.9 = (f32[8,128]{1,0:T(8,128)S(1)}, f32[8,128]{1,0:T(8,128)S(1)}, u32[]{:S(2)}, u32[]{:S(2)}) collective-permute-start(f32[8,128]{1,0:T(8,128)S(1)} %get-tuple-element.64), channel_id=1, source_target_pairs={{8,16},{16,8},{24,32},{32,24},{40,48},{48,40},{56,64},{64,56},{72,... | collective-permute-start | bytes 12296 | tf_op jit(solution)/shard_map/ppermute | solution.py:229
  40.7 8.0 %collective-permute-start.14 = (f32[96,256]{1,0:T(8,128)S(1)}, f32[96,256]{1,0:T(8,128)S(1)}, u32[]{:S(2)}, u32[]{:S(2)}) collective-permute-start(f32[96,256]{1,0:T(8,128)S(1)} %get-tuple-element.71), channel_id=1, source_target_pairs={{0,1},{1,0},{2,3},{3,2},{4,5},{5,4},{6,7},{7,6},{8,9},{9,8},{10,11... | collective-permute-start | bytes 294920 | tf_op jit(solution)/shard_map/ppermute | solution.py:232
  42.1 6.6 %collective-permute-start.15 = (f32[96,256]{1,0:T(8,128)S(1)}, f32[96,256]{1,0:T(8,128)S(1)}, u32[]{:S(2)}, u32[]{:S(2)}) collective-permute-start(f32[96,256]{1,0:T(8,128)S(1)} %get-tuple-element.72), channel_id=1, source_target_pairs={{1,2},{2,1},{3,4},{4,3},{5,6},{6,5},{7,0},{0,7},{9,10},{10,9},{11,... | collective-permute-start | bytes 294920 | tf_op jit(solution)/shard_map/ppermute | solution.py:230
  42.6 5.1 %collective-permute-start.12 = (f32[8,128]{1,0:T(8,128)S(1)}, f32[8,128]{1,0:T(8,128)S(1)}, u32[]{:S(2)}, u32[]{:S(2)}) collective-permute-start(f32[8,128]{1,0:T(8,128)S(1)} %get-tuple-element.69), channel_id=1, source_target_pairs={{0,8},{8,0},{16,24},{24,16},{32,40},{40,32},{48,56},{56,48},{64,72... | collective-permute-start | bytes 12296 | tf_op jit(solution)/shard_map/ppermute | solution.py:231
  42.6 6.1 %collective-permute-start.13 = (f32[8,128]{1,0:T(8,128)S(1)}, f32[8,128]{1,0:T(8,128)S(1)}, u32[]{:S(2)}, u32[]{:S(2)}) collective-permute-start(f32[8,128]{1,0:T(8,128)S(1)} %get-tuple-element.70), channel_id=1, source_target_pairs={{8,16},{16,8},{24,32},{32,24},{40,48},{48,40},{56,64},{64,56},{72,... | collective-permute-start | bytes 12296 | tf_op jit(solution)/shard_map/ppermute | solution.py:229
  51.7 8.1 %collective-permute-start.18 = (f32[96,256]{1,0:T(8,128)S(1)}, f32[96,256]{1,0:T(8,128)S(1)}, u32[]{:S(2)}, u32[]{:S(2)}) collective-permute-start(f32[96,256]{1,0:T(8,128)S(1)} %get-tuple-element.76), channel_id=1, source_target_pairs={{0,1},{1,0},{2,3},{3,2},{4,5},{5,4},{6,7},{7,6},{8,9},{9,8},{10,11... | collective-permute-start | bytes 294920 | tf_op jit(solution)/shard_map/ppermute | solution.py:232
  53.1 6.7 %collective-permute-start.19 = (f32[96,256]{1,0:T(8,128)S(1)}, f32[96,256]{1,0:T(8,128)S(1)}, u32[]{:S(2)}, u32[]{:S(2)}) collective-permute-start(f32[96,256]{1,0:T(8,128)S(1)} %get-tuple-element.77), channel_id=1, source_target_pairs={{1,2},{2,1},{3,4},{4,3},{5,6},{6,5},{7,0},{0,7},{9,10},{10,9},{11,... | collective-permute-start | bytes 294920 | tf_op jit(solution)/shard_map/ppermute | solution.py:230
  54.0 4.8 %collective-permute-start.16 = (f32[8,128]{1,0:T(8,128)S(1)}, f32[8,128]{1,0:T(8,128)S(1)}, u32[]{:S(2)}, u32[]{:S(2)}) collective-permute-start(f32[8,128]{1,0:T(8,128)S(1)} %get-tuple-element.74), channel_id=1, source_target_pairs={{0,8},{8,0},{16,24},{24,16},{32,40},{40,32},{48,56},{56,48},{64,72... | collective-permute-start | bytes 12296 | tf_op jit(solution)/shard_map/ppermute | solution.py:231
  54.0 5.8 %collective-permute-start.17 = (f32[8,128]{1,0:T(8,128)S(1)}, f32[8,128]{1,0:T(8,128)S(1)}, u32[]{:S(2)}, u32[]{:S(2)}) collective-permute-start(f32[8,128]{1,0:T(8,128)S(1)} %get-tuple-element.75), channel_id=1, source_target_pairs={{8,16},{16,8},{24,32},{32,24},{40,48},{48,40},{56,64},{64,56},{72,... | collective-permute-start | bytes 12296 | tf_op jit(solution)/shard_map/ppermute | solution.py:229
  62.9 9.4 %collective-permute-start.22 = (f32[96,256]{1,0:T(8,128)S(1)}, f32[96,256]{1,0:T(8,128)S(1)}, u32[]{:S(2)}, u32[]{:S(2)}) collective-permute-start(f32[96,256]{1,0:T(8,128)S(1)} %get-tuple-element.81), channel_id=1, source_target_pairs={{0,1},{1,0},{2,3},{3,2},{4,5},{5,4},{6,7},{7,6},{8,9},{9,8},{10,11... | collective-permute-start | bytes 294920 | tf_op jit(solution)/shard_map/ppermute | solution.py:232
  65.2 7.1 %collective-permute-start.23 = (f32[96,256]{1,0:T(8,128)S(1)}, f32[96,256]{1,0:T(8,128)S(1)}, u32[]{:S(2)}, u32[]{:S(2)}) collective-permute-start(f32[96,256]{1,0:T(8,128)S(1)} %get-tuple-element.82), channel_id=1, source_target_pairs={{1,2},{2,1},{3,4},{4,3},{5,6},{6,5},{7,0},{0,7},{9,10},{10,9},{11,... | collective-permute-start | bytes 294920 | tf_op jit(solution)/shard_map/ppermute | solution.py:230
  65.2 7.1 %collective-permute-start.20 = (f32[8,128]{1,0:T(8,128)S(1)}, f32[8,128]{1,0:T(8,128)S(1)}, u32[]{:S(2)}, u32[]{:S(2)}) collective-permute-start(f32[8,128]{1,0:T(8,128)S(1)} %get-tuple-element.79), channel_id=1, source_target_pairs={{0,8},{8,0},{16,24},{24,16},{32,40},{40,32},{48,56},{56,48},{64,72... | collective-permute-start | bytes 12296 | tf_op jit(solution)/shard_map/ppermute | solution.py:231
  65.2 7.1 %collective-permute-start.21 = (f32[8,128]{1,0:T(8,128)S(1)}, f32[8,128]{1,0:T(8,128)S(1)}, u32[]{:S(2)}, u32[]{:S(2)}) collective-permute-start(f32[8,128]{1,0:T(8,128)S(1)} %get-tuple-element.80), channel_id=1, source_target_pairs={{8,16},{16,8},{24,32},{32,24},{40,48},{48,40},{56,64},{64,56},{72,... | collective-permute-start | bytes 12296 | tf_op jit(solution)/shard_map/ppermute | solution.py:229
  74.7 21.8 %copy-start = (f32[64,16,16]{0,2,1:T(8,128)S(1)}, f32[64,16,16]{0,2,1:T(8,128)}, u32[]{:S(2)}) copy-start(f32[64,16,16]{0,2,1:T(8,128)} %param.23) | copy-start | bytes 196612
  74.7 40.0 %copy-start.5 = (f32[3,1024]{1,0:T(4,128)S(1)}, f32[3,1024]{1,0:T(4,128)}, u32[]{:S(2)}) copy-start(f32[3,1024]{1,0:T(4,128)} %back_ref.1) | copy-start | bytes 36868
  76.7 2.5 %collective-permute-start.24 = (f32[512,128]{1,0:T(8,128)S(1)}, f32[512,128]{1,0:T(8,128)S(1)}, u32[]{:S(2)}, u32[]{:S(2)}) collective-permute-start(f32[512,128]{1,0:T(8,128)S(1)} %get-tuple-element.87), channel_id=1, source_target_pairs={{0,1},{1,0},{2,3},{3,2},{4,5},{5,4},{6,7},{7,6},{8,9},{9,8},{10,11... | collective-permute-start | bytes 786440 | tf_op jit(solution)/shard_map/ppermute | solution.py:393
  110.5 4.2 %collective-permute-start.25 = (f32[512,128]{1,0:T(8,128)S(1)}, f32[512,128]{1,0:T(8,128)S(1)}, u32[]{:S(2)}, u32[]{:S(2)}) collective-permute-start(f32[512,128]{1,0:T(8,128)S(1)} %bitcast.18), channel_id=1, source_target_pairs={{0,1},{1,0},{2,3},{3,2},{4,5},{5,4},{6,7},{7,6},{8,9},{9,8},{10,11... | collective-permute-start | bytes 786440 | tf_op jit(solution)/shard_map/ppermute | solution.py:399
  (6 other events, 54.6 us)

commit v4 on v3

--- a/solution.py
+++ b/solution.py
@@ -145,6 +145,8 @@
         prep_body(meta_ref, *prep_in, *prep_out)
     lane = iota((ny, 128), 1)
     row = iota((ny, nx), 0)
+    first_lane, last_lane = lane == 0, lane == 127
+    first_row, last_row = row == 0, row == ny - 1
     x_odd = meta_ref[5] > 0
     y_odd = meta_ref[6] > 0
     has = [meta_ref[k] > 0 for k in range(1, 5)]
@@ -158,30 +160,29 @@
         zero_ends(nv_ref, nz)
 
     def step(z, edges):
-        acc = [jnp.zeros((ny, nx), F32) for _ in range(3)]
+        cur = [base_ref[j, z] for j in range(3)]
+        base = list(cur)
         old = []
         for j in range(3):
             at = j * nz + z
             vc = v_ref[j, z + 1]
             old.append(vc)
-            xm = pltpu.roll(vc, 1, 1)
-            head = jnp.where(lane == 0, pltpu.roll(hxlo, (128 - at) % 128, 1), xm[:, :128])
-            xm = jnp.concatenate([head, xm[:, 128:]], axis=1)
-            xp = pltpu.roll(vc, nx - 1, 1)
-            tail = jnp.where(lane == 127, pltpu.roll(hxhi, 127 - at, 1), xp[:, -128:])
-            xp = jnp.concatenate([xp[:, :-128], tail], axis=1)
-            ym = jnp.where(row == 0, hylo_ref[pl.ds(at, 1), :], pltpu.roll(vc, 1, 0))
-            yp = jnp.where(row == ny - 1, hyhi_ref[pl.ds(at, 1), :], pltpu.roll(vc, ny - 1, 0))
+            below = [pltpu.roll(vc[:, k : k + 128], 1, 1) for k in range(0, nx, 128)]
+            above = [pltpu.roll(vc[:, k : k + 128], 127, 1) for k in range(0, nx, 128)]
+            lead = [pltpu.roll(hxlo, (128 - at) % 128, 1)] + below[:-1]
+            trail = above[1:] + [pltpu.roll(hxhi, 127 - at, 1)]
+            xm = jnp.concatenate([jnp.where(first_lane, p, q) for p, q in zip(lead, below)], axis=1)
+            xp = jnp.concatenate([jnp.where(last_lane, p, q) for p, q in zip(trail, above)], axis=1)
+            ym = jnp.where(first_row, hylo_ref[pl.ds(at, 1), :], pltpu.roll(vc, 1, 0))
+            yp = jnp.where(last_row, hyhi_ref[pl.ds(at, 1), :], pltpu.roll(vc, ny - 1, 0))
             zm = v_ref[j, z]
             zp = v_ref[j, z + 2]
             for i in range(3):
                 t = coup_ref[0, i, j, z] * xm + coup_ref[1, i, j, z] * xp
                 t = t + (coup_ref[2, i, j, z] * ym + coup_ref[3, i, j, z] * yp)
                 t = t + (coup_ref[4, i, j, z] * zm + coup_ref[5, i, j, z] * zp)
-                acc[i] = acc[i] + t
+                cur[i] = cur[i] - t
         chosen = col_ref[z] == colour
-        base = [base_ref[j, z] for j in range(3)]
-        cur = [base[j] - acc[j] for j in range(3)]
         new = []
         for i in range(3):
             p = piv_ref[i, 0, z] * cur[0] + piv_ref[i, 1, z] * cur[1] + piv_ref[i, 2, z] * cur[2]
@@ -214,23 +215,39 @@
         store_edges(meta_ref, edges, ylo_ref, yhi_ref, *edge_refs)
 
 
-def swaps(size, odd):
-    out = []
-    for i in range(odd, size + odd, 2):
-        a, b = i % size, (i + 1) % size
-        out += [(a, b), (b, a)]
-    return out
+def both_ways(pairs):
+    return [(a, b) for a, b in pairs] + [(b, a) for a, b in pairs]
+
+
+def partners(nx, ny):
+    at = lambda x, y: x * ny + y
+    x_even = [(at(x, y), at(x + 1, y)) for x in range(0, nx, 2) for y in range(ny)]
+    y_even = [(at(x, y), at(x, y + 1)) for y in range(0, ny, 2) for x in range(nx)]
+    x_odd = [(at(x, y), at(x + 1, y)) for x in range(1, nx - 1, 2) for y in range(ny)]
+    x_odd += [(at(x, y), at(x, y + 1)) for x in (0, nx - 1) for y in range(0, ny, 2)]
+    y_odd = [(at(x, y), at(x, y + 1)) for y in range(1, ny - 1, 2) for x in range(nx)]
+    y_odd += [(at(x, y), at(x + 1, y)) for y in (0, ny - 1) for x in range(0, nx, 2)]
+    return [both_ways(p) for p in (x_even, x_odd, y_even, y_odd)]
 
 
 def halos(edges):
     xa, xb, ya, yb = edges
-    nx = lax.axis_size("gx")
-    ny = lax.axis_size("gy")
-    hxb = lax.ppermute(xb, "gx", swaps(nx, 1))
-    hyb = lax.ppermute(yb, "gy", swaps(ny, 1))
-    hxa = lax.ppermute(xa, "gx", swaps(nx, 0))
-    hya = lax.ppermute(ya, "gy", swaps(ny, 0))
+    axes = ("gx", "gy")
+    x_even, x_odd, y_even, y_odd = partners(lax.axis_size("gx"), lax.axis_size("gy"))
+    hxb = lax.ppermute(xb, axes, x_odd)
+    hyb = lax.ppermute(yb, axes, y_odd)
+    hxa = lax.ppermute(xa, axes, x_even)
+    hya = lax.ppermute(ya, axes, y_even)
     return hxa, hxb, hya, hyb
+
+
+def one_hot_rows(ref, rows):
+    n = ref.shape[1]
+    step = jnp.broadcast_to(rows, (16, n)) - iota((16, n), 0)
+    step = step.astype(jnp.int16)
+    one, zero = jnp.ones((16, n), BF16), jnp.zeros((16, n), BF16)
+    for at in range(0, ref.shape[0], 16):
+        ref[at : at + 16, :] = jnp.where(step == jnp.int16(at), one, zero)
 
 
 def prep_body(meta_ref, slot_ref, count_ref, cells_ref, wells_ref, segs_ref, kh_ref, rt_ref, alive_ref, lo_ref):
@@ -247,8 +264,8 @@
     tile = meta_ref[0]
     rows = ((owner ^ tile) & 1) * 512 + (owner >> 1) * 8 + (segs & 7)
     lo_ref[...] = (segs >> 3) * 64 + (slot & 63)
-    kh_ref[...] = (iota(kh_ref.shape, 0) == rows).astype(F32).astype(BF16)
-    rt_ref[...] = (iota(rt_ref.shape, 0) == (cells_ref[...] >> 8)).astype(F32).astype(BF16)
+    one_hot_rows(kh_ref, rows)
+    one_hot_rows(rt_ref, cells_ref[...] >> 8)
     own_slot = slot_ref[pl.ds(tile // 2, 1), :] - tile * 64
     own_count = jnp.broadcast_to(count_ref[pl.ds(tile // 2, 1), :].astype(F32), (8, 128)).astype(BF16)
     match = (iota((128, 128), 0) == own_slot).astype(F32).astype(BF16)
@@ -385,18 +402,18 @@
             scratch=rows,
             name=f"backward{colour}",
         )
-    pairs = swaps(lax.axis_size("gy"), 0)
+    pairs = partners(lax.axis_size("gx"), lax.axis_size("gy"))[2]
     cores = [[d for d in range(devices) if d % 2 == core] for core in range(2)]
     mine, other = call(
         terms_body, [((512, 128), F32)] * 2, [v, rt, kh, low, cells, perf_gather], name="terms", limit=24 << 20
     )
-    mine = mine + lax.ppermute(other, "gy", pairs)
+    mine = mine + lax.ppermute(other, axes, pairs)
     got = lax.all_to_all(mine.reshape(64, 8, 128), axes, 0, 0, axis_index_groups=cores, tiled=True)
     (values,) = call(
         solve_body, [((64, 8, 128), F32)], [got, well_inverses.transpose(1, 2, 0), alive], name="solve"
     )
     mine = lax.all_to_all(values, axes, 0, 0, axis_index_groups=cores, tiled=True).reshape(512, 128)
-    other = lax.ppermute(mine, "gy", pairs)
+    other = lax.ppermute(mine, axes, pairs)
     return pl.pallas_call(
         return_body,
         out_shape=jax.ShapeDtypeStruct(plain[0], F32),

time: 118 us -> 112 us (0.949)
  starting transfers between devices: 50.9 us -> 37.7 us
  blocking collectives: 31.1 us -> 37.7 us
  waiting for transfers between devices: 7.33 us -> 9.59 us
    ppermute x26, starting transfers between devices: 50.9 us -> 37.7 us  [the longest x6 24.1 us: halos(): hxa = lax.ppermute(xa, axes, x_even)]
    all_to_all x1, blocking collectives: 17.3 us -> 23.9 us  [shards(): lax.all_to_all(mine.reshape(64, 8, 128), axes, 0, 0, axis_index_groups=co...]
    ppermute x26, waiting for transfers between devices: 7.33 us -> 9.59 us  [the longest x6 5.8 us: halos(): hxa = lax.ppermute(xa, axes, x_even)]
  transfers between devices with their start and end apart: 26 -> 26, of which waited for: 7 -> 12; matrix products, arithmetic and copies ran while one was open for 0% -> 0% of each run, Pallas kernels for 2% -> 1%
where the time goes in v4:
time: 112 us
  starting transfers between devices  37.7 us (34%)
  blocking collectives  37.7 us (34%)
  Pallas kernels  26.8 us (24%)
  waiting for transfers between devices  9.59 us (9%)
    pallas_call x10, Pallas kernels, call(): pl.pallas_call(body, out_shape=tuple((pltpu.VMEM(s, d) for s, d in outs))...  24.2 us
    ppermute x6, starting transfers between devices, halos(): hxa = lax.ppermute(xa, axes, x_even)  24.1 us
    all_to_all x1, blocking collectives, shards(): lax.all_to_all(mine.reshape(64, 8, 128), axes, 0, 0, axis_index_groups=co...  23.9 us
    all_to_all x1, blocking collectives, shards(): lax.all_to_all(values, axes, 0, 0, axis_index_groups=cores, tiled=True)  13.8 us
    ppermute x6, starting transfers between devices, halos(): hya = lax.ppermute(ya, axes, y_even)  7.87 us
    ppermute x6, waiting for transfers between devices, halos(): hxa = lax.ppermute(xa, axes, x_even)  5.8 us
    ppermute x1, starting transfers between devices, shards(): other = lax.ppermute(mine, axes, pairs)  3.04 us
    pallas_call x1, Pallas kernels, shards(): pl.pallas_call(return_body, out_shape=jax.ShapeDtypeStruct(plain[0], F32)...  2.69 us
  transfers between devices with their start and end apart: 26, of which 12 were waited for; matrix products, arithmetic and copies ran while one was open for 0% of the time, Pallas kernels for 1%

profile of v4, /device:TPU:1, one launch (start us, length us, event | category | flops | bytes accessed | tf_op | source)
XLA Modules:
  0.0 112.2 jit_solution(6632181782829480382)
XLA Ops:
  0.1 3.1 %first.1 = (f32[3,32,8,256]{3,2,1,0:T(8,128)S(1)}, f32[3,3,32,8,256]{4,3,2,1,0:T(8,128)S(1)}, s32[32,8,256]{2,1,0:T(8,128)S(1)}, f32[3,34,8,256]{3,2,1,0:T(8,128...) custom-call(s32[7]{0:T(128)S(1)} %stack.47.meta_ref.r_0_, ...), custom_call_target="tpu_custom_call" | custom-call | flops 10000000000 | bytes 100000000 | tf_op jit(solution)/shard_map/first/pallas_call | solution.py:45
  3.2 1.5 %collective-permute-start.2 = (f32[96,256]{1,0:T(8,128)S(1)}, f32[96,256]{1,0:T(8,128)S(1)}, u32[]{:S(2)}, u32[]{:S(2)}) collective-permute-start(f32[96,256]{1,0:T(8,128)S(1)} %get-tuple-element.53), channel_id=1, source_target_pairs={{0,1},{8,9},{16,17},{24,25},{32,33},{40,41},{48,49},{56,57},{64,65... | collective-permute-start | bytes 294920 | tf_op jit(solution)/shard_map/ppermute | solution.py:240
  4.7 1.3 %collective-permute-start.3 = (f32[96,256]{1,0:T(8,128)S(1)}, f32[96,256]{1,0:T(8,128)S(1)}, u32[]{:S(2)}, u32[]{:S(2)}) collective-permute-start(f32[96,256]{1,0:T(8,128)S(1)} %get-tuple-element.54), channel_id=1, source_target_pairs={{1,2},{9,10},{17,18},{25,26},{33,34},{41,42},{49,50},{57,58},{65,6... | collective-permute-start | bytes 294920 | tf_op jit(solution)/shard_map/ppermute | solution.py:238
  6.0 1.3 %collective-permute-start = (f32[8,128]{1,0:T(8,128)S(1)}, f32[8,128]{1,0:T(8,128)S(1)}, u32[]{:S(2)}, u32[]{:S(2)}) collective-permute-start(f32[8,128]{1,0:T(8,128)S(1)} %get-tuple-element.51), channel_id=1, source_target_pairs={{0,8},{1,9},{2,10},{3,11},{4,12},{5,13},{6,14},{7,15},{16,24},{17,... | collective-permute-start | bytes 12296 | tf_op jit(solution)/shard_map/ppermute | solution.py:239
  7.3 1.5 %collective-permute-done.r_6_ = f32[8,128]{1,0:T(8,128)S(1)} collective-permute-done((f32[8,128]{1,0:T(8,128)S(1)}, f32[8,128]{1,0:T(8,128)S(1)}, u32[]{:S(2)}, u32[]{:S(2)}) %collective-permute-start) | collective-permute-done | bytes 4128 | tf_op jit(solution)/shard_map/ppermute | solution.py:239
  9.0 3.1 %forward1.1 = (f32[3,32,8,256]{3,2,1,0:T(8,128)S(1)}, f32[3,34,8,256]{3,2,1,0:T(8,128)S(1)}, f32[8,128]{1,0:T(8,128)S(1)}, f32[8,128]{1,0:T(8,128)S(1)}, f32[96,256]{1,0:T(8,128)S(1)}, /*index=5*/f32[96,256]{1,0:T(8,128)S(1)}) custom-call(s32[7]{0:T(128)S(1)} %stack.47.meta_ref.r_0_, f32[6,3,3,32,8,256]{5,4,3,2,1,0:T(8,128)S(1)} %bitcast.17, ...), custom_call_target="tpu_custom_call" | custom-call | tf_op jit(solution)/shard_map/forward1/pallas_call | solution.py:45
  12.1 1.2 %collective-permute-start.6 = (f32[96,256]{1,0:T(8,128)S(1)}, f32[96,256]{1,0:T(8,128)S(1)}, u32[]{:S(2)}, u32[]{:S(2)}) collective-permute-start(f32[96,256]{1,0:T(8,128)S(1)} %get-tuple-element.59), channel_id=1, source_target_pairs={{0,1},{8,9},{16,17},{24,25},{32,33},{40,41},{48,49},{56,57},{64,65... | collective-permute-start | bytes 294920 | tf_op jit(solution)/shard_map/ppermute | solution.py:240
  13.6 2.0 %collective-permute-start.4 = (f32[8,128]{1,0:T(8,128)S(1)}, f32[8,128]{1,0:T(8,128)S(1)}, u32[]{:S(2)}, u32[]{:S(2)}) collective-permute-start(f32[8,128]{1,0:T(8,128)S(1)} %get-tuple-element.57), channel_id=1, source_target_pairs={{0,8},{1,9},{2,10},{3,11},{4,12},{5,13},{6,14},{7,15},{16,24},{17,... | collective-permute-start | bytes 12296 | tf_op jit(solution)/shard_map/ppermute | solution.py:239
  15.6 1.3 %collective-permute-done.4.r_6_ = f32[8,128]{1,0:T(8,128)S(1)} collective-permute-done((f32[8,128]{1,0:T(8,128)S(1)}, f32[8,128]{1,0:T(8,128)S(1)}, u32[]{:S(2)}, u32[]{:S(2)}) %collective-permute-start.4) | collective-permute-done | bytes 4128 | tf_op jit(solution)/shard_map/ppermute | solution.py:239
  17.6 3.0 %forward2.1 = (f32[3,32,8,256]{3,2,1,0:T(8,128)S(1)}, f32[3,34,8,256]{3,2,1,0:T(8,128)S(1)}, f32[8,128]{1,0:T(8,128)S(1)}, f32[8,128]{1,0:T(8,128)S(1)}, f32[96,256]{1,0:T(8,128)S(1)}, /*index=5*/f32[96,256]{1,0:T(8,128)S(1)}) custom-call(s32[7]{0:T(128)S(1)} %stack.47.meta_ref.r_0_, f32[6,3,3,32,8,256]{5,4,3,2,1,0:T(8,128)S(1)} %bitcast.17, ...), custom_call_target="tpu_custom_call" | custom-call | tf_op jit(solution)/shard_map/forward2/pallas_call | solution.py:45
  20.7 1.5 %collective-permute-start.10 = (f32[96,256]{1,0:T(8,128)S(1)}, f32[96,256]{1,0:T(8,128)S(1)}, u32[]{:S(2)}, u32[]{:S(2)}) collective-permute-start(f32[96,256]{1,0:T(8,128)S(1)} %get-tuple-element.65), channel_id=1, source_target_pairs={{0,1},{8,9},{16,17},{24,25},{32,33},{40,41},{48,49},{56,57},{64,65... | collective-permute-start | bytes 294920 | tf_op jit(solution)/shard_map/ppermute | solution.py:240
  22.2 4.4 %collective-permute-start.8 = (f32[8,128]{1,0:T(8,128)S(1)}, f32[8,128]{1,0:T(8,128)S(1)}, u32[]{:S(2)}, u32[]{:S(2)}) collective-permute-start(f32[8,128]{1,0:T(8,128)S(1)} %get-tuple-element.63), channel_id=1, source_target_pairs={{0,8},{1,9},{2,10},{3,11},{4,12},{5,13},{6,14},{7,15},{16,24},{17,... | collective-permute-start | bytes 12296 | tf_op jit(solution)/shard_map/ppermute | solution.py:239
  26.6 1.0 collective-permute-done.8.r_6_
  27.7 3.0 %forward3.1 = (f32[3,32,8,256]{3,2,1,0:T(8,128)S(1)}, f32[3,34,8,256]{3,2,1,0:T(8,128)S(1)}, f32[8,128]{1,0:T(8,128)S(1)}, f32[8,128]{1,0:T(8,128)S(1)}, f32[96,256]{1,0:T(8,128)S(1)}, /*index=5*/f32[96,256]{1,0:T(8,128)S(1)}) custom-call(s32[7]{0:T(128)S(1)} %stack.47.meta_ref.r_0_, f32[6,3,3,32,8,256]{5,4,3,2,1,0:T(8,128)S(1)} %bitcast.17, ...), custom_call_target="tpu_custom_call" | custom-call | tf_op jit(solution)/shard_map/forward3/pallas_call | solution.py:45
  30.7 1.3 %collective-permute-start.14 = (f32[96,256]{1,0:T(8,128)S(1)}, f32[96,256]{1,0:T(8,128)S(1)}, u32[]{:S(2)}, u32[]{:S(2)}) collective-permute-start(f32[96,256]{1,0:T(8,128)S(1)} %get-tuple-element.71), channel_id=1, source_target_pairs={{0,1},{8,9},{16,17},{24,25},{32,33},{40,41},{48,49},{56,57},{64,65... | collective-permute-start | bytes 294920 | tf_op jit(solution)/shard_map/ppermute | solution.py:240
  32.0 5.5 %collective-permute-start.12 = (f32[8,128]{1,0:T(8,128)S(1)}, f32[8,128]{1,0:T(8,128)S(1)}, u32[]{:S(2)}, u32[]{:S(2)}) collective-permute-start(f32[8,128]{1,0:T(8,128)S(1)} %get-tuple-element.69), channel_id=1, source_target_pairs={{0,8},{1,9},{2,10},{3,11},{4,12},{5,13},{6,14},{7,15},{16,24},{17,... | collective-permute-start | bytes 12296 | tf_op jit(solution)/shard_map/ppermute | solution.py:239
  37.5 1.0 collective-permute-done.12.r_6_
  38.6 3.0 %backward2.1 = (f32[3,34,8,256]{3,2,1,0:T(8,128)S(1)}, f32[8,128]{1,0:T(8,128)S(1)}, f32[8,128]{1,0:T(8,128)S(1)}, f32[96,256]{1,0:T(8,128)S(1)}, f32[96,256]{1,0:T(8,128)S(1)}) custom-call(s32[7]{0:T(128)S(1)} %stack.47.meta_ref.r_0_, f32[6,3,3,32,8,256]{5,4,3,2,1,0:T(8,128)S(1)} %bitcast.17, f32[3,3,32,8,256]{4,3,2,1,0:T(8,128)S(1)} %get-tuple-element.47.r_2_, ...), custom_call_target="tpu_custom_call" | custom-call | tf_op jit(solution)/shard_map/backward2/pallas_call | solution.py:45
  41.7 1.3 %collective-permute-start.18 = (f32[96,256]{1,0:T(8,128)S(1)}, f32[96,256]{1,0:T(8,128)S(1)}, u32[]{:S(2)}, u32[]{:S(2)}) collective-permute-start(f32[96,256]{1,0:T(8,128)S(1)} %get-tuple-element.76), channel_id=1, source_target_pairs={{0,1},{8,9},{16,17},{24,25},{32,33},{40,41},{48,49},{56,57},{64,65... | collective-permute-start | bytes 294920 | tf_op jit(solution)/shard_map/ppermute | solution.py:240
  42.9 5.5 %collective-permute-start.16 = (f32[8,128]{1,0:T(8,128)S(1)}, f32[8,128]{1,0:T(8,128)S(1)}, u32[]{:S(2)}, u32[]{:S(2)}) collective-permute-start(f32[8,128]{1,0:T(8,128)S(1)} %get-tuple-element.74), channel_id=1, source_target_pairs={{0,8},{1,9},{2,10},{3,11},{4,12},{5,13},{6,14},{7,15},{16,24},{17,... | collective-permute-start | bytes 12296 | tf_op jit(solution)/shard_map/ppermute | solution.py:239
  49.6 3.1 %backward1.1 = (f32[3,34,8,256]{3,2,1,0:T(8,128)S(1)}, f32[8,128]{1,0:T(8,128)S(1)}, f32[8,128]{1,0:T(8,128)S(1)}, f32[96,256]{1,0:T(8,128)S(1)}, f32[96,256]{1,0:T(8,128)S(1)}) custom-call(s32[7]{0:T(128)S(1)} %stack.47.meta_ref.r_0_, f32[6,3,3,32,8,256]{5,4,3,2,1,0:T(8,128)S(1)} %bitcast.17, f32[3,3,32,8,256]{4,3,2,1,0:T(8,128)S(1)} %get-tuple-element.47.r_2_, ...), custom_call_target="tpu_custom_call" | custom-call | tf_op jit(solution)/shard_map/backward1/pallas_call | solution.py:45
  52.7 1.3 %collective-permute-start.22 = (f32[96,256]{1,0:T(8,128)S(1)}, f32[96,256]{1,0:T(8,128)S(1)}, u32[]{:S(2)}, u32[]{:S(2)}) collective-permute-start(f32[96,256]{1,0:T(8,128)S(1)} %get-tuple-element.81), channel_id=1, source_target_pairs={{0,1},{8,9},{16,17},{24,25},{32,33},{40,41},{48,49},{56,57},{64,65... | collective-permute-start | bytes 294920 | tf_op jit(solution)/shard_map/ppermute | solution.py:240
  54.0 5.5 %collective-permute-start.20 = (f32[8,128]{1,0:T(8,128)S(1)}, f32[8,128]{1,0:T(8,128)S(1)}, u32[]{:S(2)}, u32[]{:S(2)}) collective-permute-start(f32[8,128]{1,0:T(8,128)S(1)} %get-tuple-element.79), channel_id=1, source_target_pairs={{0,8},{1,9},{2,10},{3,11},{4,12},{5,13},{6,14},{7,15},{16,24},{17,... | collective-permute-start | bytes 12296 | tf_op jit(solution)/shard_map/ppermute | solution.py:239
  59.5 1.3 %prep.1 = (bf16[1024,1024]{1,0:T(8,128)(2,1)S(1)}, bf16[256,1024]{1,0:T(8,128)(2,1)S(1)}, f32[16,128]{1,0:T(8,128)S(1)}, s32[1,1024]{1,0:T(1,128)S(1)}) custom-call(s32[7]{0:T(128)S(1)} %stack.47.meta_ref.r_0_, s32[64,128]{1,0:T(8,128)S(1)} %bitcast.24, s32[64,128]{1,0:T(8,128)S(1)} %bitcast.25, s32[1,1024]{1,0:T(1,128)S(1)} %bitcast.21, ...), custom_call_target="tpu_custom_call" | custom-call | tf_op jit(solution)/shard_map/prep/pallas_call | solution.py:45
  60.9 2.4 %backward0.1.s_ref = f32[3,32,8,256]{3,2,1,0:T(8,128)S(1)} custom-call(s32[7]{0:T(128)S(1)} %stack.47.meta_ref.r_0_, f32[6,3,3,32,8,256]{5,4,3,2,1,0:T(8,128)S(1)} %bitcast.17, f32[3,3,32,8,256]{4,3,2,1,0:T(8,128)S(1)} %get-tuple-element.47.r_2_, s32[32,8,256]{2,1,0:T(8,128)S(1)} %get-tuple-element.48.r_3_, f32[3,32,8,256]{3,2,1,0:T(8,128)S(1)} %get-tuple-element.67.r_4_, ...), custom_call_target="tpu_custom_call" | custom-call | tf_op jit(solution)/shard_map/backward0/pallas_call | solution.py:45
  63.4 1.9 %terms.1 = (f32[512,128]{1,0:T(8,128)S(1)}, f32[512,128]{1,0:T(8,128)S(1)}) custom-call(f32[3,32,8,256]{3,2,1,0:T(8,128)S(1)} %backward0.1.s_ref, bf16[256,1024]{1,0:T(8,128)(2,1)S(1)} %get-tuple-element.83.rt_ref, bf16[1024,1024]{1,0:T(8,128)(2,1)S(1)} %get-tuple-element.84.kh_ref, s32[1,1024]{1,0:T(1,128)S(1)} %get-tuple-element.85.lo_ref, ...), custom_call_target="tpu_custom_call" | custom-call | tf_op jit(solution)/shard_map/terms/pallas_call | solution.py:45
  66.2 1.2 %collective-permute-done.24 = f32[512,128]{1,0:T(8,128)S(1)} collective-permute-done((f32[512,128]{1,0:T(8,128)S(1)}, f32[512,128]{1,0:T(8,128)S(1)}, u32[]{:S(2)}, u32[]{:S(2)}) %collective-permute-start.24) | collective-permute-done | bytes 262176 | tf_op jit(solution)/shard_map/ppermute | solution.py:410
  67.4 23.9 %all_to_all.10.got_ref = f32[64,8,128]{2,1,0:T(8,128)S(1)} all-to-all(f32[64,8,128]{2,1,0:T(8,128)S(1)} %add_bitcast_fusion), channel_id=1, replica_groups={{0,2,4,6,8,10,12,14,16,18,20,22,24,26,28,30,32,34,36,38,40,42,44,46,48,..., dimensions={0} | all-to-all | bytes 524288 | tf_op jit(solution)/shard_map/all_to_all | solution.py:411
  91.6 13.8 %all_to_all.11 = f32[64,8,128]{2,1,0:T(8,128)S(1)} all-to-all(f32[64,8,128]{2,1,0:T(8,128)S(1)} %solve.1), channel_id=1, replica_groups={{0,2,4,6,8,10,12,14,16,18,20,22,24,26,28,30,32,34,36,38,40,42,44,46,48,..., dimensions={0} | all-to-all | bytes 524288 | tf_op jit(solution)/shard_map/all_to_all | solution.py:415
  105.3 3.0 %collective-permute-start.25 = (f32[512,128]{1,0:T(8,128)S(1)}, f32[512,128]{1,0:T(8,128)S(1)}, u32[]{:S(2)}, u32[]{:S(2)}) collective-permute-start(f32[512,128]{1,0:T(8,128)S(1)} %bitcast.18), channel_id=1, source_target_pairs={{0,1},{8,9},{16,17},{24,25},{32,33},{40,41},{48,49},{56,57},{64,65... | collective-permute-start | bytes 786440 | tf_op jit(solution)/shard_map/ppermute | solution.py:416
  108.4 1.2 %collective-permute-done.25.other_ref = f32[512,128]{1,0:T(8,128)S(1)} collective-permute-done((f32[512,128]{1,0:T(8,128)S(1)}, f32[512,128]{1,0:T(8,128)S(1)}, u32[]{:S(2)}, u32[]{:S(2)}) %collective-permute-start.25) | collective-permute-done | bytes 262176 | tf_op jit(solution)/shard_map/ppermute | solution.py:416
  109.5 2.7 %back.1 = f32[3,32,8,256]{3,2,1,0:T(8,128)} custom-call(f32[512,128]{1,0:T(8,128)S(1)} %bitcast.19, f32[512,128]{1,0:T(8,128)S(1)} %collective-permute-done.25.other_ref, f32[3,32,8,256]{3,2,1,0:T(8,128)S(1)} %backward0.1.s_ref, bf16[256,1024]{1,0:T(8,128)(2,1)S(1)} %get-tuple-element.83.rt_ref, bf16[1024,1024]{1,0:T(8,128)(2,1)S(1)} %get-tuple-element.84.kh_ref, ...), custom_call_target="tpu_custom_call" | custom-call | tf_op jit(solution)/shard_map/back/pallas_call | solution.py:417
  (60 shorter events, 4.2 us)
Async XLA Ops:
  3.2 5.6 %collective-permute-start.2 = (f32[96,256]{1,0:T(8,128)S(1)}, f32[96,256]{1,0:T(8,128)S(1)}, u32[]{:S(2)}, u32[]{:S(2)}) collective-permute-start(f32[96,256]{1,0:T(8,128)S(1)} %get-tuple-element.53), channel_id=1, source_target_pairs={{0,1},{8,9},{16,17},{24,25},{32,33},{40,41},{48,49},{56,57},{64,65... | collective-permute-start | bytes 294920 | tf_op jit(solution)/shard_map/ppermute | solution.py:240
  4.7 4.3 %collective-permute-start.3 = (f32[96,256]{1,0:T(8,128)S(1)}, f32[96,256]{1,0:T(8,128)S(1)}, u32[]{:S(2)}, u32[]{:S(2)}) collective-permute-start(f32[96,256]{1,0:T(8,128)S(1)} %get-tuple-element.54), channel_id=1, source_target_pairs={{1,2},{9,10},{17,18},{25,26},{33,34},{41,42},{49,50},{57,58},{65,6... | collective-permute-start | bytes 294920 | tf_op jit(solution)/shard_map/ppermute | solution.py:238
  6.0 2.8 %collective-permute-start = (f32[8,128]{1,0:T(8,128)S(1)}, f32[8,128]{1,0:T(8,128)S(1)}, u32[]{:S(2)}, u32[]{:S(2)}) collective-permute-start(f32[8,128]{1,0:T(8,128)S(1)} %get-tuple-element.51), channel_id=1, source_target_pairs={{0,8},{1,9},{2,10},{3,11},{4,12},{5,13},{6,14},{7,15},{16,24},{17,... | collective-permute-start | bytes 12296 | tf_op jit(solution)/shard_map/ppermute | solution.py:239
  7.3 1.5 %collective-permute-start.1 = (f32[8,128]{1,0:T(8,128)S(1)}, f32[8,128]{1,0:T(8,128)S(1)}, u32[]{:S(2)}, u32[]{:S(2)}) collective-permute-start(f32[8,128]{1,0:T(8,128)S(1)} %get-tuple-element.52), channel_id=1, source_target_pairs={{8,16},{9,17},{10,18},{11,19},{12,20},{13,21},{14,22},{15,23},{24,... | collective-permute-start | bytes 12296 | tf_op jit(solution)/shard_map/ppermute | solution.py:237
  12.1 4.8 %collective-permute-start.6 = (f32[96,256]{1,0:T(8,128)S(1)}, f32[96,256]{1,0:T(8,128)S(1)}, u32[]{:S(2)}, u32[]{:S(2)}) collective-permute-start(f32[96,256]{1,0:T(8,128)S(1)} %get-tuple-element.59), channel_id=1, source_target_pairs={{0,1},{8,9},{16,17},{24,25},{32,33},{40,41},{48,49},{56,57},{64,65... | collective-permute-start | bytes 294920 | tf_op jit(solution)/shard_map/ppermute | solution.py:240
  13.3 4.3 %collective-permute-start.7 = (f32[96,256]{1,0:T(8,128)S(1)}, f32[96,256]{1,0:T(8,128)S(1)}, u32[]{:S(2)}, u32[]{:S(2)}) collective-permute-start(f32[96,256]{1,0:T(8,128)S(1)} %get-tuple-element.60), channel_id=1, source_target_pairs={{1,2},{9,10},{17,18},{25,26},{33,34},{41,42},{49,50},{57,58},{65,6... | collective-permute-start | bytes 294920 | tf_op jit(solution)/shard_map/ppermute | solution.py:238
  13.6 3.3 %collective-permute-start.4 = (f32[8,128]{1,0:T(8,128)S(1)}, f32[8,128]{1,0:T(8,128)S(1)}, u32[]{:S(2)}, u32[]{:S(2)}) collective-permute-start(f32[8,128]{1,0:T(8,128)S(1)} %get-tuple-element.57), channel_id=1, source_target_pairs={{0,8},{1,9},{2,10},{3,11},{4,12},{5,13},{6,14},{7,15},{16,24},{17,... | collective-permute-start | bytes 12296 | tf_op jit(solution)/shard_map/ppermute | solution.py:239
  15.6 1.3 %collective-permute-start.5 = (f32[8,128]{1,0:T(8,128)S(1)}, f32[8,128]{1,0:T(8,128)S(1)}, u32[]{:S(2)}, u32[]{:S(2)}) collective-permute-start(f32[8,128]{1,0:T(8,128)S(1)} %get-tuple-element.58), channel_id=1, source_target_pairs={{8,16},{9,17},{10,18},{11,19},{12,20},{13,21},{14,22},{15,23},{24,... | collective-permute-start | bytes 12296 | tf_op jit(solution)/shard_map/ppermute | solution.py:237
  20.7 7.1 %collective-permute-start.10 = (f32[96,256]{1,0:T(8,128)S(1)}, f32[96,256]{1,0:T(8,128)S(1)}, u32[]{:S(2)}, u32[]{:S(2)}) collective-permute-start(f32[96,256]{1,0:T(8,128)S(1)} %get-tuple-element.65), channel_id=1, source_target_pairs={{0,1},{8,9},{16,17},{24,25},{32,33},{40,41},{48,49},{56,57},{64,65... | collective-permute-start | bytes 294920 | tf_op jit(solution)/shard_map/ppermute | solution.py:240
  22.2 5.6 %collective-permute-start.11 = (f32[96,256]{1,0:T(8,128)S(1)}, f32[96,256]{1,0:T(8,128)S(1)}, u32[]{:S(2)}, u32[]{:S(2)}) collective-permute-start(f32[96,256]{1,0:T(8,128)S(1)} %get-tuple-element.66), channel_id=1, source_target_pairs={{1,2},{9,10},{17,18},{25,26},{33,34},{41,42},{49,50},{57,58},{65,6... | collective-permute-start | bytes 294920 | tf_op jit(solution)/shard_map/ppermute | solution.py:238
  22.2 5.4 %collective-permute-start.8 = (f32[8,128]{1,0:T(8,128)S(1)}, f32[8,128]{1,0:T(8,128)S(1)}, u32[]{:S(2)}, u32[]{:S(2)}) collective-permute-start(f32[8,128]{1,0:T(8,128)S(1)} %get-tuple-element.63), channel_id=1, source_target_pairs={{0,8},{1,9},{2,10},{3,11},{4,12},{5,13},{6,14},{7,15},{16,24},{17,... | collective-permute-start | bytes 12296 | tf_op jit(solution)/shard_map/ppermute | solution.py:239
  26.6 1.2 %collective-permute-start.9 = (f32[8,128]{1,0:T(8,128)S(1)}, f32[8,128]{1,0:T(8,128)S(1)}, u32[]{:S(2)}, u32[]{:S(2)}) collective-permute-start(f32[8,128]{1,0:T(8,128)S(1)} %get-tuple-element.64), channel_id=1, source_target_pairs={{8,16},{9,17},{10,18},{11,19},{12,20},{13,21},{14,22},{15,23},{24,... | collective-permute-start | bytes 12296 | tf_op jit(solution)/shard_map/ppermute | solution.py:237
  30.7 7.9 %collective-permute-start.14 = (f32[96,256]{1,0:T(8,128)S(1)}, f32[96,256]{1,0:T(8,128)S(1)}, u32[]{:S(2)}, u32[]{:S(2)}) collective-permute-start(f32[96,256]{1,0:T(8,128)S(1)} %get-tuple-element.71), channel_id=1, source_target_pairs={{0,1},{8,9},{16,17},{24,25},{32,33},{40,41},{48,49},{56,57},{64,65... | collective-permute-start | bytes 294920 | tf_op jit(solution)/shard_map/ppermute | solution.py:240
  32.0 6.7 %collective-permute-start.15 = (f32[96,256]{1,0:T(8,128)S(1)}, f32[96,256]{1,0:T(8,128)S(1)}, u32[]{:S(2)}, u32[]{:S(2)}) collective-permute-start(f32[96,256]{1,0:T(8,128)S(1)} %get-tuple-element.72), channel_id=1, source_target_pairs={{1,2},{9,10},{17,18},{25,26},{33,34},{41,42},{49,50},{57,58},{65,6... | collective-permute-start | bytes 294920 | tf_op jit(solution)/shard_map/ppermute | solution.py:238
  32.0 6.5 %collective-permute-start.12 = (f32[8,128]{1,0:T(8,128)S(1)}, f32[8,128]{1,0:T(8,128)S(1)}, u32[]{:S(2)}, u32[]{:S(2)}) collective-permute-start(f32[8,128]{1,0:T(8,128)S(1)} %get-tuple-element.69), channel_id=1, source_target_pairs={{0,8},{1,9},{2,10},{3,11},{4,12},{5,13},{6,14},{7,15},{16,24},{17,... | collective-permute-start | bytes 12296 | tf_op jit(solution)/shard_map/ppermute | solution.py:239
  37.5 1.2 %collective-permute-start.13 = (f32[8,128]{1,0:T(8,128)S(1)}, f32[8,128]{1,0:T(8,128)S(1)}, u32[]{:S(2)}, u32[]{:S(2)}) collective-permute-start(f32[8,128]{1,0:T(8,128)S(1)} %get-tuple-element.70), channel_id=1, source_target_pairs={{8,16},{9,17},{10,18},{11,19},{12,20},{13,21},{14,22},{15,23},{24,... | collective-permute-start | bytes 12296 | tf_op jit(solution)/shard_map/ppermute | solution.py:237
  41.7 7.9 %collective-permute-start.18 = (f32[96,256]{1,0:T(8,128)S(1)}, f32[96,256]{1,0:T(8,128)S(1)}, u32[]{:S(2)}, u32[]{:S(2)}) collective-permute-start(f32[96,256]{1,0:T(8,128)S(1)} %get-tuple-element.76), channel_id=1, source_target_pairs={{0,1},{8,9},{16,17},{24,25},{32,33},{40,41},{48,49},{56,57},{64,65... | collective-permute-start | bytes 294920 | tf_op jit(solution)/shard_map/ppermute | solution.py:240
  42.9 6.7 %collective-permute-start.19 = (f32[96,256]{1,0:T(8,128)S(1)}, f32[96,256]{1,0:T(8,128)S(1)}, u32[]{:S(2)}, u32[]{:S(2)}) collective-permute-start(f32[96,256]{1,0:T(8,128)S(1)} %get-tuple-element.77), channel_id=1, source_target_pairs={{1,2},{9,10},{17,18},{25,26},{33,34},{41,42},{49,50},{57,58},{65,6... | collective-permute-start | bytes 294920 | tf_op jit(solution)/shard_map/ppermute | solution.py:238
  42.9 6.5 %collective-permute-start.16 = (f32[8,128]{1,0:T(8,128)S(1)}, f32[8,128]{1,0:T(8,128)S(1)}, u32[]{:S(2)}, u32[]{:S(2)}) collective-permute-start(f32[8,128]{1,0:T(8,128)S(1)} %get-tuple-element.74), channel_id=1, source_target_pairs={{0,8},{1,9},{2,10},{3,11},{4,12},{5,13},{6,14},{7,15},{16,24},{17,... | collective-permute-start | bytes 12296 | tf_op jit(solution)/shard_map/ppermute | solution.py:239
  48.4 1.2 %collective-permute-start.17 = (f32[8,128]{1,0:T(8,128)S(1)}, f32[8,128]{1,0:T(8,128)S(1)}, u32[]{:S(2)}, u32[]{:S(2)}) collective-permute-start(f32[8,128]{1,0:T(8,128)S(1)} %get-tuple-element.75), channel_id=1, source_target_pairs={{8,16},{9,17},{10,18},{11,19},{12,20},{13,21},{14,22},{15,23},{24,... | collective-permute-start | bytes 12296 | tf_op jit(solution)/shard_map/ppermute | solution.py:237
  49.6 9.9 %copy-start.1 = (s32[1024]{0:T(1024)S(1)}, s32[1024]{0:T(1024)}, u32[]{:S(2)}) copy-start(s32[1024]{0:T(1024)} %param.16) | copy-start | bytes 12292
  49.6 9.9 %copy-start.2 = (s32[8192]{0:T(1024)S(1)}, s32[8192]{0:T(1024)}, u32[]{:S(2)}) copy-start(s32[8192]{0:T(1024)} %param.21) | copy-start | bytes 98308
  49.6 9.9 %copy-start.3 = (s32[8192]{0:T(1024)S(1)}, s32[8192]{0:T(1024)}, u32[]{:S(2)}) copy-start(s32[8192]{0:T(1024)} %param.22) | copy-start | bytes 98308
  49.6 9.9 %copy-start.6 = (s32[1024]{0:T(1024)S(1)}, s32[1024]{0:T(1024)}, u32[]{:S(2)}) copy-start(s32[1024]{0:T(1024)} %param.17) | copy-start | bytes 12292
  52.7 8.2 %collective-permute-start.22 = (f32[96,256]{1,0:T(8,128)S(1)}, f32[96,256]{1,0:T(8,128)S(1)}, u32[]{:S(2)}, u32[]{:S(2)}) collective-permute-start(f32[96,256]{1,0:T(8,128)S(1)} %get-tuple-element.81), channel_id=1, source_target_pairs={{0,1},{8,9},{16,17},{24,25},{32,33},{40,41},{48,49},{56,57},{64,65... | collective-permute-start | bytes 294920 | tf_op jit(solution)/shard_map/ppermute | solution.py:240
  54.0 6.9 %collective-permute-start.23 = (f32[96,256]{1,0:T(8,128)S(1)}, f32[96,256]{1,0:T(8,128)S(1)}, u32[]{:S(2)}, u32[]{:S(2)}) collective-permute-start(f32[96,256]{1,0:T(8,128)S(1)} %get-tuple-element.82), channel_id=1, source_target_pairs={{1,2},{9,10},{17,18},{25,26},{33,34},{41,42},{49,50},{57,58},{65,6... | collective-permute-start | bytes 294920 | tf_op jit(solution)/shard_map/ppermute | solution.py:238
  54.0 6.9 %collective-permute-start.20 = (f32[8,128]{1,0:T(8,128)S(1)}, f32[8,128]{1,0:T(8,128)S(1)}, u32[]{:S(2)}, u32[]{:S(2)}) collective-permute-start(f32[8,128]{1,0:T(8,128)S(1)} %get-tuple-element.79), channel_id=1, source_target_pairs={{0,8},{1,9},{2,10},{3,11},{4,12},{5,13},{6,14},{7,15},{16,24},{17,... | collective-permute-start | bytes 12296 | tf_op jit(solution)/shard_map/ppermute | solution.py:239
  59.4 1.4 %collective-permute-start.21 = (f32[8,128]{1,0:T(8,128)S(1)}, f32[8,128]{1,0:T(8,128)S(1)}, u32[]{:S(2)}, u32[]{:S(2)}) collective-permute-start(f32[8,128]{1,0:T(8,128)S(1)} %get-tuple-element.80), channel_id=1, source_target_pairs={{8,16},{9,17},{10,18},{11,19},{12,20},{13,21},{14,22},{15,23},{24,... | collective-permute-start | bytes 12296 | tf_op jit(solution)/shard_map/ppermute | solution.py:237
  63.3 28.0 %copy-start = (f32[64,16,16]{0,2,1:T(8,128)S(1)}, f32[64,16,16]{0,2,1:T(8,128)}, u32[]{:S(2)}) copy-start(f32[64,16,16]{0,2,1:T(8,128)} %param.23) | copy-start | bytes 196612
  63.3 46.2 %copy-start.5 = (f32[3,1024]{1,0:T(4,128)S(1)}, f32[3,1024]{1,0:T(4,128)}, u32[]{:S(2)}) copy-start(f32[3,1024]{1,0:T(4,128)} %back_ref.1) | copy-start | bytes 36868
  65.2 2.2 %collective-permute-start.24 = (f32[512,128]{1,0:T(8,128)S(1)}, f32[512,128]{1,0:T(8,128)S(1)}, u32[]{:S(2)}, u32[]{:S(2)}) collective-permute-start(f32[512,128]{1,0:T(8,128)S(1)} %get-tuple-element.87), channel_id=1, source_target_pairs={{0,1},{8,9},{16,17},{24,25},{32,33},{40,41},{48,49},{56,57},{64,65... | collective-permute-start | bytes 786440 | tf_op jit(solution)/shard_map/ppermute | solution.py:410
  105.3 4.2 %collective-permute-start.25 = (f32[512,128]{1,0:T(8,128)S(1)}, f32[512,128]{1,0:T(8,128)S(1)}, u32[]{:S(2)}, u32[]{:S(2)}) collective-permute-start(f32[512,128]{1,0:T(8,128)S(1)} %bitcast.18), channel_id=1, source_target_pairs={{0,1},{8,9},{16,17},{24,25},{32,33},{40,41},{48,49},{56,57},{64,65... | collective-permute-start | bytes 786440 | tf_op jit(solution)/shard_map/ppermute | solution.py:416
  (6 other events, 48.0 us)

commit v5 on v4

--- a/solution.py
+++ b/solution.py
@@ -55,27 +55,28 @@
     )(*args)
 
 
-def emit_edges(new, z, nz, edges, ylo_ref, yhi_ref):
-    xlo, xhi = edges
-    lane = iota((8, 128), 1)
-    for j in range(3):
-        at = j * nz + z
-        xlo = jnp.where(lane == at, pltpu.roll(new[j][:, :128], at, 1), xlo)
-        xhi = jnp.where(lane == at, pltpu.roll(new[j][:, -128:], (at + 1) % 128, 1), xhi)
-        ylo_ref[pl.ds(at, 1), :] = new[j][0:1, :]
-        yhi_ref[pl.ds(at, 1), :] = new[j][-1:, :]
-    return xlo, xhi
-
-
-def store_edges(meta_ref, columns, ylo_ref, yhi_ref, xa_ref, xb_ref, ya_ref, yb_ref):
+def emit_edges(meta_ref, v_ref, xa_ref, xb_ref, ya_ref, yb_ref):
+    _, layers, ny, nx = v_ref.shape
+    nz = layers - 2
     x_odd = meta_ref[5] > 0
     y_odd = meta_ref[6] > 0
-    xlo, xhi = columns
+    lane = iota((ny, 128), 1)
+    low_x = [jnp.zeros((ny, 128), F32)] * 4
+    high_x = [jnp.zeros((ny, 128), F32)] * 4
+    for j in range(3):
+        low = jnp.concatenate([v_ref[j, z + 1, 0:1, :] for z in range(nz)], axis=0)
+        high = jnp.concatenate([v_ref[j, z + 1, ny - 1 : ny, :] for z in range(nz)], axis=0)
+        ya_ref[j * nz : (j + 1) * nz, :] = jnp.where(y_odd, low, high)
+        yb_ref[j * nz : (j + 1) * nz, :] = jnp.where(y_odd, high, low)
+        for z in range(nz):
+            to = j * nz + z
+            here = lane == to
+            k = z % 4
+            low_x[k] = jnp.where(here, pltpu.roll(v_ref[j, z + 1, :, :128], to, 1), low_x[k])
+            high_x[k] = jnp.where(here, pltpu.roll(v_ref[j, z + 1, :, nx - 128 :], (to + 1) % 128, 1), high_x[k])
+    xlo, xhi = sum(low_x), sum(high_x)
     xa_ref[...] = jnp.where(x_odd, xlo, xhi)
     xb_ref[...] = jnp.where(x_odd, xhi, xlo)
-    ylo, yhi = ylo_ref[...], yhi_ref[...]
-    ya_ref[...] = jnp.where(y_odd, ylo, yhi)
-    yb_ref[...] = jnp.where(y_odd, yhi, ylo)
 
 
 def zero_ends(ref, nz):
@@ -93,7 +94,7 @@
     return out
 
 
-def first_body(meta_ref, rhs_hbm, piv_hbm, col_hbm, rhs_ref, piv_ref, col_ref, v_ref, xa_ref, xb_ref, ya_ref, yb_ref, ylo_ref, yhi_ref, sems):
+def first_body(meta_ref, rhs_hbm, piv_hbm, col_hbm, rhs_ref, piv_ref, col_ref, v_ref, xa_ref, xb_ref, ya_ref, yb_ref, sems):
     nz = rhs_ref.shape[1]
     size = nz // PARTS
     pairs = [(rhs_hbm, rhs_ref), (piv_hbm, piv_ref), (col_hbm, col_ref)]
@@ -102,25 +103,22 @@
             c.start()
     zero_ends(v_ref, nz)
 
-    def step(z, edges):
+    def step(z, carry):
         rhs = [rhs_ref[j, z] for j in range(3)]
         chosen = col_ref[z] == 0
-        new = []
         for i in range(3):
             p = piv_ref[i, 0, z] * rhs[0] + piv_ref[i, 1, z] * rhs[1] + piv_ref[i, 2, z] * rhs[2]
             p = jnp.where(chosen, p, 0.0)
             v_ref[i, z + 1] = p
-            new.append(p)
-        return emit_edges(new, z, nz, edges, ylo_ref, yhi_ref)
-
-    def block(part, edges):
+        return carry
+
+    def block(part, carry):
         for c in chunk_copies(pairs, sems, part, size, (1, 2, 0)):
             c.wait()
-        return lax.fori_loop(0, size, lambda k, e: step(part * size + k, e), edges, unroll=UNROLL)
-
-    zero = jnp.zeros((8, 128), F32)
-    edges = lax.fori_loop(0, PARTS, block, (zero, zero))
-    store_edges(meta_ref, edges, ylo_ref, yhi_ref, xa_ref, xb_ref, ya_ref, yb_ref)
+        return lax.fori_loop(0, size, lambda k, e: step(part * size + k, e), carry, unroll=UNROLL)
+
+    lax.fori_loop(0, PARTS, block, 0)
+    emit_edges(meta_ref, v_ref, xa_ref, xb_ref, ya_ref, yb_ref)
 
 
 def turn_body(colour, forward, final, load, *refs):
@@ -131,7 +129,7 @@
         prep_in, refs = refs[:5], refs[5:]
         coup_hbm, coup_ref = coup_ref, refs.pop(0)
         prep_out, refs = refs[:4], refs[4:]
-    refs, (hylo_ref, hyhi_ref, ylo_ref, yhi_ref) = refs[:-4], refs[-4:]
+    refs, (hylo_ref, hyhi_ref) = refs[:-2], refs[-2:]
     u_ref = refs.pop(0) if forward else None
     nv_ref, *edge_refs = refs
     nz = base_ref.shape[1]
@@ -159,7 +157,7 @@
     if not final:
         zero_ends(nv_ref, nz)
 
-    def step(z, edges):
+    def step(z, carry):
         cur = [base_ref[j, z] for j in range(3)]
         base = list(cur)
         old = []
@@ -183,7 +181,6 @@
                 t = t + (coup_ref[4, i, j, z] * zm + coup_ref[5, i, j, z] * zp)
                 cur[i] = cur[i] - t
         chosen = col_ref[z] == colour
-        new = []
         for i in range(3):
             p = piv_ref[i, 0, z] * cur[0] + piv_ref[i, 1, z] * cur[1] + piv_ref[i, 2, z] * cur[2]
             if forward:
@@ -196,23 +193,19 @@
                 nv_ref[i, z] = p
             else:
                 nv_ref[i, z + 1] = p
-            new.append(p)
-        if final:
-            return edges
-        return emit_edges(new, z, nz, edges, ylo_ref, yhi_ref)
-
-    def block(part, edges):
+        return carry
+
+    def block(part, carry):
         for c in chunk_copies(pairs, sems, part, size, (3,)):
             c.wait()
-        return lax.fori_loop(0, size, lambda k, e: step(part * size + k, e), edges, unroll=UNROLL)
-
-    zero = jnp.zeros((ny, 128), F32)
+        return lax.fori_loop(0, size, lambda k, e: step(part * size + k, e), carry, unroll=UNROLL)
+
     if load:
-        edges = lax.fori_loop(0, PARTS, block, (zero, zero))
+        lax.fori_loop(0, PARTS, block, 0)
     else:
-        edges = lax.fori_loop(0, nz, step, (zero, zero), unroll=UNROLL)
+        lax.fori_loop(0, nz, step, 0, unroll=UNROLL)
     if not final:
-        store_edges(meta_ref, edges, ylo_ref, yhi_ref, *edge_refs)
+        emit_edges(meta_ref, nv_ref, *edge_refs)
 
 
 def both_ways(pairs):
@@ -353,7 +346,7 @@
     edges = [((ny, 128), F32)] * 2 + [((3 * nz, nx), F32)] * 2
     n = perf_cells.shape[0]
     cells = perf_cells.reshape(1, n)
-    rows = [pltpu.VMEM((3 * nz, nx), F32)] * 4
+    rows = [pltpu.VMEM((3 * nz, nx), F32)] * 2
     prep_ins = [
         well_slot.reshape(-1, 128),
         seg_count.reshape(-1, 128),
@@ -369,7 +362,7 @@
         [meta, rhs, pivots, colours],
         smem=1,
         hbm=(1, 2, 3),
-        scratch=rows[:2] + [pltpu.SemaphoreType.DMA((3, PARTS))],
+        scratch=[pltpu.SemaphoreType.DMA((3, PARTS))],
         name="first",
         cost=pl.CostEstimate(flops=10**10, transcendentals=0, bytes_accessed=10**8),
     )

time: 112 us -> 111 us (level)
  Pallas kernels: 26.8 us -> 25.2 us
    pallas_call x10, Pallas kernels: 24.2 us -> 22.5 us  [call(): pl.pallas_call(body, out_shape=tuple((pltpu.VMEM(s, d) for s, d in outs))...]
where the time goes in v5:
time: 111 us
  starting transfers between devices  37.7 us (34%)
  blocking collectives  37.7 us (34%)
  Pallas kernels  25.2 us (23%)
  waiting for transfers between devices  9.59 us (9%)
    ppermute x6, starting transfers between devices, halos(): hxa = lax.ppermute(xa, axes, x_even)  24.1 us
    all_to_all x1, blocking collectives, shards(): lax.all_to_all(mine.reshape(64, 8, 128), axes, 0, 0, axis_index_groups=co...  23.9 us
    pallas_call x10, Pallas kernels, call(): pl.pallas_call(body, out_shape=tuple((pltpu.VMEM(s, d) for s, d in outs))...  22.5 us
    all_to_all x1, blocking collectives, shards(): lax.all_to_all(values, axes, 0, 0, axis_index_groups=cores, tiled=True)  13.8 us
    ppermute x6, starting transfers between devices, halos(): hya = lax.ppermute(ya, axes, y_even)  7.86 us
    ppermute x6, waiting for transfers between devices, halos(): hxa = lax.ppermute(xa, axes, x_even)  5.8 us
    ppermute x1, starting transfers between devices, shards(): other = lax.ppermute(mine, axes, pairs)  3.04 us
    pallas_call x1, Pallas kernels, shards(): pl.pallas_call(return_body, out_shape=jax.ShapeDtypeStruct(plain[0], F32)...  2.69 us
  transfers between devices with their start and end apart: 26, of which 12 were waited for; matrix products, arithmetic and copies ran while one was open for 0% of the time, Pallas kernels for 1%

profile of v5, /device:TPU:1, one launch (start us, length us, event | category | flops | bytes accessed | tf_op | source)
XLA Modules:
  0.0 110.6 jit_solution(17943628539730491177)
XLA Ops:
  0.1 3.2 %first.1 = (f32[3,32,8,256]{3,2,1,0:T(8,128)S(1)}, f32[3,3,32,8,256]{4,3,2,1,0:T(8,128)S(1)}, s32[32,8,256]{2,1,0:T(8,128)S(1)}, f32[3,34,8,256]{3,2,1,0:T(8,128...) custom-call(s32[7]{0:T(128)S(1)} %stack.47.meta_ref.r_0_, ...), custom_call_target="tpu_custom_call" | custom-call | flops 10000000000 | bytes 100000000 | tf_op jit(solution)/shard_map/first/pallas_call | solution.py:45
  3.3 1.5 %collective-permute-start.2 = (f32[96,256]{1,0:T(8,128)S(1)}, f32[96,256]{1,0:T(8,128)S(1)}, u32[]{:S(2)}, u32[]{:S(2)}) collective-permute-start(f32[96,256]{1,0:T(8,128)S(1)} %get-tuple-element.53), channel_id=1, source_target_pairs={{0,1},{8,9},{16,17},{24,25},{32,33},{40,41},{48,49},{56,57},{64,65... | collective-permute-start | bytes 294920 | tf_op jit(solution)/shard_map/ppermute | solution.py:233
  4.8 1.3 %collective-permute-start.3 = (f32[96,256]{1,0:T(8,128)S(1)}, f32[96,256]{1,0:T(8,128)S(1)}, u32[]{:S(2)}, u32[]{:S(2)}) collective-permute-start(f32[96,256]{1,0:T(8,128)S(1)} %get-tuple-element.54), channel_id=1, source_target_pairs={{1,2},{9,10},{17,18},{25,26},{33,34},{41,42},{49,50},{57,58},{65,6... | collective-permute-start | bytes 294920 | tf_op jit(solution)/shard_map/ppermute | solution.py:231
  6.1 1.3 %collective-permute-start = (f32[8,128]{1,0:T(8,128)S(1)}, f32[8,128]{1,0:T(8,128)S(1)}, u32[]{:S(2)}, u32[]{:S(2)}) collective-permute-start(f32[8,128]{1,0:T(8,128)S(1)} %get-tuple-element.51), channel_id=1, source_target_pairs={{0,8},{1,9},{2,10},{3,11},{4,12},{5,13},{6,14},{7,15},{16,24},{17,... | collective-permute-start | bytes 12296 | tf_op jit(solution)/shard_map/ppermute | solution.py:232
  7.4 1.5 %collective-permute-done.r_6_ = f32[8,128]{1,0:T(8,128)S(1)} collective-permute-done((f32[8,128]{1,0:T(8,128)S(1)}, f32[8,128]{1,0:T(8,128)S(1)}, u32[]{:S(2)}, u32[]{:S(2)}) %collective-permute-start) | collective-permute-done | bytes 4128 | tf_op jit(solution)/shard_map/ppermute | solution.py:232
  9.1 2.7 %forward1.1 = (f32[3,32,8,256]{3,2,1,0:T(8,128)S(1)}, f32[3,34,8,256]{3,2,1,0:T(8,128)S(1)}, f32[8,128]{1,0:T(8,128)S(1)}, f32[8,128]{1,0:T(8,128)S(1)}, f32[96,256]{1,0:T(8,128)S(1)}, /*index=5*/f32[96,256]{1,0:T(8,128)S(1)}) custom-call(s32[7]{0:T(128)S(1)} %stack.47.meta_ref.r_0_, f32[6,3,3,32,8,256]{5,4,3,2,1,0:T(8,128)S(1)} %bitcast.17, ...), custom_call_target="tpu_custom_call" | custom-call | tf_op jit(solution)/shard_map/forward1/pallas_call | solution.py:45
  11.8 1.2 %collective-permute-start.6 = (f32[96,256]{1,0:T(8,128)S(1)}, f32[96,256]{1,0:T(8,128)S(1)}, u32[]{:S(2)}, u32[]{:S(2)}) collective-permute-start(f32[96,256]{1,0:T(8,128)S(1)} %get-tuple-element.59), channel_id=1, source_target_pairs={{0,1},{8,9},{16,17},{24,25},{32,33},{40,41},{48,49},{56,57},{64,65... | collective-permute-start | bytes 294920 | tf_op jit(solution)/shard_map/ppermute | solution.py:233
  13.3 2.0 %collective-permute-start.4 = (f32[8,128]{1,0:T(8,128)S(1)}, f32[8,128]{1,0:T(8,128)S(1)}, u32[]{:S(2)}, u32[]{:S(2)}) collective-permute-start(f32[8,128]{1,0:T(8,128)S(1)} %get-tuple-element.57), channel_id=1, source_target_pairs={{0,8},{1,9},{2,10},{3,11},{4,12},{5,13},{6,14},{7,15},{16,24},{17,... | collective-permute-start | bytes 12296 | tf_op jit(solution)/shard_map/ppermute | solution.py:232
  15.3 1.3 %collective-permute-done.4.r_6_ = f32[8,128]{1,0:T(8,128)S(1)} collective-permute-done((f32[8,128]{1,0:T(8,128)S(1)}, f32[8,128]{1,0:T(8,128)S(1)}, u32[]{:S(2)}, u32[]{:S(2)}) %collective-permute-start.4) | collective-permute-done | bytes 4128 | tf_op jit(solution)/shard_map/ppermute | solution.py:232
  17.3 2.7 %forward2.1 = (f32[3,32,8,256]{3,2,1,0:T(8,128)S(1)}, f32[3,34,8,256]{3,2,1,0:T(8,128)S(1)}, f32[8,128]{1,0:T(8,128)S(1)}, f32[8,128]{1,0:T(8,128)S(1)}, f32[96,256]{1,0:T(8,128)S(1)}, /*index=5*/f32[96,256]{1,0:T(8,128)S(1)}) custom-call(s32[7]{0:T(128)S(1)} %stack.47.meta_ref.r_0_, f32[6,3,3,32,8,256]{5,4,3,2,1,0:T(8,128)S(1)} %bitcast.17, ...), custom_call_target="tpu_custom_call" | custom-call | tf_op jit(solution)/shard_map/forward2/pallas_call | solution.py:45
  20.1 1.5 %collective-permute-start.10 = (f32[96,256]{1,0:T(8,128)S(1)}, f32[96,256]{1,0:T(8,128)S(1)}, u32[]{:S(2)}, u32[]{:S(2)}) collective-permute-start(f32[96,256]{1,0:T(8,128)S(1)} %get-tuple-element.65), channel_id=1, source_target_pairs={{0,1},{8,9},{16,17},{24,25},{32,33},{40,41},{48,49},{56,57},{64,65... | collective-permute-start | bytes 294920 | tf_op jit(solution)/shard_map/ppermute | solution.py:233
  21.6 4.4 %collective-permute-start.8 = (f32[8,128]{1,0:T(8,128)S(1)}, f32[8,128]{1,0:T(8,128)S(1)}, u32[]{:S(2)}, u32[]{:S(2)}) collective-permute-start(f32[8,128]{1,0:T(8,128)S(1)} %get-tuple-element.63), channel_id=1, source_target_pairs={{0,8},{1,9},{2,10},{3,11},{4,12},{5,13},{6,14},{7,15},{16,24},{17,... | collective-permute-start | bytes 12296 | tf_op jit(solution)/shard_map/ppermute | solution.py:232
  26.0 1.0 collective-permute-done.8.r_6_
  27.1 2.6 %forward3.1 = (f32[3,32,8,256]{3,2,1,0:T(8,128)S(1)}, f32[3,34,8,256]{3,2,1,0:T(8,128)S(1)}, f32[8,128]{1,0:T(8,128)S(1)}, f32[8,128]{1,0:T(8,128)S(1)}, f32[96,256]{1,0:T(8,128)S(1)}, /*index=5*/f32[96,256]{1,0:T(8,128)S(1)}) custom-call(s32[7]{0:T(128)S(1)} %stack.47.meta_ref.r_0_, f32[6,3,3,32,8,256]{5,4,3,2,1,0:T(8,128)S(1)} %bitcast.17, ...), custom_call_target="tpu_custom_call" | custom-call | tf_op jit(solution)/shard_map/forward3/pallas_call | solution.py:45
  29.8 1.3 %collective-permute-start.14 = (f32[96,256]{1,0:T(8,128)S(1)}, f32[96,256]{1,0:T(8,128)S(1)}, u32[]{:S(2)}, u32[]{:S(2)}) collective-permute-start(f32[96,256]{1,0:T(8,128)S(1)} %get-tuple-element.71), channel_id=1, source_target_pairs={{0,1},{8,9},{16,17},{24,25},{32,33},{40,41},{48,49},{56,57},{64,65... | collective-permute-start | bytes 294920 | tf_op jit(solution)/shard_map/ppermute | solution.py:233
  31.0 5.5 %collective-permute-start.12 = (f32[8,128]{1,0:T(8,128)S(1)}, f32[8,128]{1,0:T(8,128)S(1)}, u32[]{:S(2)}, u32[]{:S(2)}) collective-permute-start(f32[8,128]{1,0:T(8,128)S(1)} %get-tuple-element.69), channel_id=1, source_target_pairs={{0,8},{1,9},{2,10},{3,11},{4,12},{5,13},{6,14},{7,15},{16,24},{17,... | collective-permute-start | bytes 12296 | tf_op jit(solution)/shard_map/ppermute | solution.py:232
  37.7 2.7 %backward2.1 = (f32[3,34,8,256]{3,2,1,0:T(8,128)S(1)}, f32[8,128]{1,0:T(8,128)S(1)}, f32[8,128]{1,0:T(8,128)S(1)}, f32[96,256]{1,0:T(8,128)S(1)}, f32[96,256]{1,0:T(8,128)S(1)}) custom-call(s32[7]{0:T(128)S(1)} %stack.47.meta_ref.r_0_, f32[6,3,3,32,8,256]{5,4,3,2,1,0:T(8,128)S(1)} %bitcast.17, f32[3,3,32,8,256]{4,3,2,1,0:T(8,128)S(1)} %get-tuple-element.47.r_2_, ...), custom_call_target="tpu_custom_call" | custom-call | tf_op jit(solution)/shard_map/backward2/pallas_call | solution.py:45
  40.4 1.3 %collective-permute-start.18 = (f32[96,256]{1,0:T(8,128)S(1)}, f32[96,256]{1,0:T(8,128)S(1)}, u32[]{:S(2)}, u32[]{:S(2)}) collective-permute-start(f32[96,256]{1,0:T(8,128)S(1)} %get-tuple-element.76), channel_id=1, source_target_pairs={{0,1},{8,9},{16,17},{24,25},{32,33},{40,41},{48,49},{56,57},{64,65... | collective-permute-start | bytes 294920 | tf_op jit(solution)/shard_map/ppermute | solution.py:233
  41.7 5.5 %collective-permute-start.16 = (f32[8,128]{1,0:T(8,128)S(1)}, f32[8,128]{1,0:T(8,128)S(1)}, u32[]{:S(2)}, u32[]{:S(2)}) collective-permute-start(f32[8,128]{1,0:T(8,128)S(1)} %get-tuple-element.74), channel_id=1, source_target_pairs={{0,8},{1,9},{2,10},{3,11},{4,12},{5,13},{6,14},{7,15},{16,24},{17,... | collective-permute-start | bytes 12296 | tf_op jit(solution)/shard_map/ppermute | solution.py:232
  48.4 2.7 %backward1.1 = (f32[3,34,8,256]{3,2,1,0:T(8,128)S(1)}, f32[8,128]{1,0:T(8,128)S(1)}, f32[8,128]{1,0:T(8,128)S(1)}, f32[96,256]{1,0:T(8,128)S(1)}, f32[96,256]{1,0:T(8,128)S(1)}) custom-call(s32[7]{0:T(128)S(1)} %stack.47.meta_ref.r_0_, f32[6,3,3,32,8,256]{5,4,3,2,1,0:T(8,128)S(1)} %bitcast.17, f32[3,3,32,8,256]{4,3,2,1,0:T(8,128)S(1)} %get-tuple-element.47.r_2_, ...), custom_call_target="tpu_custom_call" | custom-call | tf_op jit(solution)/shard_map/backward1/pallas_call | solution.py:45
  51.1 1.3 %collective-permute-start.22 = (f32[96,256]{1,0:T(8,128)S(1)}, f32[96,256]{1,0:T(8,128)S(1)}, u32[]{:S(2)}, u32[]{:S(2)}) collective-permute-start(f32[96,256]{1,0:T(8,128)S(1)} %get-tuple-element.81), channel_id=1, source_target_pairs={{0,1},{8,9},{16,17},{24,25},{32,33},{40,41},{48,49},{56,57},{64,65... | collective-permute-start | bytes 294920 | tf_op jit(solution)/shard_map/ppermute | solution.py:233
  52.3 5.5 %collective-permute-start.20 = (f32[8,128]{1,0:T(8,128)S(1)}, f32[8,128]{1,0:T(8,128)S(1)}, u32[]{:S(2)}, u32[]{:S(2)}) collective-permute-start(f32[8,128]{1,0:T(8,128)S(1)} %get-tuple-element.79), channel_id=1, source_target_pairs={{0,8},{1,9},{2,10},{3,11},{4,12},{5,13},{6,14},{7,15},{16,24},{17,... | collective-permute-start | bytes 12296 | tf_op jit(solution)/shard_map/ppermute | solution.py:232
  57.9 1.3 %prep.1 = (bf16[1024,1024]{1,0:T(8,128)(2,1)S(1)}, bf16[256,1024]{1,0:T(8,128)(2,1)S(1)}, f32[16,128]{1,0:T(8,128)S(1)}, s32[1,1024]{1,0:T(1,128)S(1)}) custom-call(s32[7]{0:T(128)S(1)} %stack.47.meta_ref.r_0_, s32[64,128]{1,0:T(8,128)S(1)} %bitcast.24, s32[64,128]{1,0:T(8,128)S(1)} %bitcast.25, s32[1,1024]{1,0:T(1,128)S(1)} %bitcast.21, ...), custom_call_target="tpu_custom_call" | custom-call | tf_op jit(solution)/shard_map/prep/pallas_call | solution.py:45
  59.3 2.4 %backward0.1.s_ref = f32[3,32,8,256]{3,2,1,0:T(8,128)S(1)} custom-call(s32[7]{0:T(128)S(1)} %stack.47.meta_ref.r_0_, f32[6,3,3,32,8,256]{5,4,3,2,1,0:T(8,128)S(1)} %bitcast.17, f32[3,3,32,8,256]{4,3,2,1,0:T(8,128)S(1)} %get-tuple-element.47.r_2_, s32[32,8,256]{2,1,0:T(8,128)S(1)} %get-tuple-element.48.r_3_, f32[3,32,8,256]{3,2,1,0:T(8,128)S(1)} %get-tuple-element.67.r_4_, ...), custom_call_target="tpu_custom_call" | custom-call | tf_op jit(solution)/shard_map/backward0/pallas_call | solution.py:45
  61.7 1.9 %terms.1 = (f32[512,128]{1,0:T(8,128)S(1)}, f32[512,128]{1,0:T(8,128)S(1)}) custom-call(f32[3,32,8,256]{3,2,1,0:T(8,128)S(1)} %backward0.1.s_ref, bf16[256,1024]{1,0:T(8,128)(2,1)S(1)} %get-tuple-element.83.rt_ref, bf16[1024,1024]{1,0:T(8,128)(2,1)S(1)} %get-tuple-element.84.kh_ref, s32[1,1024]{1,0:T(1,128)S(1)} %get-tuple-element.85.lo_ref, ...), custom_call_target="tpu_custom_call" | custom-call | tf_op jit(solution)/shard_map/terms/pallas_call | solution.py:45
  63.6 1.0 collective-permute-start.24
  64.6 1.2 %collective-permute-done.24 = f32[512,128]{1,0:T(8,128)S(1)} collective-permute-done((f32[512,128]{1,0:T(8,128)S(1)}, f32[512,128]{1,0:T(8,128)S(1)}, u32[]{:S(2)}, u32[]{:S(2)}) %collective-permute-start.24) | collective-permute-done | bytes 262176 | tf_op jit(solution)/shard_map/ppermute | solution.py:403
  65.8 23.9 %all_to_all.10.got_ref = f32[64,8,128]{2,1,0:T(8,128)S(1)} all-to-all(f32[64,8,128]{2,1,0:T(8,128)S(1)} %add_bitcast_fusion), channel_id=1, replica_groups={{0,2,4,6,8,10,12,14,16,18,20,22,24,26,28,30,32,34,36,38,40,42,44,46,48,..., dimensions={0} | all-to-all | bytes 524288 | tf_op jit(solution)/shard_map/all_to_all | solution.py:404
  89.9 13.8 %all_to_all.11 = f32[64,8,128]{2,1,0:T(8,128)S(1)} all-to-all(f32[64,8,128]{2,1,0:T(8,128)S(1)} %solve.1), channel_id=1, replica_groups={{0,2,4,6,8,10,12,14,16,18,20,22,24,26,28,30,32,34,36,38,40,42,44,46,48,..., dimensions={0} | all-to-all | bytes 524288 | tf_op jit(solution)/shard_map/all_to_all | solution.py:408
  103.7 3.0 %collective-permute-start.25 = (f32[512,128]{1,0:T(8,128)S(1)}, f32[512,128]{1,0:T(8,128)S(1)}, u32[]{:S(2)}, u32[]{:S(2)}) collective-permute-start(f32[512,128]{1,0:T(8,128)S(1)} %bitcast.18), channel_id=1, source_target_pairs={{0,1},{8,9},{16,17},{24,25},{32,33},{40,41},{48,49},{56,57},{64,65... | collective-permute-start | bytes 786440 | tf_op jit(solution)/shard_map/ppermute | solution.py:409
  106.7 1.2 %collective-permute-done.25.other_ref = f32[512,128]{1,0:T(8,128)S(1)} collective-permute-done((f32[512,128]{1,0:T(8,128)S(1)}, f32[512,128]{1,0:T(8,128)S(1)}, u32[]{:S(2)}, u32[]{:S(2)}) %collective-permute-start.25) | collective-permute-done | bytes 262176 | tf_op jit(solution)/shard_map/ppermute | solution.py:409
  107.9 2.7 %back.1 = f32[3,32,8,256]{3,2,1,0:T(8,128)} custom-call(f32[512,128]{1,0:T(8,128)S(1)} %bitcast.19, f32[512,128]{1,0:T(8,128)S(1)} %collective-permute-done.25.other_ref, f32[3,32,8,256]{3,2,1,0:T(8,128)S(1)} %backward0.1.s_ref, bf16[256,1024]{1,0:T(8,128)(2,1)S(1)} %get-tuple-element.83.rt_ref, bf16[1024,1024]{1,0:T(8,128)(2,1)S(1)} %get-tuple-element.84.kh_ref, ...), custom_call_target="tpu_custom_call" | custom-call | tf_op jit(solution)/shard_map/back/pallas_call | solution.py:410
  (60 shorter events, 4.2 us)
Async XLA Ops:
  3.3 5.6 %collective-permute-start.2 = (f32[96,256]{1,0:T(8,128)S(1)}, f32[96,256]{1,0:T(8,128)S(1)}, u32[]{:S(2)}, u32[]{:S(2)}) collective-permute-start(f32[96,256]{1,0:T(8,128)S(1)} %get-tuple-element.53), channel_id=1, source_target_pairs={{0,1},{8,9},{16,17},{24,25},{32,33},{40,41},{48,49},{56,57},{64,65... | collective-permute-start | bytes 294920 | tf_op jit(solution)/shard_map/ppermute | solution.py:233
  4.8 4.3 %collective-permute-start.3 = (f32[96,256]{1,0:T(8,128)S(1)}, f32[96,256]{1,0:T(8,128)S(1)}, u32[]{:S(2)}, u32[]{:S(2)}) collective-permute-start(f32[96,256]{1,0:T(8,128)S(1)} %get-tuple-element.54), channel_id=1, source_target_pairs={{1,2},{9,10},{17,18},{25,26},{33,34},{41,42},{49,50},{57,58},{65,6... | collective-permute-start | bytes 294920 | tf_op jit(solution)/shard_map/ppermute | solution.py:231
  6.1 2.8 %collective-permute-start = (f32[8,128]{1,0:T(8,128)S(1)}, f32[8,128]{1,0:T(8,128)S(1)}, u32[]{:S(2)}, u32[]{:S(2)}) collective-permute-start(f32[8,128]{1,0:T(8,128)S(1)} %get-tuple-element.51), channel_id=1, source_target_pairs={{0,8},{1,9},{2,10},{3,11},{4,12},{5,13},{6,14},{7,15},{16,24},{17,... | collective-permute-start | bytes 12296 | tf_op jit(solution)/shard_map/ppermute | solution.py:232
  7.4 1.5 %collective-permute-start.1 = (f32[8,128]{1,0:T(8,128)S(1)}, f32[8,128]{1,0:T(8,128)S(1)}, u32[]{:S(2)}, u32[]{:S(2)}) collective-permute-start(f32[8,128]{1,0:T(8,128)S(1)} %get-tuple-element.52), channel_id=1, source_target_pairs={{8,16},{9,17},{10,18},{11,19},{12,20},{13,21},{14,22},{15,23},{24,... | collective-permute-start | bytes 12296 | tf_op jit(solution)/shard_map/ppermute | solution.py:230
  11.8 4.8 %collective-permute-start.6 = (f32[96,256]{1,0:T(8,128)S(1)}, f32[96,256]{1,0:T(8,128)S(1)}, u32[]{:S(2)}, u32[]{:S(2)}) collective-permute-start(f32[96,256]{1,0:T(8,128)S(1)} %get-tuple-element.59), channel_id=1, source_target_pairs={{0,1},{8,9},{16,17},{24,25},{32,33},{40,41},{48,49},{56,57},{64,65... | collective-permute-start | bytes 294920 | tf_op jit(solution)/shard_map/ppermute | solution.py:233
  13.0 4.3 %collective-permute-start.7 = (f32[96,256]{1,0:T(8,128)S(1)}, f32[96,256]{1,0:T(8,128)S(1)}, u32[]{:S(2)}, u32[]{:S(2)}) collective-permute-start(f32[96,256]{1,0:T(8,128)S(1)} %get-tuple-element.60), channel_id=1, source_target_pairs={{1,2},{9,10},{17,18},{25,26},{33,34},{41,42},{49,50},{57,58},{65,6... | collective-permute-start | bytes 294920 | tf_op jit(solution)/shard_map/ppermute | solution.py:231
  13.3 3.3 %collective-permute-start.4 = (f32[8,128]{1,0:T(8,128)S(1)}, f32[8,128]{1,0:T(8,128)S(1)}, u32[]{:S(2)}, u32[]{:S(2)}) collective-permute-start(f32[8,128]{1,0:T(8,128)S(1)} %get-tuple-element.57), channel_id=1, source_target_pairs={{0,8},{1,9},{2,10},{3,11},{4,12},{5,13},{6,14},{7,15},{16,24},{17,... | collective-permute-start | bytes 12296 | tf_op jit(solution)/shard_map/ppermute | solution.py:232
  15.3 1.3 %collective-permute-start.5 = (f32[8,128]{1,0:T(8,128)S(1)}, f32[8,128]{1,0:T(8,128)S(1)}, u32[]{:S(2)}, u32[]{:S(2)}) collective-permute-start(f32[8,128]{1,0:T(8,128)S(1)} %get-tuple-element.58), channel_id=1, source_target_pairs={{8,16},{9,17},{10,18},{11,19},{12,20},{13,21},{14,22},{15,23},{24,... | collective-permute-start | bytes 12296 | tf_op jit(solution)/shard_map/ppermute | solution.py:230
  20.1 7.1 %collective-permute-start.10 = (f32[96,256]{1,0:T(8,128)S(1)}, f32[96,256]{1,0:T(8,128)S(1)}, u32[]{:S(2)}, u32[]{:S(2)}) collective-permute-start(f32[96,256]{1,0:T(8,128)S(1)} %get-tuple-element.65), channel_id=1, source_target_pairs={{0,1},{8,9},{16,17},{24,25},{32,33},{40,41},{48,49},{56,57},{64,65... | collective-permute-start | bytes 294920 | tf_op jit(solution)/shard_map/ppermute | solution.py:233
  21.6 5.6 %collective-permute-start.11 = (f32[96,256]{1,0:T(8,128)S(1)}, f32[96,256]{1,0:T(8,128)S(1)}, u32[]{:S(2)}, u32[]{:S(2)}) collective-permute-start(f32[96,256]{1,0:T(8,128)S(1)} %get-tuple-element.66), channel_id=1, source_target_pairs={{1,2},{9,10},{17,18},{25,26},{33,34},{41,42},{49,50},{57,58},{65,6... | collective-permute-start | bytes 294920 | tf_op jit(solution)/shard_map/ppermute | solution.py:231
  21.6 5.4 %collective-permute-start.8 = (f32[8,128]{1,0:T(8,128)S(1)}, f32[8,128]{1,0:T(8,128)S(1)}, u32[]{:S(2)}, u32[]{:S(2)}) collective-permute-start(f32[8,128]{1,0:T(8,128)S(1)} %get-tuple-element.63), channel_id=1, source_target_pairs={{0,8},{1,9},{2,10},{3,11},{4,12},{5,13},{6,14},{7,15},{16,24},{17,... | collective-permute-start | bytes 12296 | tf_op jit(solution)/shard_map/ppermute | solution.py:232
  26.0 1.2 %collective-permute-start.9 = (f32[8,128]{1,0:T(8,128)S(1)}, f32[8,128]{1,0:T(8,128)S(1)}, u32[]{:S(2)}, u32[]{:S(2)}) collective-permute-start(f32[8,128]{1,0:T(8,128)S(1)} %get-tuple-element.64), channel_id=1, source_target_pairs={{8,16},{9,17},{10,18},{11,19},{12,20},{13,21},{14,22},{15,23},{24,... | collective-permute-start | bytes 12296 | tf_op jit(solution)/shard_map/ppermute | solution.py:230
  29.8 7.9 %collective-permute-start.14 = (f32[96,256]{1,0:T(8,128)S(1)}, f32[96,256]{1,0:T(8,128)S(1)}, u32[]{:S(2)}, u32[]{:S(2)}) collective-permute-start(f32[96,256]{1,0:T(8,128)S(1)} %get-tuple-element.71), channel_id=1, source_target_pairs={{0,1},{8,9},{16,17},{24,25},{32,33},{40,41},{48,49},{56,57},{64,65... | collective-permute-start | bytes 294920 | tf_op jit(solution)/shard_map/ppermute | solution.py:233
  31.0 6.7 %collective-permute-start.15 = (f32[96,256]{1,0:T(8,128)S(1)}, f32[96,256]{1,0:T(8,128)S(1)}, u32[]{:S(2)}, u32[]{:S(2)}) collective-permute-start(f32[96,256]{1,0:T(8,128)S(1)} %get-tuple-element.72), channel_id=1, source_target_pairs={{1,2},{9,10},{17,18},{25,26},{33,34},{41,42},{49,50},{57,58},{65,6... | collective-permute-start | bytes 294920 | tf_op jit(solution)/shard_map/ppermute | solution.py:231
  31.0 6.5 %collective-permute-start.12 = (f32[8,128]{1,0:T(8,128)S(1)}, f32[8,128]{1,0:T(8,128)S(1)}, u32[]{:S(2)}, u32[]{:S(2)}) collective-permute-start(f32[8,128]{1,0:T(8,128)S(1)} %get-tuple-element.69), channel_id=1, source_target_pairs={{0,8},{1,9},{2,10},{3,11},{4,12},{5,13},{6,14},{7,15},{16,24},{17,... | collective-permute-start | bytes 12296 | tf_op jit(solution)/shard_map/ppermute | solution.py:232
  36.5 1.2 %collective-permute-start.13 = (f32[8,128]{1,0:T(8,128)S(1)}, f32[8,128]{1,0:T(8,128)S(1)}, u32[]{:S(2)}, u32[]{:S(2)}) collective-permute-start(f32[8,128]{1,0:T(8,128)S(1)} %get-tuple-element.70), channel_id=1, source_target_pairs={{8,16},{9,17},{10,18},{11,19},{12,20},{13,21},{14,22},{15,23},{24,... | collective-permute-start | bytes 12296 | tf_op jit(solution)/shard_map/ppermute | solution.py:230
  40.4 7.9 %collective-permute-start.18 = (f32[96,256]{1,0:T(8,128)S(1)}, f32[96,256]{1,0:T(8,128)S(1)}, u32[]{:S(2)}, u32[]{:S(2)}) collective-permute-start(f32[96,256]{1,0:T(8,128)S(1)} %get-tuple-element.76), channel_id=1, source_target_pairs={{0,1},{8,9},{16,17},{24,25},{32,33},{40,41},{48,49},{56,57},{64,65... | collective-permute-start | bytes 294920 | tf_op jit(solution)/shard_map/ppermute | solution.py:233
  41.6 6.7 %collective-permute-start.19 = (f32[96,256]{1,0:T(8,128)S(1)}, f32[96,256]{1,0:T(8,128)S(1)}, u32[]{:S(2)}, u32[]{:S(2)}) collective-permute-start(f32[96,256]{1,0:T(8,128)S(1)} %get-tuple-element.77), channel_id=1, source_target_pairs={{1,2},{9,10},{17,18},{25,26},{33,34},{41,42},{49,50},{57,58},{65,6... | collective-permute-start | bytes 294920 | tf_op jit(solution)/shard_map/ppermute | solution.py:231
  41.7 6.5 %collective-permute-start.16 = (f32[8,128]{1,0:T(8,128)S(1)}, f32[8,128]{1,0:T(8,128)S(1)}, u32[]{:S(2)}, u32[]{:S(2)}) collective-permute-start(f32[8,128]{1,0:T(8,128)S(1)} %get-tuple-element.74), channel_id=1, source_target_pairs={{0,8},{1,9},{2,10},{3,11},{4,12},{5,13},{6,14},{7,15},{16,24},{17,... | collective-permute-start | bytes 12296 | tf_op jit(solution)/shard_map/ppermute | solution.py:232
  47.1 1.2 %collective-permute-start.17 = (f32[8,128]{1,0:T(8,128)S(1)}, f32[8,128]{1,0:T(8,128)S(1)}, u32[]{:S(2)}, u32[]{:S(2)}) collective-permute-start(f32[8,128]{1,0:T(8,128)S(1)} %get-tuple-element.75), channel_id=1, source_target_pairs={{8,16},{9,17},{10,18},{11,19},{12,20},{13,21},{14,22},{15,23},{24,... | collective-permute-start | bytes 12296 | tf_op jit(solution)/shard_map/ppermute | solution.py:230
  48.3 9.5 %copy-start.1 = (s32[1024]{0:T(1024)S(1)}, s32[1024]{0:T(1024)}, u32[]{:S(2)}) copy-start(s32[1024]{0:T(1024)} %param.16) | copy-start | bytes 12292
  48.3 9.5 %copy-start.2 = (s32[8192]{0:T(1024)S(1)}, s32[8192]{0:T(1024)}, u32[]{:S(2)}) copy-start(s32[8192]{0:T(1024)} %param.21) | copy-start | bytes 98308
  48.3 9.5 %copy-start.3 = (s32[8192]{0:T(1024)S(1)}, s32[8192]{0:T(1024)}, u32[]{:S(2)}) copy-start(s32[8192]{0:T(1024)} %param.22) | copy-start | bytes 98308
  48.3 9.5 %copy-start.6 = (s32[1024]{0:T(1024)S(1)}, s32[1024]{0:T(1024)}, u32[]{:S(2)}) copy-start(s32[1024]{0:T(1024)} %param.17) | copy-start | bytes 12292
  51.1 8.2 %collective-permute-start.22 = (f32[96,256]{1,0:T(8,128)S(1)}, f32[96,256]{1,0:T(8,128)S(1)}, u32[]{:S(2)}, u32[]{:S(2)}) collective-permute-start(f32[96,256]{1,0:T(8,128)S(1)} %get-tuple-element.81), channel_id=1, source_target_pairs={{0,1},{8,9},{16,17},{24,25},{32,33},{40,41},{48,49},{56,57},{64,65... | collective-permute-start | bytes 294920 | tf_op jit(solution)/shard_map/ppermute | solution.py:233
  52.3 6.9 %collective-permute-start.23 = (f32[96,256]{1,0:T(8,128)S(1)}, f32[96,256]{1,0:T(8,128)S(1)}, u32[]{:S(2)}, u32[]{:S(2)}) collective-permute-start(f32[96,256]{1,0:T(8,128)S(1)} %get-tuple-element.82), channel_id=1, source_target_pairs={{1,2},{9,10},{17,18},{25,26},{33,34},{41,42},{49,50},{57,58},{65,6... | collective-permute-start | bytes 294920 | tf_op jit(solution)/shard_map/ppermute | solution.py:231
  52.3 6.9 %collective-permute-start.20 = (f32[8,128]{1,0:T(8,128)S(1)}, f32[8,128]{1,0:T(8,128)S(1)}, u32[]{:S(2)}, u32[]{:S(2)}) collective-permute-start(f32[8,128]{1,0:T(8,128)S(1)} %get-tuple-element.79), channel_id=1, source_target_pairs={{0,8},{1,9},{2,10},{3,11},{4,12},{5,13},{6,14},{7,15},{16,24},{17,... | collective-permute-start | bytes 12296 | tf_op jit(solution)/shard_map/ppermute | solution.py:232
  57.8 1.4 %collective-permute-start.21 = (f32[8,128]{1,0:T(8,128)S(1)}, f32[8,128]{1,0:T(8,128)S(1)}, u32[]{:S(2)}, u32[]{:S(2)}) collective-permute-start(f32[8,128]{1,0:T(8,128)S(1)} %get-tuple-element.80), channel_id=1, source_target_pairs={{8,16},{9,17},{10,18},{11,19},{12,20},{13,21},{14,22},{15,23},{24,... | collective-permute-start | bytes 12296 | tf_op jit(solution)/shard_map/ppermute | solution.py:230
  61.7 28.0 %copy-start = (f32[64,16,16]{0,2,1:T(8,128)S(1)}, f32[64,16,16]{0,2,1:T(8,128)}, u32[]{:S(2)}) copy-start(f32[64,16,16]{0,2,1:T(8,128)} %param.23) | copy-start | bytes 196612
  61.7 46.2 %copy-start.5 = (f32[3,1024]{1,0:T(4,128)S(1)}, f32[3,1024]{1,0:T(4,128)}, u32[]{:S(2)}) copy-start(f32[3,1024]{1,0:T(4,128)} %back_ref.1) | copy-start | bytes 36868
  63.6 2.2 %collective-permute-start.24 = (f32[512,128]{1,0:T(8,128)S(1)}, f32[512,128]{1,0:T(8,128)S(1)}, u32[]{:S(2)}, u32[]{:S(2)}) collective-permute-start(f32[512,128]{1,0:T(8,128)S(1)} %get-tuple-element.87), channel_id=1, source_target_pairs={{0,1},{8,9},{16,17},{24,25},{32,33},{40,41},{48,49},{56,57},{64,65... | collective-permute-start | bytes 786440 | tf_op jit(solution)/shard_map/ppermute | solution.py:403
  103.7 4.2 %collective-permute-start.25 = (f32[512,128]{1,0:T(8,128)S(1)}, f32[512,128]{1,0:T(8,128)S(1)}, u32[]{:S(2)}, u32[]{:S(2)}) collective-permute-start(f32[512,128]{1,0:T(8,128)S(1)} %bitcast.18), channel_id=1, source_target_pairs={{0,1},{8,9},{16,17},{24,25},{32,33},{40,41},{48,49},{56,57},{64,65... | collective-permute-start | bytes 786440 | tf_op jit(solution)/shard_map/ppermute | solution.py:409
  (6 other events, 48.1 us)
